TPU v7x, 32 devices: a whole 2x2x4 slice. The times are simulated.
32 devices in a mesh: gx: 4 (over z), gy: 4 (over x, core), gz: 2 (over y).
Axes of the slice: x: 2, y: 2, z: 4, core: 2. Of those that a mesh axis runs over, the one named last changes fastest.
Arguments:
- pop_flow: float32 [19, 8, 64, 512], P(None, 'gz', 'gx', 'gy'), may hold values from 0.01 to 0.5, as said below
- pop_therm: float32 [7, 8, 64, 512], P(None, 'gz', 'gx', 'gy'), may hold values from 0.04 to 0.6, as said below
- flags: int32 [8, 64, 512], P('gz', 'gx', 'gy'), may hold values from 0 to 3, as said below
- nozzle_id: int32 [64, 512], P('gx', 'gy'), may hold values from 0 to 63
- jet_velocity: float32 [3, 64], replicated, may hold values from -0.2 to 0.2
- cot_flow: float32 [19, 8, 64, 512], P(None, 'gz', 'gx', 'gy'), may hold values from -6 to 6
- cot_therm: float32 [7, 8, 64, 512], P(None, 'gz', 'gx', 'gy'), may hold values from -6 to 6
- cot_plate: float32 [20, 64, 512], P('gz', 'gx', 'gy'), may hold values from -6 to 6
Outputs:
- grad_flow: float32 [19, 8, 64, 512], P(None, 'gz', 'gx', 'gy')
- grad_therm: float32 [7, 8, 64, 512], P(None, 'gz', 'gx', 'gy')
- grad_plate: float32 [20, 64, 512], P('gz', 'gx', 'gy')
Inputs may be any that keep to these rules, and one draw needn't show every extreme that they name: `flags`: cells of the top layer are nozzle inlets (2) or walls (1); the other cells on the four side faces are outlets (3); all other cells are fluid (0) or wall (1), with no walls on the layer z = 0. `pop_flow`: every population is positive. `pop_therm`: every population is positive.
All inputs are finite; a program needn't handle non-finite values.
Results may differ from a plain program's by a relative error of at most 0.0003.
Values sent between devices are 32-bit elements; how exact they have to be, the bound alone decides.
No kernel may reach another device: no remote copies, remote signals or barrier semaphores. Data moves between devices by JAX's collectives and lax.ppermute only.
A program may use at most 64 MiB of HBM per device.

v0:
```python
import jax
import jax.numpy as jnp
from jax import lax
from jax.sharding import PartitionSpec as P

VELOCITY = (
    (0, 0, 0),
    (1, 0, 0),
    (-1, 0, 0),
    (0, 1, 0),
    (0, -1, 0),
    (0, 0, 1),
    (0, 0, -1),
    (1, 1, 0),
    (-1, -1, 0),
    (1, -1, 0),
    (-1, 1, 0),
    (1, 0, 1),
    (-1, 0, -1),
    (1, 0, -1),
    (-1, 0, 1),
    (0, 1, 1),
    (0, -1, -1),
    (0, 1, -1),
    (0, -1, 1),
)
OPPOSITE = tuple((VELOCITY.index((-a, -b, -c)) for a, b, c in VELOCITY))
WEIGHTS_FLOW = (1.0 / 3.0,) + (1.0 / 18.0,) * 6 + (1.0 / 36.0,) * 12
WEIGHTS_HEAT = (0.25,) + (0.125,) * 6
DIRECTIONS = VELOCITY + VELOCITY[:7]
tau_flow = 0.8
tau_heat = 0.9
diffusion = 0.12
coupling = 0.3
jet_heat = 0.4


def with_halo(x, sides, width):
    for axis, dim in sides:
        size, length = (lax.axis_size(axis), x.shape[dim])
        up = [(i, (i + 1) % size) for i in range(size - 1)]
        down = [(j, i) for i, j in up]
        last = lax.slice_in_dim(x, length - width, length, axis=dim)
        first = lax.slice_in_dim(x, 0, width, axis=dim)
        before = lax.ppermute(last, axis, up)
        after = lax.ppermute(first, axis, down)
        x = jnp.concatenate([before, x, after], axis=dim)
    return x


def moment(pops, component):
    total = jnp.zeros_like(pops[0])
    for q in range(pops.shape[0]):
        sign = VELOCITY[q][component]
        if sign != 0:
            total = total + sign * pops[q]
    return total


def flow_equilibrium(density, vel_x, vel_y, vel_z):
    speed_sq = vel_x * vel_x + vel_y * vel_y + vel_z * vel_z
    terms = []
    for weight, (cx, cy, cz) in zip(WEIGHTS_FLOW, VELOCITY):
        along = cx * vel_x + cy * vel_y + cz * vel_z
        terms.append(weight * density * (1.0 + 3.0 * along + 4.5 * along * along - 1.5 * speed_sq))
    return jnp.stack(terms)


def heat_equilibrium(temper, vel_x, vel_y, vel_z):
    terms = []
    for weight, (cx, cy, cz) in zip(WEIGHTS_HEAT, VELOCITY[:7]):
        along = cx * vel_x + cy * vel_y + cz * vel_z
        terms.append(weight * temper * (1.0 + 4.0 * along))
    return jnp.stack(terms)


def collide(flow, heat, flags, jet):
    density = jnp.sum(flow, axis=0)
    vel_x = moment(flow, 0) / density
    vel_y = moment(flow, 1) / density
    vel_z = moment(flow, 2) / density
    temper = jnp.sum(heat, axis=0)
    relaxed_flow = flow - (flow - flow_equilibrium(density, vel_x, vel_y, vel_z)) / tau_flow
    relaxed_heat = heat - (heat - heat_equilibrium(temper, vel_x, vel_y, vel_z)) / tau_heat
    bounced_flow = jnp.stack([flow[o] for o in OPPOSITE])
    bounced_heat = jnp.stack([heat[o] for o in OPPOSITE[:7]])
    inlet_flow = flow_equilibrium(density, jet[0], jet[1], jet[2])
    inlet_heat = heat_equilibrium(jet_heat * jnp.ones_like(temper), jet[0], jet[1], jet[2])
    wall = (flags == 1)[None]
    inlet = (flags == 2)[None]
    out_flow = jnp.where(wall, bounced_flow, jnp.where(inlet, inlet_flow, relaxed_flow))
    out_heat = jnp.where(wall, bounced_heat, jnp.where(inlet, inlet_heat, relaxed_heat))
    return (out_flow, out_heat)


def lookup(nozzle_id, jet_velocity):
    labels = jnp.arange(jet_velocity.shape[1], dtype=jnp.int32)
    match = nozzle_id[None] == labels[:, None, None]
    return jnp.sum(jnp.where(match[None], jet_velocity[:, :, None, None], 0.0), axis=1)


def padded_total(padded):
    beside_all = padded[2:, 1:-1, 1:-1] + padded[:-2, 1:-1, 1:-1]
    beside_all = beside_all + padded[1:-1, 2:, 1:-1] + padded[1:-1, :-2, 1:-1]
    beside_all = beside_all + padded[1:-1, 1:-1, 2:] + padded[1:-1, 1:-1, :-2]
    return beside_all


def local(pop_flow, pop_therm, flags, nozzle_id, jet_velocity, cot_flow, cot_therm, cot_plate):
    combined = jnp.concatenate([cot_flow, cot_therm], axis=0)
    padded = with_halo(combined, (("gx", 2), ("gy", 3), ("gz", 1)), 1)
    size_z, size_x, size_y = combined.shape[1:]
    star = jnp.stack(
        [
            padded[q, 1 + cz : 1 + cz + size_z, 1 + cx : 1 + cx + size_x, 1 + cy : 1 + cy + size_y]
            for q, (cx, cy, cz) in enumerate(DIRECTIONS)
        ]
    )
    beside_all = padded_total(with_halo(cot_plate, (("gx", 1), ("gy", 2), ("gz", 0)), 1))
    base = lax.axis_index("gz") == 0
    star_flow = star[:19]
    star_heat = star[19:]
    for q in range(19):
        if VELOCITY[q][2] == -1:
            star_flow = star_flow.at[q, 0].add(jnp.where(base, cot_flow[OPPOSITE[q], 0], 0.0))
    star_heat = star_heat.at[6, 0].add(jnp.where(base, -cot_therm[5, 0], 0.0))
    jet = lookup(nozzle_id, jet_velocity)[:, None]
    _, back = jax.vjp(lambda f, h: collide(f, h, flags, jet), pop_flow, pop_therm)
    grad_flow, grad_heat = back((star_flow, star_heat))
    grad_heat = grad_heat.at[:, 0].add(jnp.where(base, coupling * cot_plate[0], 0.0)[None])
    grad_plate = cot_plate + diffusion * (beside_all - 6.0 * cot_plate)
    grad_plate = grad_plate.at[0].add(
        jnp.where(base, -coupling * cot_plate[0] + 0.25 * cot_therm[5, 0], 0.0)
    )
    return (grad_flow, grad_heat, grad_plate)


def solution(mesh):
    return jax.shard_map(
        local,
        mesh=mesh,
        in_specs=(
            P(None, "gz", "gx", "gy"),
            P(None, "gz", "gx", "gy"),
            P("gz", "gx", "gy"),
            P("gx", "gy"),
            P(),
            P(None, "gz", "gx", "gy"),
            P(None, "gz", "gx", "gy"),
            P("gz", "gx", "gy"),
        ),
        out_specs=(P(None, "gz", "gx", "gy"), P(None, "gz", "gx", "gy"), P("gz", "gx", "gy")),
        check_vma=False,
    )
```

profile of v0, /device:TPU:21, one launch (start us, length us, event | category | flops | bytes accessed | tf_op | source)
XLA Modules:
  0.0 77.9 jit_solution(5278045631311865446)
XLA Ops:
  0.7 1.2 %constant_dynamic-update-slice_fusion.1 = f32[26,4,16,128]{3,2,1,0:T(8,128)S(1)} fusion(f32[19,4,16,128]{3,2,1,0:T(8,128)} %param.29), kind=kLoop, calls=%fused_computation.46 | loop fusion | bytes 1245184
  2.0 2.2 %collective-permute-start = (f32[26,4,1,128]{3,2,1,0:T(1,128)S(1)}, f32[26,4,1,128]{3,2,1,0:T(1,128)S(1)}, u32[]{:S(2)}, u32[]{:S(2)}) collective-permute-start(f32[26,4,1,128]{3,2,1,0:T(1,128)S(1)} %get-tuple-element.133), channel_id=1, source_target_pairs={{8,0},{16,8},{24,16},{9,1},{17,9},{25,17},{10,2},{18,10},{26,18},{... | collective-permute-start | bytes 159752 | tf_op jit(solution)/shard_map/ppermute | solution.py:46
  4.2 3.2 %collective-permute-start.1 = (f32[26,4,1,128]{3,2,1,0:T(1,128)S(1)}, f32[26,4,1,128]{3,2,1,0:T(1,128)S(1)}, u32[]{:S(2)}, u32[]{:S(2)}) collective-permute-start(f32[26,4,1,128]{3,2,1,0:T(1,128)S(1)} %get-tuple-element.132), channel_id=1, source_target_pairs={{0,8},{8,16},{16,24},{1,9},{9,17},{17,25},{2,10},{10,18},{18,26},{... | collective-permute-start | bytes 159752 | tf_op jit(solution)/shard_map/ppermute | solution.py:45
  7.5 1.9 %collective-permute-start.6 = (f32[10,1,128]{2,1,0:T(1,128)S(1)}, f32[10,1,128]{2,1,0:T(1,128)S(1)}, u32[]{:S(2)}, u32[]{:S(2)}) collective-permute-start(f32[10,1,128]{2,1,0:T(1,128)S(1)} %get-tuple-element.171), channel_id=1, source_target_pairs={{0,8},{8,16},{16,24},{1,9},{9,17},{17,25},{2,10},{10,18},{18,26},{... | collective-permute-start | bytes 15368 | tf_op jit(solution)/shard_map/ppermute | solution.py:45
  9.4 3.4 %collective-permute-start.7 = (f32[10,1,128]{2,1,0:T(1,128)S(1)}, f32[10,1,128]{2,1,0:T(1,128)S(1)}, u32[]{:S(2)}, u32[]{:S(2)}) collective-permute-start(f32[10,1,128]{2,1,0:T(1,128)S(1)} %get-tuple-element.172), channel_id=1, source_target_pairs={{8,0},{16,8},{24,16},{9,1},{17,9},{25,17},{10,2},{18,10},{26,18},{... | collective-permute-start | bytes 15368 | tf_op jit(solution)/shard_map/ppermute | solution.py:46
  12.8 1.4 %constant_dynamic-update-slice_fusion.20 = f32[19,4,16,128]{3,2,1,0:T(8,128)} fusion(f32[19,4,16,128]{3,2,1,0:T(8,128)} %param.29), kind=kLoop, calls=%fused_computation.65 | loop fusion | bytes 65536
  17.1 4.8 %collective-permute-start.8 = (f32[10,18,1]{2,1,0:T(8,128)S(1)}, f32[10,18,1]{2,1,0:T(8,128)S(1)}, u32[]{:S(2)}, u32[]{:S(2)}) collective-permute-start(f32[10,18,1]{2,1,0:T(8,128)S(1)} %get-tuple-element.168), channel_id=1, source_target_pairs={{0,2},{2,4},{4,6},{1,3},{3,5},{5,7},{8,10},{10,12},{12,14},{9,11},... | collective-permute-start | bytes 2168 | tf_op jit(solution)/shard_map/ppermute | solution.py:45
  22.0 1.9 %collective-permute-start.9 = (f32[10,18,1]{2,1,0:T(8,128)S(1)}, f32[10,18,1]{2,1,0:T(8,128)S(1)}, u32[]{:S(2)}, u32[]{:S(2)}) collective-permute-start(f32[10,18,1]{2,1,0:T(8,128)S(1)} %get-tuple-element.167), channel_id=1, source_target_pairs={{2,0},{4,2},{6,4},{3,1},{5,3},{7,5},{10,8},{12,10},{14,12},{11,9},... | collective-permute-start | bytes 2168 | tf_op jit(solution)/shard_map/ppermute | solution.py:46
  24.5 3.6 %collective-permute-done.9 = f32[10,18,1]{2,1,0:T(8,128)S(1)} collective-permute-done((f32[10,18,1]{2,1,0:T(8,128)S(1)}, f32[10,18,1]{2,1,0:T(8,128)S(1)}, u32[]{:S(2)}, u32[]{:S(2)}) %collective-permute-start.9) | collective-permute-done | bytes 752 | tf_op jit(solution)/shard_map/ppermute | solution.py:46
  28.2 2.1 %collective-permute-start.10 = (f32[1,18,130]{2,1,0:T(8,128)S(1)}, f32[1,18,130]{2,1,0:T(8,128)S(1)}, u32[]{:S(2)}, u32[]{:S(2)}) collective-permute-start(f32[1,18,130]{2,1,0:T(8,128)S(1)} %get-tuple-element.157), channel_id=1, source_target_pairs={{1,0},{3,2},{5,4},{7,6},{9,8},{11,10},{13,12},{15,14},{17,16},{19,... | collective-permute-start | bytes 28088 | tf_op jit(solution)/shard_map/ppermute | solution.py:46
  30.4 1.3 %collective-permute-start.11 = (f32[1,18,130]{2,1,0:T(8,128)S(1)}, f32[1,18,130]{2,1,0:T(8,128)S(1)}, u32[]{:S(2)}, u32[]{:S(2)}) collective-permute-start(f32[1,18,130]{2,1,0:T(8,128)S(1)} %get-tuple-element.158), channel_id=1, source_target_pairs={{0,1},{2,3},{4,5},{6,7},{8,9},{10,11},{12,13},{14,15},{16,17},{18,... | collective-permute-start | bytes 28088 | tf_op jit(solution)/shard_map/ppermute | solution.py:45
  33.0 2.0 %collective-permute-done.11 = f32[1,18,130]{2,1,0:T(8,128)S(1)} collective-permute-done((f32[1,18,130]{2,1,0:T(8,128)S(1)}, f32[1,18,130]{2,1,0:T(8,128)S(1)}, u32[]{:S(2)}, u32[]{:S(2)}) %collective-permute-start.11) | collective-permute-done | bytes 9392 | tf_op jit(solution)/shard_map/ppermute | solution.py:45
  37.1 1.3 %copy.102 = f32[26,4,18,1]{0,1,3,2:T(4,128)} copy(f32[26,4,18,1]{3,2,1,0:T(8,128)S(1)} %get-tuple-element.127) | data formatting | bytes 14976 | tf_op jit(solution)/shard_map/slice | solution.py:44
  38.4 1.9 %collective-permute-start.2 = (f32[26,4,18,1]{0,1,3,2:T(4,128)}, f32[26,4,18,1]{0,1,3,2:T(4,128)S(1)}, u32[]{:S(2)}, u32[]{:S(2)}) collective-permute-start(f32[26,4,18,1]{0,1,3,2:T(4,128)} %copy.102), channel_id=1, source_target_pairs={{2,0},{4,2},{6,4},{3,1},{5,3},{7,5},{10,8},{12,10},{14,12},{11,9},... | collective-permute-start | bytes 22472 | tf_op jit(solution)/shard_map/ppermute | solution.py:46
  41.0 3.6 %collective-permute-start.3 = (f32[26,4,18,1]{0,1,3,2:T(4,128)S(1)}, f32[26,4,18,1]{0,1,3,2:T(4,128)}, u32[]{:S(2)}, u32[]{:S(2)}) collective-permute-start(f32[26,4,18,1]{0,1,3,2:T(4,128)S(1)} %copy.104), channel_id=1, source_target_pairs={{0,2},{2,4},{4,6},{1,3},{3,5},{5,7},{8,10},{10,12},{12,14},{9,11},... | collective-permute-start | bytes 22472 | tf_op jit(solution)/shard_map/ppermute | solution.py:45
  45.3 1.2 %copy.103 = f32[26,4,18,1]{3,2,1,0:T(8,128)S(1)} copy(f32[26,4,18,1]{0,1,3,2:T(4,128)S(1)} %collective-permute-done.2) | data formatting | bytes 14976 | tf_op jit(solution)/shard_map/ppermute | solution.py:46
  46.5 1.9 %copy.105 = f32[26,4,18,1]{3,2,1,0:T(8,128)S(1)} copy(f32[26,4,18,1]{0,1,3,2:T(4,128)} %collective-permute-done.3) | data formatting | bytes 14976 | tf_op jit(solution)/shard_map/ppermute | solution.py:45
  49.7 2.0 %collective-permute-start.4 = (f32[26,1,18,130]{3,1,2,0:T(1,128)S(1)}, f32[26,1,18,130]{3,1,2,0:T(1,128)S(1)}, u32[]{:S(2)}, u32[]{:S(2)}) collective-permute-start(f32[26,1,18,130]{3,1,2,0:T(1,128)S(1)} %copy.108), channel_id=1, source_target_pairs={{1,0},{3,2},{5,4},{7,6},{9,8},{11,10},{13,12},{15,14},{17,16},{19,... | collective-permute-start | bytes 730088 | tf_op jit(solution)/shard_map/ppermute | solution.py:46
  52.3 1.3 %collective-permute-start.5 = (f32[26,1,18,130]{3,1,2,0:T(1,128)S(1)}, f32[26,1,18,130]{3,1,2,0:T(1,128)S(1)}, u32[]{:S(2)}, u32[]{:S(2)}) collective-permute-start(f32[26,1,18,130]{3,1,2,0:T(1,128)S(1)} %copy.110), channel_id=1, source_target_pairs={{0,1},{2,3},{4,5},{6,7},{8,9},{10,11},{12,13},{14,15},{16,17},{18,... | collective-permute-start | bytes 730088 | tf_op jit(solution)/shard_map/ppermute | solution.py:45
  53.8 8.6 %collective-permute-done.4 = f32[26,1,18,130]{3,1,2,0:T(1,128)S(1)} collective-permute-done((f32[26,1,18,130]{3,1,2,0:T(1,128)S(1)}, f32[26,1,18,130]{3,1,2,0:T(1,128)S(1)}, u32[]{:S(2)}, u32[]{:S(2)}) %collective-permute-start.4) | collective-permute-done | bytes 243392 | tf_op jit(solution)/shard_map/ppermute | solution.py:46
  62.4 4.6 %collective-permute-done.5 = f32[26,1,18,130]{3,1,2,0:T(1,128)S(1)} collective-permute-done((f32[26,1,18,130]{3,1,2,0:T(1,128)S(1)}, f32[26,1,18,130]{3,1,2,0:T(1,128)S(1)}, u32[]{:S(2)}, u32[]{:S(2)}) %collective-permute-start.5) | collective-permute-done | bytes 243392 | tf_op jit(solution)/shard_map/ppermute | solution.py:45
  67.7 0.8 %copy-done.3 = f32[7,4,16,128]{3,2,1,0:T(8,128)S(1)} copy-done((f32[7,4,16,128]{3,2,1,0:T(8,128)S(1)}, f32[7,4,16,128]{3,2,1,0:T(8,128)}, u32[]{:S(2)}) %copy-start.3) | copy-done | bytes 229400
  73.2 0.8 %copy-done.1 = f32[19,4,16,128]{3,2,1,0:T(8,128)S(1)} copy-done((f32[19,4,16,128]{3,2,1,0:T(8,128)S(1)}, f32[19,4,16,128]{3,2,1,0:T(8,128)}, u32[]{:S(2)}) %copy-start.1) | copy-done | bytes 622616
  76.8 1.1 %add_add_fusion = f32[19,4,16,128]{3,2,1,0:T(8,128)} fusion(f32[1,4,16,128]{3,2,1,0:T(8,128)S(1)} %get-tuple-element.115, f32[1,4,16,128]{3,2,1,0:T(8,128)S(1)} %get-tuple-element.114, f32[1,4,16,128]{3,2,1,0:T(8,128)S(1)} %get-tuple-element.113, f32[1,4,16,128]{3,2,1,0:T(8,128)S(1)} %get-tuple-element.112, f32[1,4,16,128]{3,2,1,0:T(8,128)S(1)} %get-tuple-element.109, ...), kind=kLoop, calls=%fused_computation.7 | loop fusion | flops 8871936 | bytes 2080787 | tf_op jit(solution)/shard_map/transpose(jvp())/add_any | solution.py:78
  (138 shorter events, 18.3 us)
Async XLA Ops:
  0.6 1.2 %copy-start.7 = (f32[7,4,16,128]{3,2,1,0:T(8,128)S(1)}, f32[7,4,16,128]{3,2,1,0:T(8,128)}, u32[]{:S(2)}) copy-start(f32[7,4,16,128]{3,2,1,0:T(8,128)} %param.30) | copy-start | bytes 688132
  0.6 6.8 %copy-start.4 = (f32[10,16,128]{2,1,0:T(8,128)S(1)}, f32[10,16,128]{2,1,0:T(8,128)}, u32[]{:S(2)}) copy-start(f32[10,16,128]{2,1,0:T(8,128)} %param.31) | copy-start | bytes 245764
  0.7 14.1 %copy-start.32 = (s32[16,128]{1,0:T(8,128)S(1)}, s32[16,128]{1,0:T(8,128)}, u32[]{:S(2)}) copy-start(s32[16,128]{1,0:T(8,128)} %param.27) | copy-start | bytes 24580
  0.7 14.2 %copy-start.33 = (f32[3,64]{1,0:T(4,128)S(1)}, f32[3,64]{1,0:T(4,128)}, u32[]{:S(2)}) copy-start(f32[3,64]{1,0:T(4,128)} %param.28) | copy-start | bytes 2308
  1.9 29.8 %copy-start.11 = (s32[4,16,128]{2,1,0:T(8,128)S(1)}, s32[4,16,128]{2,1,0:T(8,128)}, u32[]{:S(2)}) copy-start(s32[4,16,128]{2,1,0:T(8,128)} %param.26) | copy-start | bytes 98308
  1.9 30.4 %copy-start = (f32[19,4,16,128]{3,2,1,0:T(8,128)S(1)}, f32[19,4,16,128]{3,2,1,0:T(8,128)}, u32[]{:S(2)}) copy-start(f32[19,4,16,128]{3,2,1,0:T(8,128)} %param.24) | copy-start | bytes 1867780
  2.0 30.3 %copy-start.8 = (f32[7,4,16,128]{3,2,1,0:T(8,128)S(1)}, f32[7,4,16,128]{3,2,1,0:T(8,128)}, u32[]{:S(2)}) copy-start(f32[7,4,16,128]{3,2,1,0:T(8,128)} %param.25) | copy-start | bytes 688132
  2.0 33.8 %collective-permute-start = (f32[26,4,1,128]{3,2,1,0:T(1,128)S(1)}, f32[26,4,1,128]{3,2,1,0:T(1,128)S(1)}, u32[]{:S(2)}, u32[]{:S(2)}) collective-permute-start(f32[26,4,1,128]{3,2,1,0:T(1,128)S(1)} %get-tuple-element.133), channel_id=1, source_target_pairs={{8,0},{16,8},{24,16},{9,1},{17,9},{25,17},{10,2},{18,10},{26,18},{... | collective-permute-start | bytes 159752 | tf_op jit(solution)/shard_map/ppermute | solution.py:46
  4.2 31.5 %collective-permute-start.1 = (f32[26,4,1,128]{3,2,1,0:T(1,128)S(1)}, f32[26,4,1,128]{3,2,1,0:T(1,128)S(1)}, u32[]{:S(2)}, u32[]{:S(2)}) collective-permute-start(f32[26,4,1,128]{3,2,1,0:T(1,128)S(1)} %get-tuple-element.132), channel_id=1, source_target_pairs={{0,8},{8,16},{16,24},{1,9},{9,17},{17,25},{2,10},{10,18},{18,26},{... | collective-permute-start | bytes 159752 | tf_op jit(solution)/shard_map/ppermute | solution.py:45
  7.5 9.5 %collective-permute-start.6 = (f32[10,1,128]{2,1,0:T(1,128)S(1)}, f32[10,1,128]{2,1,0:T(1,128)S(1)}, u32[]{:S(2)}, u32[]{:S(2)}) collective-permute-start(f32[10,1,128]{2,1,0:T(1,128)S(1)} %get-tuple-element.171), channel_id=1, source_target_pairs={{0,8},{8,16},{16,24},{1,9},{9,17},{17,25},{2,10},{10,18},{18,26},{... | collective-permute-start | bytes 15368 | tf_op jit(solution)/shard_map/ppermute | solution.py:45
  9.4 7.6 %collective-permute-start.7 = (f32[10,1,128]{2,1,0:T(1,128)S(1)}, f32[10,1,128]{2,1,0:T(1,128)S(1)}, u32[]{:S(2)}, u32[]{:S(2)}) collective-permute-start(f32[10,1,128]{2,1,0:T(1,128)S(1)} %get-tuple-element.172), channel_id=1, source_target_pairs={{8,0},{16,8},{24,16},{9,1},{17,9},{25,17},{10,2},{18,10},{26,18},{... | collective-permute-start | bytes 15368 | tf_op jit(solution)/shard_map/ppermute | solution.py:46
  17.1 7.4 %collective-permute-start.8 = (f32[10,18,1]{2,1,0:T(8,128)S(1)}, f32[10,18,1]{2,1,0:T(8,128)S(1)}, u32[]{:S(2)}, u32[]{:S(2)}) collective-permute-start(f32[10,18,1]{2,1,0:T(8,128)S(1)} %get-tuple-element.168), channel_id=1, source_target_pairs={{0,2},{2,4},{4,6},{1,3},{3,5},{5,7},{8,10},{10,12},{12,14},{9,11},... | collective-permute-start | bytes 2168 | tf_op jit(solution)/shard_map/ppermute | solution.py:45
  22.0 6.2 %collective-permute-start.9 = (f32[10,18,1]{2,1,0:T(8,128)S(1)}, f32[10,18,1]{2,1,0:T(8,128)S(1)}, u32[]{:S(2)}, u32[]{:S(2)}) collective-permute-start(f32[10,18,1]{2,1,0:T(8,128)S(1)} %get-tuple-element.167), channel_id=1, source_target_pairs={{2,0},{4,2},{6,4},{3,1},{5,3},{7,5},{10,8},{12,10},{14,12},{11,9},... | collective-permute-start | bytes 2168 | tf_op jit(solution)/shard_map/ppermute | solution.py:46
  28.2 4.7 %collective-permute-start.10 = (f32[1,18,130]{2,1,0:T(8,128)S(1)}, f32[1,18,130]{2,1,0:T(8,128)S(1)}, u32[]{:S(2)}, u32[]{:S(2)}) collective-permute-start(f32[1,18,130]{2,1,0:T(8,128)S(1)} %get-tuple-element.157), channel_id=1, source_target_pairs={{1,0},{3,2},{5,4},{7,6},{9,8},{11,10},{13,12},{15,14},{17,16},{19,... | collective-permute-start | bytes 28088 | tf_op jit(solution)/shard_map/ppermute | solution.py:46
  30.4 4.6 %collective-permute-start.11 = (f32[1,18,130]{2,1,0:T(8,128)S(1)}, f32[1,18,130]{2,1,0:T(8,128)S(1)}, u32[]{:S(2)}, u32[]{:S(2)}) collective-permute-start(f32[1,18,130]{2,1,0:T(8,128)S(1)} %get-tuple-element.158), channel_id=1, source_target_pairs={{0,1},{2,3},{4,5},{6,7},{8,9},{10,11},{12,13},{14,15},{16,17},{18,... | collective-permute-start | bytes 28088 | tf_op jit(solution)/shard_map/ppermute | solution.py:45
  38.4 6.9 %collective-permute-start.2 = (f32[26,4,18,1]{0,1,3,2:T(4,128)}, f32[26,4,18,1]{0,1,3,2:T(4,128)S(1)}, u32[]{:S(2)}, u32[]{:S(2)}) collective-permute-start(f32[26,4,18,1]{0,1,3,2:T(4,128)} %copy.102), channel_id=1, source_target_pairs={{2,0},{4,2},{6,4},{3,1},{5,3},{7,5},{10,8},{12,10},{14,12},{11,9},... | collective-permute-start | bytes 22472 | tf_op jit(solution)/shard_map/ppermute | solution.py:46
  41.0 5.5 %collective-permute-start.3 = (f32[26,4,18,1]{0,1,3,2:T(4,128)S(1)}, f32[26,4,18,1]{0,1,3,2:T(4,128)}, u32[]{:S(2)}, u32[]{:S(2)}) collective-permute-start(f32[26,4,18,1]{0,1,3,2:T(4,128)S(1)} %copy.104), channel_id=1, source_target_pairs={{0,2},{2,4},{4,6},{1,3},{3,5},{5,7},{8,10},{10,12},{12,14},{9,11},... | collective-permute-start | bytes 22472 | tf_op jit(solution)/shard_map/ppermute | solution.py:45
  49.2 4.4 %copy-start.2 = (f32[19,4,16,128]{3,2,1,0:T(8,128)S(1)}, f32[19,4,16,128]{3,2,1,0:T(8,128)}, u32[]{:S(2)}) copy-start(f32[19,4,16,128]{3,2,1,0:T(8,128)} %constant_dynamic-update-slice_fusion.19) | copy-start | bytes 1867780
  49.7 12.6 %collective-permute-start.4 = (f32[26,1,18,130]{3,1,2,0:T(1,128)S(1)}, f32[26,1,18,130]{3,1,2,0:T(1,128)S(1)}, u32[]{:S(2)}, u32[]{:S(2)}) collective-permute-start(f32[26,1,18,130]{3,1,2,0:T(1,128)S(1)} %copy.108), channel_id=1, source_target_pairs={{1,0},{3,2},{5,4},{7,6},{9,8},{11,10},{13,12},{15,14},{17,16},{19,... | collective-permute-start | bytes 730088 | tf_op jit(solution)/shard_map/ppermute | solution.py:46
  52.3 14.8 %collective-permute-start.5 = (f32[26,1,18,130]{3,1,2,0:T(1,128)S(1)}, f32[26,1,18,130]{3,1,2,0:T(1,128)S(1)}, u32[]{:S(2)}, u32[]{:S(2)}) collective-permute-start(f32[26,1,18,130]{3,1,2,0:T(1,128)S(1)} %copy.110), channel_id=1, source_target_pairs={{0,1},{2,3},{4,5},{6,7},{8,9},{10,11},{12,13},{14,15},{16,17},{18,... | collective-permute-start | bytes 730088 | tf_op jit(solution)/shard_map/ppermute | solution.py:45
  69.1 3.7 %copy-start.9 = (pred[4,16,128]{2,1,0:T(8,128)(4,1)S(1)}, pred[4,16,128]{2,1,0:T(8,128)(4,1)}, u32[]{:S(2)}) copy-start(pred[4,16,128]{2,1,0:T(8,128)(4,1)} %get-tuple-element.192) | copy-start | bytes 24580
  72.9 1.2 %copy-start.5 = (f32[4,16,128]{2,1,0:T(8,128)S(1)}, f32[4,16,128]{2,1,0:T(8,128)}, u32[]{:S(2)}) copy-start(f32[4,16,128]{2,1,0:T(8,128)} %reduce_sum.29) | copy-start | bytes 98308
  75.4 1.4 %copy-start.34 = (pred[19]{0:T(512)(128)(4,1)S(1)}, pred[19]{0:T(512)(128)(4,1)}, u32[]{:S(2)}) copy-start(pred[19]{0:T(512)(128)(4,1)} %constant.292.clone.1) | copy-start | bytes 61
  75.7 2.2 %copy-start.6 = (f32[7,4,16,128]{3,2,1,0:T(8,128)}, f32[7,4,16,128]{3,2,1,0:T(8,128)S(1)}, u32[]{:S(2)}) copy-start(f32[7,4,16,128]{3,2,1,0:T(8,128)S(1)} %fusion.10) | copy-start | bytes 688132
  (24 other events, 18.5 us)
where the time goes:
time: 78.8 us; the launch traced here: 77.9 us
  starting transfers between devices  29.7 us (38%)
  waiting for transfers between devices  18.8 us (24%)
  other arithmetic  15 us (19%)
  local copies, waits for them, and re-layouts  13 us (16%)
  between operations  1.38 us (2%)
    ppermute x6, starting transfers between devices, with_halo(): before = lax.ppermute(last, axis, up)  16.1 us
    ppermute x6, starting transfers between devices, with_halo(): after = lax.ppermute(first, axis, down)  13.6 us
    ppermute x6, waiting for transfers between devices, with_halo(): after = lax.ppermute(first, axis, down)  12.2 us
    ppermute x6, waiting for transfers between devices, with_halo(): before = lax.ppermute(last, axis, up)  6.62 us
    unnamed x75, local copies, waits for them, and re-layouts  6.1 us
    scatter-add x4, other arithmetic, local(): star_flow.at[q, 0].add(jnp.where(base, cot_flow[OPPOSITE[q], 0], 0.0))  2.8 us
    mul x4, other arithmetic, flow_equilibrium(): weight * density  2.53 us
    ppermute x2, local copies, waits for them, and re-layouts, with_halo(): before = lax.ppermute(last, axis, up)  1.99 us
  transfers between devices with their start and end apart: 12, of which 4 were waited for; matrix products, arithmetic and copies ran while one was open for 13% of the time, Pallas kernels for 0%

commit v1 on v0

v1 whole, which is shorter than its diff:
```python
import functools

import jax
import jax.numpy as jnp
from jax import lax
from jax.experimental import pallas as pl
from jax.experimental.pallas import tpu as pltpu
from jax.sharding import PartitionSpec as P

VELOCITY = (
    (0, 0, 0),
    (1, 0, 0),
    (-1, 0, 0),
    (0, 1, 0),
    (0, -1, 0),
    (0, 0, 1),
    (0, 0, -1),
    (1, 1, 0),
    (-1, -1, 0),
    (1, -1, 0),
    (-1, 1, 0),
    (1, 0, 1),
    (-1, 0, -1),
    (1, 0, -1),
    (-1, 0, 1),
    (0, 1, 1),
    (0, -1, -1),
    (0, 1, -1),
    (0, -1, 1),
)
OPPOSITE = tuple((VELOCITY.index((-a, -b, -c)) for a, b, c in VELOCITY))
WEIGHTS_FLOW = (1.0 / 3.0,) + (1.0 / 18.0,) * 6 + (1.0 / 36.0,) * 12
WEIGHTS_HEAT = (0.25,) + (0.125,) * 6
FLOW = 19
HEAT = 7
DIRECTIONS = VELOCITY + VELOCITY[:HEAT]
tau_flow = 0.8
tau_heat = 0.9
diffusion = 0.12
coupling = 0.3

AXES = ("gx", "gy", "gz")
COMPONENT = {"gx": 0, "gy": 1, "gz": 2}
VMEM_LIMIT = 8 << 20


def moving(component, sign):
    return [k for k, c in enumerate(DIRECTIONS) if c[component] == sign]


XP, XM = moving(0, 1), moving(0, -1)
YP, YM = moving(1, 1), moving(1, -1)
ZP, ZM = moving(2, 1), moving(2, -1)
XZP = [k for k in ZP if DIRECTIONS[k][0] != 0]
XZM = [k for k in ZM if DIRECTIONS[k][0] != 0]


def rounds(size):
    return 1 if size == 2 else 2


def swap(value, axis, turn):
    sizes = [lax.axis_size(name) for name in AXES]
    at = AXES.index(axis)
    pairs = []
    for a in range(sizes[0]):
        for b in range(sizes[1]):
            for c in range(sizes[2]):
                here = [a, b, c]
                there = [a, b, c]
                i = here[at]
                j = i ^ 1 if turn == 0 else (i + 1 if i % 2 else i - 1)
                if 0 <= j < sizes[at]:
                    there[at] = j
                elif axis == "gy":
                    there[at] = sizes[at] - 1 - i
                else:
                    there[1] = b ^ 1
                flat = lambda p: (p[0] * sizes[1] + p[1]) * sizes[2] + p[2]
                pairs.append((flat(here), flat(there)))
    return lax.ppermute(value, AXES, pairs)


def place(axis):
    i = lax.axis_index(axis)
    return lax.rem(i, 2) == 0, i < lax.axis_size(axis) - 1, i > 0


def outgoing(axis, turn, to_higher, to_lower):
    even, _, _ = place(axis)
    return jnp.where(even, to_higher, to_lower) if turn == 0 else jnp.where(even, to_lower, to_higher)


def incoming(axis, turns):
    even, higher, lower = place(axis)
    first, last = turns[0], turns[-1]
    zero = jnp.zeros_like(first)
    above = jnp.where(higher, jnp.where(even, first, last), zero)
    below = jnp.where(lower, jnp.where(even, last, first), zero)
    return above, below


def slab(cot_flow, cot_heat, k, z):
    return cot_flow[k, z] if k < FLOW else cot_heat[k - FLOW, z]


def row_of(cot_flow, cot_heat, k, z, x):
    return cot_flow[k, z, x : x + 1, :] if k < FLOW else cot_heat[k - FLOW, z, x : x + 1, :]


def padded(rows):
    return -(-rows // 8) * 8


def pack_faces(nzt, nxt, cot_flow, cot_heat, cot_plate, *outs):
    depth, width = cot_flow.shape[1], cot_flow.shape[2]
    layers = cot_plate.shape[0]
    for turn in range(nzt):
        out = outs[turn]
        for n, (hi, lo) in enumerate(zip(ZM, ZP)):
            out[n * width : (n + 1) * width, :] = outgoing(
                "gz", turn, slab(cot_flow, cot_heat, hi, depth - 1), slab(cot_flow, cot_heat, lo, 0)
            )
        n = len(ZM)
        out[n * width : (n + 1) * width, :] = outgoing("gz", turn, cot_plate[layers - 1], cot_plate[0])
    for turn in range(nxt):
        out = outs[nzt + turn]
        for n, (hi, lo) in enumerate(zip(XM, XP)):
            for z in range(depth):
                r = n * depth + z
                out[r : r + 1, :] = outgoing(
                    "gx",
                    turn,
                    row_of(cot_flow, cot_heat, hi, z, width - 1),
                    row_of(cot_flow, cot_heat, lo, z, 0),
                )
        for l in range(layers):
            r = len(XM) * depth + l
            out[r : r + 1, :] = outgoing(
                "gx", turn, cot_plate[l, width - 1 : width, :], cot_plate[l, 0:1, :]
            )


class Halo:
    def __init__(self, cot_flow, cot_heat, z_in, x_in, xz_in):
        self.flow, self.heat = cot_flow, cot_heat
        self.depth, self.width = cot_flow.shape[1], cot_flow.shape[2]
        self.z_in, self.x_in, self.xz_in = z_in, x_in, xz_in

    def face(self, k, n=None):
        up = n is not None and n > 0 or (n is None and DIRECTIONS[k][2] == 1)
        at = (ZP if up else ZM).index(k) if n is None else len(ZP)
        rows = slice(at * self.width, (at + 1) * self.width)
        above, below = incoming("gz", [r[rows, :] for r in self.z_in])
        return above if up else below

    def row(self, k, z):
        up = DIRECTIONS[k][0] == 1
        if 0 <= z < self.depth:
            at = (XP if up else XM).index(k) * self.depth + z
            above, below = incoming("gx", [r[at : at + 1, :] for r in self.x_in])
            return above if up else below
        from_above = z >= self.depth
        at = (XZP if from_above else XZM).index(k)
        above, below = incoming("gz", [r[at : at + 1, :] for r in self.xz_in])
        return above if from_above else below

    def shifted(self, k, z):
        cx, _, cz = DIRECTIONS[k]
        at = z + cz
        plane = slab(self.flow, self.heat, k, at) if 0 <= at < self.depth else self.face(k)
        if cx == 0:
            return plane
        return shift_rows(plane, cx, self.row(k, at))


def shift_rows(plane, sign, halo_row):
    width = plane.shape[0]
    x = lax.broadcasted_iota(jnp.int32, plane.shape, 0)
    if sign == 1:
        return jnp.where(x == width - 1, halo_row, pltpu.roll(plane, width - 1, 0))
    return jnp.where(x == 0, halo_row, pltpu.roll(plane, 1, 0))


def shift_lanes(plane, sign, halo, lane):
    length = plane.shape[1]
    y = lax.broadcasted_iota(jnp.int32, plane.shape, 1)
    edge = length - 1 if sign == 1 else 0
    turn = (edge - lane) % length
    column = pltpu.roll(halo, turn, 1) if turn else halo
    return jnp.where(y == edge, column, pltpu.roll(plane, length - 1 if sign == 1 else 1, 1))


def pack_edges(nzt, nxt, nyt, cot_flow, cot_heat, cot_plate, *refs):
    z_in, x_in = refs[:nzt], refs[nzt : nzt + nxt]
    outs = refs[nzt + nxt :]
    halo = Halo(cot_flow, cot_heat, z_in, x_in, None)
    depth, width = halo.depth, halo.width
    length = cot_flow.shape[3]
    layers = cot_plate.shape[0]
    y = lax.broadcasted_iota(jnp.int32, (width, length), 1)

    def put(packed, plane, source, lane):
        turn = (lane - source) % length
        return jnp.where(y == lane, pltpu.roll(plane, turn, 1) if turn else plane, packed)

    packs = []
    for side, source in ((YM, length - 1), (YP, 0)):
        packed = jnp.zeros((width, length), jnp.float32)
        for n, k in enumerate(side):
            for z in range(depth):
                packed = put(packed, halo.shifted(k, z), source, n * depth + z)
        for l in range(layers):
            packed = put(packed, cot_plate[l], source, len(side) * depth + l)
        packs.append(packed)
    for turn in range(nyt):
        outs[turn][...] = outgoing("gy", turn, packs[0], packs[1])
    for turn in range(nzt):
        out = outs[nyt + turn]
        out[...] = jnp.zeros_like(out)
        for n, (hi, lo) in enumerate(zip(XZM, XZP)):
            out[n : n + 1, :] = outgoing("gz", turn, halo.row(hi, depth - 1), halo.row(lo, 0))


def prepare(pop_flow, pop_heat, flags, nozzle, jet_velocity, ue_out, ratio_out):
    jets = [jnp.zeros(nozzle.shape, jnp.float32)] * 3
    which = nozzle[...]
    for n in range(jet_velocity.shape[1]):
        hit = which == n
        jets = [jnp.where(hit, jet_velocity[c, n], jets[c]) for c in range(3)]
    for z in range(pop_flow.shape[1]):
        inlet = flags[z] == 2
        pops = [pop_flow[q, z] for q in range(FLOW)]
        rho = sum(pops[1:], pops[0])
        inverse = 1.0 / rho
        for c in range(3):
            plus = [pops[q] for q in range(FLOW) if VELOCITY[q][c] == 1]
            minus = [pops[q] for q in range(FLOW) if VELOCITY[q][c] == -1]
            total = sum(plus[1:], plus[0]) - sum(minus[1:], minus[0])
            ue_out[c, z] = jnp.where(inlet, jets[c], total * inverse)
        heat = [pop_heat[q, z] for q in range(HEAT)]
        ratio_out[z] = sum(heat[1:], heat[0]) * inverse


def finish(nzt, nxt, nyt, flags, ue_in, ratio_in, cot_flow, cot_heat, cot_plate, *refs):
    z_in, refs = refs[:nzt], refs[nzt:]
    x_in, refs = refs[:nxt], refs[nxt:]
    y_in, refs = refs[:nyt], refs[nyt:]
    xz_in, (grad_flow, grad_heat, grad_plate) = refs[:nzt], refs[nzt:]
    halo = Halo(cot_flow, cot_heat, z_in, x_in, xz_in)
    depth, width = halo.depth, halo.width
    layers = cot_plate.shape[0]
    y_above, y_below = incoming("gy", [r[...] for r in y_in])
    base = lax.axis_index("gz") == 0

    for z in range(depth):
        star = []
        for k, (cx, cy, cz) in enumerate(DIRECTIONS):
            plane = halo.shifted(k, z)
            if cy == 1:
                plane = shift_lanes(plane, 1, y_above, YP.index(k) * depth + z)
            elif cy == -1:
                plane = shift_lanes(plane, -1, y_below, YM.index(k) * depth + z)
            if cz == -1 and z == 0:
                if k < FLOW:
                    bounced = cot_flow[OPPOSITE[k], 0]
                else:
                    bounced = -cot_heat[OPPOSITE[k - FLOW], 0]
                plane = jnp.where(base, bounced, plane)
            star.append(plane)
        kind = flags[z]
        wall, inlet = kind == 1, kind == 2
        ue = [ue_in[c, z] for c in range(3)]
        ratio = ratio_in[z]
        s, t = star[:FLOW], star[FLOW:]

        zero_moment = WEIGHTS_FLOW[0] * s[0]
        first = [None] * 3
        second = {}
        add = lambda a, b: b if a is None else a + b
        pair_sum = None
        for group, weight in ((range(1, 7), WEIGHTS_FLOW[1]), (range(7, 19), WEIGHTS_FLOW[7])):
            odd = [None] * 3
            even = {}
            total = None
            for q in group:
                o = OPPOSITE[q]
                if o < q:
                    continue
                c = VELOCITY[q]
                plus, minus = s[q] + s[o], s[q] - s[o]
                total = add(total, plus)
                for i in range(3):
                    if c[i]:
                        odd[i] = add(odd[i], minus if c[i] == 1 else -minus)
                    for j in range(i, 3):
                        if c[i] * c[j]:
                            even[i, j] = add(even.get((i, j)), plus if c[i] * c[j] == 1 else -plus)
            zero_moment = zero_moment + weight * total
            for i in range(3):
                first[i] = add(first[i], weight * odd[i])
            for key, value in even.items():
                second[key] = add(second.get(key), weight * value)
        heat_first = [WEIGHTS_HEAT[1] * (t[2 * c + 1] - t[2 * c + 2]) for c in range(3)]
        heat_zero = WEIGHTS_HEAT[0] * t[0] + WEIGHTS_HEAT[1] * (
            (t[1] + t[2]) + (t[3] + t[4]) + (t[5] + t[6])
        )

        bent = [
            sum(second[min(i, j), max(i, j)] * ue[j] for j in range(3)) for i in range(3)
        ]
        dot = lambda a, b: a[0] * b[0] + a[1] * b[1] + a[2] * b[2]
        speed = dot(ue, ue)
        gain = zero_moment * (1.0 - 1.5 * speed) + 3.0 * dot(first, ue) + 4.5 * dot(bent, ue)
        pull = [
            (3.0 / tau_flow) * (first[i] + 3.0 * bent[i] - ue[i] * zero_moment)
            + (4.0 / tau_heat) * ratio * heat_first[i]
            for i in range(3)
        ]
        common = jnp.where(inlet, gain, (1.0 / tau_flow) * gain - dot(ue, pull))
        pull = [jnp.where(inlet, 0.0, p) for p in pull]
        keep = jnp.where(inlet, 0.0, 1.0 - 1.0 / tau_flow)
        for q in range(FLOW):
            o = OPPOSITE[q]
            value = keep * s[q] + common
            for i in range(3):
                if VELOCITY[q][i] == 1:
                    value = value + pull[i]
                elif VELOCITY[q][i] == -1:
                    value = value - pull[i]
            grad_flow[q, z] = jnp.where(wall, s[o], value)
        heat_common = jnp.where(
            inlet, 0.0, (1.0 / tau_heat) * (heat_zero + 4.0 * dot(heat_first, ue))
        )
        heat_keep = jnp.where(inlet, 0.0, 1.0 - 1.0 / tau_heat)
        for q in range(HEAT):
            value = jnp.where(wall, t[OPPOSITE[q]], heat_keep * t[q] + heat_common)
            if z == 0:
                value = value + jnp.where(base, coupling * cot_plate[0], 0.0)
            grad_heat[q, z] = value

    x_above, x_below = incoming("gx", [r[...] for r in x_in])
    z_rows = slice(len(ZP) * width, (len(ZP) + 1) * width)
    z_above, z_below = incoming("gz", [r[z_rows, :] for r in z_in])
    for l in range(layers):
        own = cot_plate[l]
        up = cot_plate[l + 1] if l + 1 < layers else z_above
        down = cot_plate[l - 1] if l > 0 else z_below
        r = len(XP) * depth + l
        total = up + down
        total = total + shift_rows(own, 1, x_above[r : r + 1, :])
        total = total + shift_rows(own, -1, x_below[r : r + 1, :])
        total = total + shift_lanes(own, 1, y_above, len(YP) * depth + l)
        total = total + shift_lanes(own, -1, y_below, len(YM) * depth + l)
        value = own + diffusion * (total - 6.0 * own)
        if l == 0:
            value = value + jnp.where(base, 0.25 * cot_heat[5, 0] - coupling * own, 0.0)
        grad_plate[l] = value


def kernel_call(body, shapes, count, smem=(), name=None):
    specs = [
        pl.BlockSpec(memory_space=pltpu.SMEM if i in smem else pltpu.VMEM) for i in range(count)
    ]
    return pl.pallas_call(
        body,
        out_shape=[jax.ShapeDtypeStruct(s, jnp.float32) for s in shapes],
        in_specs=specs,
        out_specs=[pl.BlockSpec(memory_space=pltpu.VMEM)] * len(shapes),
        compiler_params=pltpu.CompilerParams(vmem_limit_bytes=VMEM_LIMIT),
        name=name,
    )


def local(pop_flow, pop_heat, flags, nozzle_id, jet_velocity, cot_flow, cot_heat, cot_plate):
    nxt, nyt, nzt = (rounds(lax.axis_size(a)) for a in AXES)
    _, depth, width, length = cot_flow.shape
    layers = cot_plate.shape[0]
    cots = (cot_flow, cot_heat, cot_plate)
    face = ((len(ZM) + 1) * width, length)
    side = (padded(len(XM) * depth + layers), length)
    sends = kernel_call(
        functools.partial(pack_faces, nzt, nxt), [face] * nzt + [side] * nxt, 3, name="faces"
    )(*cots)
    z_in = [swap(sends[t], "gz", t) for t in range(nzt)]
    x_in = [swap(sends[nzt + t], "gx", t) for t in range(nxt)]
    ue, ratio = kernel_call(
        prepare, [(3, depth, width, length), (depth, width, length)], 5, (4,), name="prepare"
    )(pop_flow, pop_heat, flags, nozzle_id, jet_velocity)
    sends = kernel_call(
        functools.partial(pack_edges, nzt, nxt, nyt),
        [(width, length)] * nyt + [(8, length)] * nzt,
        3 + nzt + nxt,
        name="edges",
    )(*cots, *z_in, *x_in)
    y_in = [swap(sends[t], "gy", t) for t in range(nyt)]
    xz_in = [swap(sends[nyt + t], "gz", t) for t in range(nzt)]
    return tuple(
        kernel_call(
            functools.partial(finish, nzt, nxt, nyt),
            [cot_flow.shape, cot_heat.shape, cot_plate.shape],
            6 + 2 * nzt + nxt + nyt,
            name="finish",
        )(flags, ue, ratio, *cots, *z_in, *x_in, *y_in, *xz_in)
    )


def solution(mesh):
    return jax.shard_map(
        local,
        mesh=mesh,
        in_specs=(
            P(None, "gz", "gx", "gy"),
            P(None, "gz", "gx", "gy"),
            P("gz", "gx", "gy"),
            P("gx", "gy"),
            P(),
            P(None, "gz", "gx", "gy"),
            P(None, "gz", "gx", "gy"),
            P("gz", "gx", "gy"),
        ),
        out_specs=(P(None, "gz", "gx", "gy"), P(None, "gz", "gx", "gy"), P("gz", "gx", "gy")),
        check_vma=False,
    )
```

time: 78.8 us -> 17.8 us (0.23)
  the two profiles are of different devices: /device:TPU:21 before, /device:TPU:0 now
where the time goes in v1:
time: 17.8 us; the launch traced here: 17.4 us
  starting transfers between devices  6.8 us (38%)
  waiting for transfers between devices  4.5 us (25%)
  local copies, waits for them, and re-layouts  2.94 us (17%)
  Pallas kernels  2.45 us (14%)
  between operations  0.73 us (4%)
    ppermute x6, starting transfers between devices, swap(): return lax.ppermute(value, AXES, pairs)  6.8 us
    ppermute x6, waiting for transfers between devices, swap(): return lax.ppermute(value, AXES, pairs)  4.5 us
    unnamed x22, local copies, waits for them, and re-layouts  2.94 us
    pallas_call x1, Pallas kernels, local(): kernel_call(functools.partial(finish, nzt, nxt, nyt), [cot_flow.shape, co...  1.41 us
    pallas_call x1, Pallas kernels, local(): kernel_call(prepare, [(3, depth, width, length), (depth, width, length)],...  0.78 us
  transfers between devices with their start and end apart: 6, of which 2 were waited for; matrix products, arithmetic and copies ran while one was open for 0% of the time, Pallas kernels for 4%

profile of v1, /device:TPU:0, one launch (start us, length us, event | category | flops | bytes accessed | tf_op | source)
XLA Modules:
  0.0 17.4 jit_solution(7045946435013000462)
XLA Ops:
  0.6 0.0 copy-start
  0.6 1.1 %copy-done = f32[19,4,16,128]{3,2,1,0:T(8,128)S(1)} copy-done((f32[19,4,16,128]{3,2,1,0:T(8,128)S(1)}, f32[19,4,16,128]{3,2,1,0:T(8,128)}, u32[]{:S(2)}) %copy-start) | copy-done | bytes 622616
  1.7 0.9 %copy-done.2 = f32[7,4,16,128]{3,2,1,0:T(8,128)S(1)} copy-done((f32[7,4,16,128]{3,2,1,0:T(8,128)S(1)}, f32[7,4,16,128]{3,2,1,0:T(8,128)}, u32[]{:S(2)}) %copy-start.2) | copy-done | bytes 229400
  2.6 0.9 %copy-done.4 = f32[10,16,128]{2,1,0:T(8,128)S(1)} copy-done((f32[10,16,128]{2,1,0:T(8,128)S(1)}, f32[10,16,128]{2,1,0:T(8,128)}, u32[]{:S(2)}) %copy-start.4) | copy-done | bytes 81944
  3.6 0.0 copy-start.6
  3.6 3.0 %collective-permute-start = (f32[112,128]{1,0:T(8,128)S(1)}, f32[112,128]{1,0:T(8,128)S(1)}, u32[]{:S(2)}, u32[]{:S(2)}) collective-permute-start(f32[112,128]{1,0:T(8,128)S(1)} %get-tuple-element.13), channel_id=1, source_target_pairs={{0,1},{1,0},{2,3},{3,2},{4,5},{5,4},{6,7},{7,6},{8,9},{9,8},{10,11... | collective-permute-start | bytes 172040 | tf_op jit(solution)/shard_map/ppermute | solution.py:81
  6.6 1.6 %collective-permute-start.1 = (f32[40,128]{1,0:T(8,128)S(1)}, f32[40,128]{1,0:T(8,128)S(1)}, u32[]{:S(2)}, u32[]{:S(2)}) collective-permute-start(f32[40,128]{1,0:T(8,128)S(1)} %get-tuple-element.14), channel_id=1, source_target_pairs={{0,8},{1,9},{2,10},{3,11},{4,12},{5,13},{6,14},{7,15},{8,0},{9,1},... | collective-permute-start | bytes 61448 | tf_op jit(solution)/shard_map/ppermute | solution.py:81
  8.2 0.0 collective-permute-start.2
  8.2 2.2 %collective-permute-done.1.refs_1_ = f32[40,128]{1,0:T(8,128)S(1)} collective-permute-done((f32[40,128]{1,0:T(8,128)S(1)}, f32[40,128]{1,0:T(8,128)S(1)}, u32[]{:S(2)}, u32[]{:S(2)}) %collective-permute-start.1) | collective-permute-done | bytes 20512 | tf_op jit(solution)/shard_map/ppermute | solution.py:81
  10.4 0.0 collective-permute-done.2.refs_2_
  10.4 0.0 collective-permute-done.refs_0_
  10.4 0.0 copy-start.10
  10.4 0.0 copy-start.5
  10.4 0.2 %edges.1 = (f32[16,128]{1,0:T(8,128)S(1)}, f32[16,128]{1,0:T(8,128)S(1)}, f32[8,128]{1,0:T(8,128)S(1)}) custom-call(f32[19,4,16,128]{3,2,1,0:T(8,128)S(1)} %copy-done, f32[7,4,16,128]{3,2,1,0:T(8,128)S(1)} %copy-done.2, f32[10,16,128]{2,1,0:T(8,128)S(1)} %copy-done.4, f32[112,128]{1,0:T(8,128)S(1)} %collective-permute-done.refs_0_, ...), custom_call_target="tpu_custom_call" | custom-call | tf_op jit(solution)/shard_map/edges/pallas_call | solution.py:390
  10.7 0.0 copy-start.1
  10.7 0.1 collective-permute-start.3
  10.7 1.6 %collective-permute-start.4 = (f32[16,128]{1,0:T(8,128)S(1)}, f32[16,128]{1,0:T(8,128)S(1)}, u32[]{:S(2)}, u32[]{:S(2)}) collective-permute-start(f32[16,128]{1,0:T(8,128)S(1)} %get-tuple-element.17), channel_id=1, source_target_pairs={{0,6},{1,7},{2,4},{3,5},{4,2},{5,3},{6,0},{7,1},{8,14},{9,15},{10,... | collective-permute-start | bytes 24584 | tf_op jit(solution)/shard_map/ppermute | solution.py:81
  12.4 0.5 %collective-permute-start.5 = (f32[8,128]{1,0:T(8,128)S(1)}, f32[8,128]{1,0:T(8,128)S(1)}, u32[]{:S(2)}, u32[]{:S(2)}) collective-permute-start(f32[8,128]{1,0:T(8,128)S(1)} %get-tuple-element.18), channel_id=1, source_target_pairs={{0,1},{1,0},{2,3},{3,2},{4,5},{5,4},{6,7},{7,6},{8,9},{9,8},{10,11... | collective-permute-start | bytes 12296 | tf_op jit(solution)/shard_map/ppermute | solution.py:81
  12.9 0.0 copy-done.7
  12.9 0.8 %prepare.1 = (f32[3,4,16,128]{3,2,1,0:T(8,128)S(1)}, f32[4,16,128]{2,1,0:T(8,128)S(1)}) custom-call(f32[19,4,16,128]{3,2,1,0:T(8,128)S(1)} %copy-done.6, f32[7,4,16,128]{3,2,1,0:T(8,128)S(1)} %copy-done.7, s32[4,16,128]{2,1,0:T(8,128)S(1)} %copy-done.8, s32[16,128]{1,0:T(8,128)S(1)} %copy-done.9, f32[3,64]{1,0:T(4,128)S(1)} %copy-done.10), custom_call_target="tpu_custom_call" | custom-call | tf_op jit(solution)/shard_map/prepare/pallas_call | solution.py:387
  13.7 2.3 %collective-permute-done.5.refs_5_ = f32[8,128]{1,0:T(8,128)S(1)} collective-permute-done((f32[8,128]{1,0:T(8,128)S(1)}, f32[8,128]{1,0:T(8,128)S(1)}, u32[]{:S(2)}, u32[]{:S(2)}) %collective-permute-start.5) | collective-permute-done | bytes 4128 | tf_op jit(solution)/shard_map/ppermute | solution.py:81
  16.0 0.0 collective-permute-done.3.refs_3_
  16.0 0.0 collective-permute-done.4.refs_4_
  16.0 1.4 %finish.1 = (f32[19,4,16,128]{3,2,1,0:T(8,128)}, f32[7,4,16,128]{3,2,1,0:T(8,128)}, f32[10,16,128]{2,1,0:T(8,128)}) custom-call(s32[4,16,128]{2,1,0:T(8,128)S(1)} %copy-done.8, f32[3,4,16,128]{3,2,1,0:T(8,128)S(1)} %get-tuple-element.11.ue_in, f32[4,16,128]{2,1,0:T(8,128)S(1)} %get-tuple-element.12.ratio_in, f32[19,4,16,128]{3,2,1,0:T(8,128)S(1)} %copy-done.1, ...), custom_call_target="tpu_custom_call" | custom-call | tf_op jit(solution)/shard_map/finish/pallas_call | solution.py:399
  (14 shorter events, 0.1 us)
Async XLA Ops:
  0.6 1.1 %copy-start = (f32[19,4,16,128]{3,2,1,0:T(8,128)S(1)}, f32[19,4,16,128]{3,2,1,0:T(8,128)}, u32[]{:S(2)}) copy-start(f32[19,4,16,128]{3,2,1,0:T(8,128)} %cot_flow.5) | copy-start | bytes 1867780
  1.7 0.9 %copy-start.2 = (f32[7,4,16,128]{3,2,1,0:T(8,128)S(1)}, f32[7,4,16,128]{3,2,1,0:T(8,128)}, u32[]{:S(2)}) copy-start(f32[7,4,16,128]{3,2,1,0:T(8,128)} %cot_heat.5) | copy-start | bytes 688132
  2.6 0.9 %copy-start.4 = (f32[10,16,128]{2,1,0:T(8,128)S(1)}, f32[10,16,128]{2,1,0:T(8,128)}, u32[]{:S(2)}) copy-start(f32[10,16,128]{2,1,0:T(8,128)} %cot_plate.5) | copy-start | bytes 245764
  3.6 9.3 %copy-start.6 = (f32[19,4,16,128]{3,2,1,0:T(8,128)S(1)}, f32[19,4,16,128]{3,2,1,0:T(8,128)}, u32[]{:S(2)}) copy-start(f32[19,4,16,128]{3,2,1,0:T(8,128)} %pop_flow.1) | copy-start | bytes 1867780
  3.6 6.8 %collective-permute-start = (f32[112,128]{1,0:T(8,128)S(1)}, f32[112,128]{1,0:T(8,128)S(1)}, u32[]{:S(2)}, u32[]{:S(2)}) collective-permute-start(f32[112,128]{1,0:T(8,128)S(1)} %get-tuple-element.13), channel_id=1, source_target_pairs={{0,1},{1,0},{2,3},{3,2},{4,5},{5,4},{6,7},{7,6},{8,9},{9,8},{10,11... | collective-permute-start | bytes 172040 | tf_op jit(solution)/shard_map/ppermute | solution.py:81
  6.6 3.8 %collective-permute-start.1 = (f32[40,128]{1,0:T(8,128)S(1)}, f32[40,128]{1,0:T(8,128)S(1)}, u32[]{:S(2)}, u32[]{:S(2)}) collective-permute-start(f32[40,128]{1,0:T(8,128)S(1)} %get-tuple-element.14), channel_id=1, source_target_pairs={{0,8},{1,9},{2,10},{3,11},{4,12},{5,13},{6,14},{7,15},{8,0},{9,1},... | collective-permute-start | bytes 61448 | tf_op jit(solution)/shard_map/ppermute | solution.py:81
  8.2 4.7 %copy-start.7 = (f32[7,4,16,128]{3,2,1,0:T(8,128)S(1)}, f32[7,4,16,128]{3,2,1,0:T(8,128)}, u32[]{:S(2)}) copy-start(f32[7,4,16,128]{3,2,1,0:T(8,128)} %pop_heat.1) | copy-start | bytes 688132
  8.2 4.7 %copy-start.8 = (s32[4,16,128]{2,1,0:T(8,128)S(1)}, s32[4,16,128]{2,1,0:T(8,128)}, u32[]{:S(2)}) copy-start(s32[4,16,128]{2,1,0:T(8,128)} %flags.3) | copy-start | bytes 98308
  8.2 2.2 %collective-permute-start.2 = (f32[40,128]{1,0:T(8,128)S(1)}, f32[40,128]{1,0:T(8,128)S(1)}, u32[]{:S(2)}, u32[]{:S(2)}) collective-permute-start(f32[40,128]{1,0:T(8,128)S(1)} %get-tuple-element.15), channel_id=1, source_target_pairs={{0,2},{1,3},{2,0},{3,1},{4,6},{5,7},{6,4},{7,5},{8,16},{9,17},{10,... | collective-permute-start | bytes 61448 | tf_op jit(solution)/shard_map/ppermute | solution.py:81
  10.4 2.5 %copy-start.9 = (s32[16,128]{1,0:T(8,128)S(1)}, s32[16,128]{1,0:T(8,128)}, u32[]{:S(2)}) copy-start(s32[16,128]{1,0:T(8,128)} %nozzle.1) | copy-start | bytes 24580
  10.4 2.5 %copy-start.10 = (f32[3,64]{1,0:T(4,128)S(1)}, f32[3,64]{1,0:T(4,128)}, u32[]{:S(2)}) copy-start(f32[3,64]{1,0:T(4,128)} %jet_velocity.1) | copy-start | bytes 2308
  10.4 5.5 %copy-start.5 = (f32[10,16,128]{2,1,0:T(8,128)S(1)}, f32[10,16,128]{2,1,0:T(8,128)}, u32[]{:S(2)}) copy-start(f32[10,16,128]{2,1,0:T(8,128)} %cot_plate.5) | copy-start | bytes 245764
  10.7 5.3 %copy-start.1 = (f32[19,4,16,128]{3,2,1,0:T(8,128)S(1)}, f32[19,4,16,128]{3,2,1,0:T(8,128)}, u32[]{:S(2)}) copy-start(f32[19,4,16,128]{3,2,1,0:T(8,128)} %cot_flow.5) | copy-start | bytes 1867780
  10.7 5.3 %collective-permute-start.3 = (f32[16,128]{1,0:T(8,128)S(1)}, f32[16,128]{1,0:T(8,128)S(1)}, u32[]{:S(2)}, u32[]{:S(2)}) collective-permute-start(f32[16,128]{1,0:T(8,128)S(1)} %get-tuple-element.16), channel_id=1, source_target_pairs={{0,2},{1,3},{2,0},{3,1},{4,6},{5,7},{6,4},{7,5},{8,10},{9,11},{10,... | collective-permute-start | bytes 24584 | tf_op jit(solution)/shard_map/ppermute | solution.py:81
  10.7 5.2 %collective-permute-start.4 = (f32[16,128]{1,0:T(8,128)S(1)}, f32[16,128]{1,0:T(8,128)S(1)}, u32[]{:S(2)}, u32[]{:S(2)}) collective-permute-start(f32[16,128]{1,0:T(8,128)S(1)} %get-tuple-element.17), channel_id=1, source_target_pairs={{0,6},{1,7},{2,4},{3,5},{4,2},{5,3},{6,0},{7,1},{8,14},{9,15},{10,... | collective-permute-start | bytes 24584 | tf_op jit(solution)/shard_map/ppermute | solution.py:81
  12.4 3.6 %copy-start.3 = (f32[7,4,16,128]{3,2,1,0:T(8,128)S(1)}, f32[7,4,16,128]{3,2,1,0:T(8,128)}, u32[]{:S(2)}) copy-start(f32[7,4,16,128]{3,2,1,0:T(8,128)} %cot_heat.5) | copy-start | bytes 688132
  12.4 3.6 %collective-permute-start.5 = (f32[8,128]{1,0:T(8,128)S(1)}, f32[8,128]{1,0:T(8,128)S(1)}, u32[]{:S(2)}, u32[]{:S(2)}) collective-permute-start(f32[8,128]{1,0:T(8,128)S(1)} %get-tuple-element.18), channel_id=1, source_target_pairs={{0,1},{1,0},{2,3},{3,2},{4,5},{5,4},{6,7},{7,6},{8,9},{9,8},{10,11... | collective-permute-start | bytes 12296 | tf_op jit(solution)/shard_map/ppermute | solution.py:81

commit v2 on v1

v2 whole, which is shorter than its diff:
```python
import functools

import jax
import jax.numpy as jnp
from jax import lax
from jax.experimental import pallas as pl
from jax.experimental.pallas import tpu as pltpu
from jax.sharding import PartitionSpec as P

VELOCITY = (
    (0, 0, 0),
    (1, 0, 0),
    (-1, 0, 0),
    (0, 1, 0),
    (0, -1, 0),
    (0, 0, 1),
    (0, 0, -1),
    (1, 1, 0),
    (-1, -1, 0),
    (1, -1, 0),
    (-1, 1, 0),
    (1, 0, 1),
    (-1, 0, -1),
    (1, 0, -1),
    (-1, 0, 1),
    (0, 1, 1),
    (0, -1, -1),
    (0, 1, -1),
    (0, -1, 1),
)
OPPOSITE = tuple((VELOCITY.index((-a, -b, -c)) for a, b, c in VELOCITY))
WEIGHTS_FLOW = (1.0 / 3.0,) + (1.0 / 18.0,) * 6 + (1.0 / 36.0,) * 12
WEIGHTS_HEAT = (0.25,) + (0.125,) * 6
FLOW = 19
HEAT = 7
DIRECTIONS = VELOCITY + VELOCITY[:HEAT]
tau_flow = 0.8
tau_heat = 0.9
diffusion = 0.12
coupling = 0.3

AXES = ("gx", "gy", "gz")
COMPONENT = {"gx": 0, "gy": 1, "gz": 2}
VMEM_LIMIT = 8 << 20
VMEM_FIRST = 8 << 20


def moving(component, sign):
    return [k for k, c in enumerate(DIRECTIONS) if c[component] == sign]


XP, XM = moving(0, 1), moving(0, -1)
YP, YM = moving(1, 1), moving(1, -1)
ZP, ZM = moving(2, 1), moving(2, -1)
XZP = [k for k in ZP if DIRECTIONS[k][0] != 0]
XZM = [k for k in ZM if DIRECTIONS[k][0] != 0]


def rounds(size):
    return 1 if size == 2 else 2


def swap(value, axis, turn):
    sizes = [lax.axis_size(name) for name in AXES]
    at = AXES.index(axis)
    pairs = []
    for a in range(sizes[0]):
        for b in range(sizes[1]):
            for c in range(sizes[2]):
                here = [a, b, c]
                there = [a, b, c]
                i = here[at]
                j = i ^ 1 if turn == 0 else (i + 1 if i % 2 else i - 1)
                if 0 <= j < sizes[at]:
                    there[at] = j
                elif axis == "gy":
                    there[at] = sizes[at] - 1 - i
                else:
                    there[1] = b ^ 1
                flat = lambda p: (p[0] * sizes[1] + p[1]) * sizes[2] + p[2]
                pairs.append((flat(here), flat(there)))
    return lax.ppermute(value, AXES, pairs)


def place(axis):
    i = lax.axis_index(axis)
    return lax.rem(i, 2) == 0, i < lax.axis_size(axis) - 1, i > 0


def outgoing(axis, turn, to_higher, to_lower):
    even, _, _ = place(axis)
    return jnp.where(even, to_higher, to_lower) if turn == 0 else jnp.where(even, to_lower, to_higher)


def incoming(axis, turns):
    even, higher, lower = place(axis)
    first, last = turns[0], turns[-1]
    zero = jnp.zeros_like(first)
    above = jnp.where(higher, jnp.where(even, first, last), zero)
    below = jnp.where(lower, jnp.where(even, last, first), zero)
    return above, below


def slab(cot_flow, cot_heat, k, z):
    return cot_flow[k, z] if k < FLOW else cot_heat[k - FLOW, z]


def padded(rows):
    return -(-rows // 8) * 8


def pack_first(nxt, nzt, cot_flow, cot_heat, cot_plate, *refs):
    x_outs, z_outs = refs[:nxt], refs[nxt : nxt + nzt]
    to_higher, to_lower, x_sems, plate_sems, z_sems = refs[nxt + nzt :]
    depth, width = cot_flow.shape[1], cot_flow.shape[2]
    layers = cot_plate.shape[0]
    copies = []

    def start(source, target, sem):
        copies.append(pltpu.make_async_copy(source, target, sem))
        copies[-1].start()

    for side, (rows, ks, x) in enumerate(((to_higher, XM, width - 1), (to_lower, XP, 0))):
        for n, k in enumerate(ks):
            ref = cot_flow.at[k] if k < FLOW else cot_heat.at[k - FLOW]
            start(ref.at[:, x, :], rows.at[n * depth : (n + 1) * depth, :], x_sems.at[side, n])
        n = len(ks) * depth
        start(cot_plate.at[:, x, :], rows.at[n : n + layers, :], plate_sems.at[side])
    even, _, _ = place("gz")
    for turn in range(nzt):
        up = even if turn == 0 else jnp.logical_not(even)
        z = jnp.where(up, depth - 1, 0)
        for n, (hi, lo) in enumerate(zip(ZM, ZP)):
            ref, skip = (cot_flow, 0) if hi < FLOW else (cot_heat, FLOW)
            k = jnp.where(up, hi - skip, lo - skip)
            start(ref.at[k, z], z_outs[turn].at[n * width : (n + 1) * width, :], z_sems.at[turn, n])
    for copy in copies:
        copy.wait()
    for turn in range(nxt):
        x_outs[turn][...] = outgoing("gx", turn, to_higher[...], to_lower[...])


def halo_row(x_in, k, z, depth):
    up = DIRECTIONS[k][0] == 1
    at = (XP if up else XM).index(k) * depth + z
    above, below = incoming("gx", [r[at : at + 1, :] for r in x_in])
    return above if up else below


class Halo:
    def __init__(self, cot_flow, cot_heat, x_in, z_in, rest_in=None):
        self.flow, self.heat = cot_flow, cot_heat
        self.depth, self.width = cot_flow.shape[1], cot_flow.shape[2]
        self.x_in, self.z_in, self.rest_in = x_in, z_in, rest_in

    def face(self, k):
        up = DIRECTIONS[k][2] == 1
        at = (ZP if up else ZM).index(k) * self.width
        above, below = incoming("gz", [r[at : at + self.width, :] for r in self.z_in])
        return above if up else below

    def row(self, k, z):
        if 0 <= z < self.depth:
            return halo_row(self.x_in, k, z, self.depth)
        from_above = z >= self.depth
        at = self.width + (XZP if from_above else XZM).index(k)
        above, below = incoming("gz", [r[at : at + 1, :] for r in self.rest_in])
        return above if from_above else below

    def shifted(self, k, z):
        cx, _, cz = DIRECTIONS[k]
        at = z + cz
        plane = slab(self.flow, self.heat, k, at) if 0 <= at < self.depth else self.face(k)
        if cx == 0:
            return plane
        return shift_rows(plane, cx, self.row(k, at))


def shift_rows(plane, sign, halo_row):
    width = plane.shape[0]
    x = lax.broadcasted_iota(jnp.int32, plane.shape, 0)
    if sign == 1:
        return jnp.where(x == width - 1, halo_row, pltpu.roll(plane, width - 1, 0))
    return jnp.where(x == 0, halo_row, pltpu.roll(plane, 1, 0))


def shift_lanes(plane, sign):
    length = plane.shape[1]
    y = lax.broadcasted_iota(jnp.int32, plane.shape, 1)
    if sign == 1:
        return jnp.where(y == length - 1, 0.0, pltpu.roll(plane, length - 1, 1))
    return jnp.where(y == 0, 0.0, pltpu.roll(plane, 1, 1))


def column_lane(n, z, depth):
    return 2 * (n * depth + z)


def plate_lane(l, depth):
    return column_lane(len(YM), 0, depth) + l


def turned(plane, by):
    by %= plane.shape[1]
    return pltpu.roll(plane, by, 1) if by else plane


def pack_rest(nxt, nzt, depth, cot_plate, *refs):
    x_in, outs = refs[:nxt], refs[-nzt:]
    layers, width = cot_plate.shape[:2]
    for turn in range(nzt):
        out = outs[turn]
        out[:width, :] = outgoing("gz", turn, cot_plate[layers - 1], cot_plate[0])
        out[width:, :] = jnp.zeros((out.shape[0] - width, out.shape[1]), jnp.float32)
        for n, (hi, lo) in enumerate(zip(XZM, XZP)):
            out[width + n : width + n + 1, :] = outgoing(
                "gz", turn, halo_row(x_in, hi, depth - 1, depth), halo_row(x_in, lo, 0, depth)
            )


def pack_columns(nxt, nyt, nzt, cot_flow, cot_heat, cot_plate, *refs):
    x_in, z_in = refs[:nxt], refs[nxt : nxt + nzt]
    outs = refs[-nyt:]
    halo = Halo(cot_flow, cot_heat, x_in, z_in)
    depth, width = halo.depth, halo.width
    length = cot_flow.shape[3]
    layers = cot_plate.shape[0]
    y = lax.broadcasted_iota(jnp.int32, (width, length), 1)

    def put(packed, plane, source, lane):
        return jnp.where(y == lane, turned(plane, lane - source), packed)

    packs = []
    for side, source in ((YM, length - 1), (YP, 0)):
        packed = jnp.zeros((width, length), jnp.float32)
        for n, k in enumerate(side):
            for z in range(depth):
                packed = put(packed, halo.shifted(k, z), source, column_lane(n, z, depth))
        for l in range(layers):
            packed = put(packed, cot_plate[l], source, plate_lane(l, depth))
        packs.append(packed)
    for turn in range(nyt):
        outs[turn][...] = outgoing("gy", turn, packs[0], packs[1])


def prepare(pop_flow, pop_heat, flags, nozzle, jet_velocity, *refs):
    ue_out, ratio_out, ends_out, kinds_out = refs[-4:]
    jets = [jnp.zeros(nozzle.shape, jnp.float32)] * 3
    which = nozzle[...]
    for n in range(jet_velocity.shape[1]):
        hit = which == n
        jets = [jnp.where(hit, jet_velocity[c, n], jets[c]) for c in range(3)]
    y = lax.broadcasted_iota(jnp.int32, nozzle.shape, 1)
    ends = [None] * 4
    kinds = None
    for z in range(pop_flow.shape[1]):
        kind = flags[z]
        inlet = kind == 2
        pops = [pop_flow[q, z] for q in range(FLOW)]
        rho = sum(pops[1:], pops[0])
        inverse = 1.0 / rho
        values = []
        for c in range(3):
            plus = [pops[q] for q in range(FLOW) if VELOCITY[q][c] == 1]
            minus = [pops[q] for q in range(FLOW) if VELOCITY[q][c] == -1]
            total = sum(plus[1:], plus[0]) - sum(minus[1:], minus[0])
            values.append(jnp.where(inlet, jets[c], total * inverse))
            ue_out[c, z] = values[c]
        heat = [pop_heat[q, z] for q in range(HEAT)]
        values.append(sum(heat[1:], heat[0]) * inverse)
        ratio_out[z] = values[3]
        if z == 0:
            ends, kinds = values, kind
        else:
            here = end_lanes(y, z)
            ends = [jnp.where(here, turned(v, 2 * z), e) for v, e in zip(values, ends)]
            kinds = jnp.where(here, turned(kind, 2 * z), kinds)
    for c in range(4):
        ends_out[c] = ends[c]
    kinds_out[...] = kinds


def end_lanes(y, z):
    return (y == 2 * z) | (y == (2 * z - 1) % y.shape[1])


def collide_back(s, t, ue, ratio, wall, inlet):
    add = lambda a, b: b if a is None else a + b
    zero_moment = WEIGHTS_FLOW[0] * s[0]
    first = [None] * 3
    second = {}
    for group, weight in ((range(1, 7), WEIGHTS_FLOW[1]), (range(7, 19), WEIGHTS_FLOW[7])):
        odd = [None] * 3
        even = {}
        total = None
        for q in group:
            o = OPPOSITE[q]
            if o < q:
                continue
            c = VELOCITY[q]
            plus, minus = s[q] + s[o], s[q] - s[o]
            total = add(total, plus)
            for i in range(3):
                if c[i]:
                    odd[i] = add(odd[i], minus if c[i] == 1 else -minus)
                for j in range(i, 3):
                    if c[i] * c[j]:
                        even[i, j] = add(even.get((i, j)), plus if c[i] * c[j] == 1 else -plus)
        zero_moment = zero_moment + weight * total
        for i in range(3):
            first[i] = add(first[i], weight * odd[i])
        for key, value in even.items():
            second[key] = add(second.get(key), weight * value)
    heat_first = [WEIGHTS_HEAT[1] * (t[2 * c + 1] - t[2 * c + 2]) for c in range(3)]
    heat_zero = WEIGHTS_HEAT[0] * t[0] + WEIGHTS_HEAT[1] * (
        (t[1] + t[2]) + (t[3] + t[4]) + (t[5] + t[6])
    )
    dot = lambda a, b: a[0] * b[0] + a[1] * b[1] + a[2] * b[2]
    bent = [sum(second[min(i, j), max(i, j)] * ue[j] for j in range(3)) for i in range(3)]
    gain = zero_moment * (1.0 - 1.5 * dot(ue, ue)) + 3.0 * dot(first, ue) + 4.5 * dot(bent, ue)
    pull = [
        (3.0 / tau_flow) * (first[i] + 3.0 * bent[i] - ue[i] * zero_moment)
        + (4.0 / tau_heat) * ratio * heat_first[i]
        for i in range(3)
    ]
    common = jnp.where(inlet, gain, (1.0 / tau_flow) * gain - dot(ue, pull))
    pull = [jnp.where(inlet, 0.0, p) for p in pull]
    keep = jnp.where(inlet, 0.0, 1.0 - 1.0 / tau_flow)
    flow = []
    for q in range(FLOW):
        value = keep * s[q] + common
        for i in range(3):
            if VELOCITY[q][i] == 1:
                value = value + pull[i]
            elif VELOCITY[q][i] == -1:
                value = value - pull[i]
        flow.append(jnp.where(wall, s[OPPOSITE[q]], value))
    heat_common = jnp.where(inlet, 0.0, (1.0 / tau_heat) * (heat_zero + 4.0 * dot(heat_first, ue)))
    heat_keep = jnp.where(inlet, 0.0, 1.0 - 1.0 / tau_heat)
    heat = [
        jnp.where(wall, t[OPPOSITE[q]], heat_keep * t[q] + heat_common) for q in range(HEAT)
    ]
    return flow, heat


def interior(nxt, nzt, flags, ue_in, ratio_in, cot_flow, cot_heat, cot_plate, *refs):
    x_in, z_in = refs[:nxt], refs[nxt : nxt + nzt]
    rest_in = refs[nxt + nzt : nxt + 2 * nzt]
    grad_flow, grad_heat, grad_plate = refs[-3:]
    halo = Halo(cot_flow, cot_heat, x_in, z_in, rest_in)
    depth, width = halo.depth, halo.width
    layers = cot_plate.shape[0]
    base = lax.axis_index("gz") == 0

    for z in range(depth):
        star = []
        for k, (_, cy, cz) in enumerate(DIRECTIONS):
            plane = halo.shifted(k, z)
            if cy:
                plane = shift_lanes(plane, cy)
            if cz == -1 and z == 0:
                if k < FLOW:
                    bounced = cot_flow[OPPOSITE[k], 0]
                else:
                    bounced = -cot_heat[OPPOSITE[k - FLOW], 0]
                plane = jnp.where(base, bounced, plane)
            star.append(plane)
        kind = flags[z]
        flow, heat = collide_back(
            star[:FLOW], star[FLOW:], [ue_in[c, z] for c in range(3)], ratio_in[z], kind == 1, kind == 2
        )
        for q in range(FLOW):
            grad_flow[q, z] = flow[q]
        for q in range(HEAT):
            value = heat[q]
            if z == 0:
                value = value + jnp.where(base, coupling * cot_plate[0], 0.0)
            grad_heat[q, z] = value

    x_above, x_below = incoming("gx", [r[...] for r in x_in])
    z_above, z_below = incoming("gz", [r[:width, :] for r in rest_in])
    for l in range(layers):
        own = cot_plate[l]
        up = cot_plate[l + 1] if l + 1 < layers else z_above
        down = cot_plate[l - 1] if l > 0 else z_below
        r = len(XP) * depth + l
        total = up + down
        total = total + shift_rows(own, 1, x_above[r : r + 1, :])
        total = total + shift_rows(own, -1, x_below[r : r + 1, :])
        total = total + shift_lanes(own, 1) + shift_lanes(own, -1)
        value = own + diffusion * (total - 6.0 * own)
        if l == 0:
            value = value + jnp.where(base, 0.25 * cot_heat[5, 0] - coupling * own, 0.0)
        grad_plate[l] = value


def finish(nyt, depth, ends, kinds, main_flow, main_heat, main_plate, *refs):
    y_in = refs[:nyt]
    out_flow, out_heat, out_plate, flow_buf, heat_buf, plate_buf, sems = refs[nyt:]
    above, below = incoming("gy", [r[...] for r in y_in])
    layers = main_plate.shape[0]
    length = above.shape[1]
    y = lax.broadcasted_iota(jnp.int32, above.shape, 1)
    zero = jnp.zeros_like(above)
    from_below, from_above = y == 0, y == length - 1
    for z in range(1, depth):
        from_below = from_below | (y == 2 * z)
        from_above = from_above | (y == 2 * z - 1)
    star = []
    for k, c in enumerate(DIRECTIONS):
        if c[1] == -1:
            lane = column_lane(YM.index(k), 0, depth)
            star.append(jnp.where(from_below, turned(below, -lane), zero))
        elif c[1] == 1:
            lane = column_lane(YP.index(k), 0, depth)
            star.append(jnp.where(from_above, turned(above, -lane - 1), zero))
        else:
            star.append(zero)
    kind = kinds[...]
    flow, heat = collide_back(
        star[:FLOW], star[FLOW:], [ends[c] for c in range(3)], ends[3], kind == 1, kind == 2
    )
    edge = (y == 0) | (y == length - 1)
    copies = []
    for values, main, buf, out, first in (
        (flow, main_flow, flow_buf, out_flow, 0),
        (heat, main_heat, heat_buf, out_heat, FLOW),
    ):
        for q, value in enumerate(values):
            for z in range(depth):
                buf[q, z] = main[q, z] + jnp.where(edge, turned(value, -2 * z), 0.0)
            copies.append(pltpu.make_async_copy(buf.at[q], out.at[q], sems.at[first + q]))
            copies[-1].start()
    for l in range(layers):
        lane = plate_lane(l, depth)
        beside = jnp.where(
            y == 0, turned(below, -lane), jnp.where(from_above, turned(above, length - 1 - lane), 0.0)
        )
        beside = jnp.where(edge, beside, 0.0)
        plate_buf[l] = main_plate[l] + diffusion * beside
    copies.append(pltpu.make_async_copy(plate_buf, out_plate, sems.at[FLOW + HEAT]))
    copies[-1].start()
    for copy in copies:
        copy.wait()


def kernel_call(body, outs, count, name, cost=0, smem=(), scratch=(), **params):
    return pl.pallas_call(
        body,
        out_shape=outs,
        in_specs=[
            pl.BlockSpec(memory_space=pltpu.SMEM if i in smem else pltpu.VMEM) for i in range(count)
        ],
        out_specs=[pl.BlockSpec(memory_space=pltpu.VMEM)] * len(outs),
        scratch_shapes=scratch,
        compiler_params=pltpu.CompilerParams(vmem_limit_bytes=VMEM_LIMIT),
        cost_estimate=pl.CostEstimate(flops=0, bytes_accessed=cost, transcendentals=0),
        name=name,
    )


def local(pop_flow, pop_heat, flags, nozzle_id, jet_velocity, cot_flow, cot_heat, cot_plate):
    nxt, nyt, nzt = (rounds(lax.axis_size(a)) for a in AXES)
    _, depth, width, length = cot_flow.shape
    layers = cot_plate.shape[0]
    f32 = jnp.float32
    array = lambda *shape: jax.ShapeDtypeStruct(shape, f32)
    cots = (cot_flow, cot_heat, cot_plate)
    side = padded(len(XM) * depth + layers)

    first = pl.pallas_call(
        functools.partial(pack_first, nxt, nzt),
        out_shape=[pltpu.VMEM((side, length), f32)] * nxt
        + [pltpu.VMEM((len(ZM) * width, length), f32)] * nzt,
        in_specs=[pl.BlockSpec(memory_space=pltpu.HBM)] * 3,
        out_specs=[pl.BlockSpec(memory_space=pltpu.VMEM)] * (nxt + nzt),
        scratch_shapes=[
            pltpu.VMEM((side, length), f32),
            pltpu.VMEM((side, length), f32),
            pltpu.SemaphoreType.DMA((2, len(XM))),
            pltpu.SemaphoreType.DMA((2,)),
            pltpu.SemaphoreType.DMA((nzt, len(ZM))),
        ],
        compiler_params=pltpu.CompilerParams(vmem_limit_bytes=VMEM_FIRST),
        cost_estimate=pl.CostEstimate(flops=0, bytes_accessed=2 << 20, transcendentals=0),
        name="first",
    )(*(pltpu.with_memory_space_constraint(c, pltpu.HBM) for c in cots))
    x_in = [swap(v, "gx", t) for t, v in enumerate(first[:nxt])]
    z_in = [swap(v, "gz", t) for t, v in enumerate(first[nxt:])]
    ue, ratio, end_values, end_kinds = kernel_call(
        prepare,
        [
            array(3, depth, width, length),
            array(depth, width, length),
            array(4, width, length),
            jax.ShapeDtypeStruct((width, length), jnp.int32),
        ],
        5 + nzt,
        "prepare",
        cost=2 << 20,
        smem=(4,),
    )(pop_flow, pop_heat, flags, nozzle_id, jet_velocity, *first[nxt:])
    rest = kernel_call(
        functools.partial(pack_rest, nxt, nzt, depth),
        [array(width + padded(len(XZM)), length)] * nzt,
        1 + nxt + 1,
        "rest",
        cost=1 << 17,
    )(cot_plate, *x_in, ratio)
    rest_in = [swap(v, "gz", t) for t, v in enumerate(rest)]
    columns = kernel_call(
        functools.partial(pack_columns, nxt, nyt, nzt),
        [array(width, length)] * nyt,
        3 + nxt + 2 * nzt,
        "columns",
        cost=1 << 18,
    )(*cots, *x_in, *z_in, *rest)
    y_in = [swap(v, "gy", t) for t, v in enumerate(columns)]
    main = kernel_call(
        functools.partial(interior, nxt, nzt),
        [array(*c.shape) for c in cots],
        6 + nxt + 2 * nzt + nyt,
        "interior",
        cost=2 << 20,
    )(flags, ue, ratio, *cots, *x_in, *z_in, *rest_in, *columns)
    return tuple(
        pl.pallas_call(
            functools.partial(finish, nyt, depth),
            out_shape=[array(*c.shape) for c in cots],
            in_specs=[pl.BlockSpec(memory_space=pltpu.VMEM)] * (5 + nyt),
            out_specs=[pl.BlockSpec(memory_space=pltpu.HBM)] * 3,
            scratch_shapes=[pltpu.VMEM(c.shape, f32) for c in cots]
            + [pltpu.SemaphoreType.DMA((FLOW + HEAT + 1,))],
            compiler_params=pltpu.CompilerParams(vmem_limit_bytes=VMEM_LIMIT),
            name="finish",
        )(end_values, end_kinds, *main, *y_in)
    )


def solution(mesh):
    return jax.shard_map(
        local,
        mesh=mesh,
        in_specs=(
            P(None, "gz", "gx", "gy"),
            P(None, "gz", "gx", "gy"),
            P("gz", "gx", "gy"),
            P("gx", "gy"),
            P(),
            P(None, "gz", "gx", "gy"),
            P(None, "gz", "gx", "gy"),
            P("gz", "gx", "gy"),
        ),
        out_specs=(P(None, "gz", "gx", "gy"), P(None, "gz", "gx", "gy"), P("gz", "gx", "gy")),
        check_vma=False,
    )
```

time: 17.8 us -> 15 us (0.84)
  the two profiles are of different devices: /device:TPU:0 before, /device:TPU:17 now
where the time goes in v2:
time: 15 us; the launch traced here: 14.7 us
  starting transfers between devices  6.51 us (43%)
  Pallas kernels  4.03 us (27%)
  waiting for transfers between devices  3.42 us (23%)
  between operations  0.75 us (5%)
    ppermute x6, starting transfers between devices, swap(): return lax.ppermute(value, AXES, pairs)  6.51 us
    ppermute x6, waiting for transfers between devices, swap(): return lax.ppermute(value, AXES, pairs)  3.42 us
    pallas_call x1, Pallas kernels, local(): pl.pallas_call(functools.partial(finish, nyt, depth), out_shape=[array(*c...  1.35 us
    pallas_call x1, Pallas kernels, local(): pl.pallas_call(functools.partial(pack_first, nxt, nzt), out_shape=[pltpu....  1.1 us
    pallas_call x1, Pallas kernels, local(): kernel_call(prepare, [array(3, depth, width, length), array(depth, width,...  0.85 us
    pallas_call x1, Pallas kernels, local(): kernel_call(functools.partial(interior, nxt, nzt), [array(*c.shape) for c...  0.51 us
  transfers between devices with their start and end apart: 6, of which 3 were waited for; matrix products, arithmetic and copies ran while one was open for 0% of the time, Pallas kernels for 11%

profile of v2, /device:TPU:17, one launch (start us, length us, event | category | flops | bytes accessed | tf_op | source)
XLA Modules:
  0.0 14.7 jit_solution(5266891268906621608)
XLA Ops:
  0.6 0.0 copy-start.5
  0.6 0.0 copy-start.4
  0.7 0.0 copy-start.3
  0.7 0.0 copy-start.6
  0.7 1.1 %first.1 = (f32[40,128]{1,0:T(8,128)S(1)}, f32[40,128]{1,0:T(8,128)S(1)}, f32[96,128]{1,0:T(8,128)S(1)}) custom-call(f32[19,4,16,128]{3,2,1,0:T(8,128)} %cot_flow.5, f32[7,4,16,128]{3,2,1,0:T(8,128)} %cot_heat.5, f32[10,16,128]{2,1,0:T(8,128)} %cot_plate.7), custom_call_target="tpu_custom_call" | custom-call | bytes 2097152 | tf_op jit(solution)/shard_map/first/pallas_call | solution.py:471
  1.8 0.0 copy-start
  1.8 1.3 %collective-permute-start.2 = (f32[96,128]{1,0:T(8,128)S(1)}, f32[96,128]{1,0:T(8,128)S(1)}, u32[]{:S(2)}, u32[]{:S(2)}) collective-permute-start(f32[96,128]{1,0:T(8,128)S(1)} %get-tuple-element.15.refs_0_), channel_id=1, source_target_pairs={{0,1},{1,0},{2,3},{3,2},{4,5},{5,4},{6,7},{7,6},{8,9},{9,8},{10,11... | collective-permute-start | bytes 147464 | tf_op jit(solution)/shard_map/ppermute | solution.py:82
  3.1 1.3 %collective-permute-start = (f32[40,128]{1,0:T(8,128)S(1)}, f32[40,128]{1,0:T(8,128)S(1)}, u32[]{:S(2)}, u32[]{:S(2)}) collective-permute-start(f32[40,128]{1,0:T(8,128)S(1)} %get-tuple-element.20), channel_id=1, source_target_pairs={{0,8},{1,9},{2,10},{3,11},{4,12},{5,13},{6,14},{7,15},{8,0},{9,1},... | collective-permute-start | bytes 61448 | tf_op jit(solution)/shard_map/ppermute | solution.py:82
  4.4 0.0 collective-permute-start.1
  4.4 0.0 copy-start.1
  4.5 0.8 %prepare.1 = (f32[3,4,16,128]{3,2,1,0:T(8,128)S(1)}, f32[4,16,128]{2,1,0:T(8,128)S(1)}, f32[4,16,128]{2,1,0:T(8,128)S(1)}, s32[16,128]{1,0:T(8,128)S(1)}) custom-call(f32[19,4,16,128]{3,2,1,0:T(8,128)S(1)} %copy-done.3, f32[7,4,16,128]{3,2,1,0:T(8,128)S(1)} %copy-done.4, s32[4,16,128]{2,1,0:T(8,128)S(1)} %copy-done.5, s32[16,128]{1,0:T(8,128)S(1)} %copy-done.6, ...), custom_call_target="tpu_custom_call" | custom-call | bytes 2097152 | tf_op jit(solution)/shard_map/prepare/pallas_call | solution.py:490
  5.3 0.7 %collective-permute-done.refs_0_ = f32[40,128]{1,0:T(8,128)S(1)} collective-permute-done((f32[40,128]{1,0:T(8,128)S(1)}, f32[40,128]{1,0:T(8,128)S(1)}, u32[]{:S(2)}, u32[]{:S(2)}) %collective-permute-start) | collective-permute-done | bytes 20512 | tf_op jit(solution)/shard_map/ppermute | solution.py:82
  6.0 1.3 %collective-permute-done.1.refs_1_ = f32[40,128]{1,0:T(8,128)S(1)} collective-permute-done((f32[40,128]{1,0:T(8,128)S(1)}, f32[40,128]{1,0:T(8,128)S(1)}, u32[]{:S(2)}, u32[]{:S(2)}) %collective-permute-start.1) | collective-permute-done | bytes 20512 | tf_op jit(solution)/shard_map/ppermute | solution.py:82
  7.4 0.3 %collective-permute-start.3 = (f32[24,128]{1,0:T(8,128)S(1)}, f32[24,128]{1,0:T(8,128)S(1)}, u32[]{:S(2)}, u32[]{:S(2)}) collective-permute-start(f32[24,128]{1,0:T(8,128)S(1)} %rest.1.refs_3_), channel_id=1, source_target_pairs={{0,1},{1,0},{2,3},{3,2},{4,5},{5,4},{6,7},{7,6},{8,9},{9,8},{10,11... | collective-permute-start | bytes 36872 | tf_op jit(solution)/shard_map/ppermute | solution.py:82
  7.6 0.0 collective-permute-done.2.refs_2_
  7.6 0.0 copy-done.1
  7.7 0.2 %columns.1 = (f32[16,128]{1,0:T(8,128)S(1)}, f32[16,128]{1,0:T(8,128)S(1)}) custom-call(f32[19,4,16,128]{3,2,1,0:T(8,128)S(1)} %copy-done, f32[7,4,16,128]{3,2,1,0:T(8,128)S(1)} %copy-done.1, f32[10,16,128]{2,1,0:T(8,128)S(1)} %copy-done.2, f32[40,128]{1,0:T(8,128)S(1)} %collective-permute-done.refs_0_, f32[40,128]{1,0:T(8,128)S(1)} %collective-permute-done.1.refs_1_, ...), custom_call_target="tpu_custom_call" | custom-call | bytes 262144 | tf_op jit(solution)/shard_map/columns/pallas_call | solution.py:511
  7.9 2.4 %collective-permute-start.4 = (f32[16,128]{1,0:T(8,128)S(1)}, f32[16,128]{1,0:T(8,128)S(1)}, u32[]{:S(2)}, u32[]{:S(2)}) collective-permute-start(f32[16,128]{1,0:T(8,128)S(1)} %get-tuple-element.22.refs_4_), channel_id=1, source_target_pairs={{0,2},{1,3},{2,0},{3,1},{4,6},{5,7},{6,4},{7,5},{8,10},{9,11},{10,... | collective-permute-start | bytes 24584 | tf_op jit(solution)/shard_map/ppermute | solution.py:82
  10.3 1.2 %collective-permute-start.5 = (f32[16,128]{1,0:T(8,128)S(1)}, f32[16,128]{1,0:T(8,128)S(1)}, u32[]{:S(2)}, u32[]{:S(2)}) collective-permute-start(f32[16,128]{1,0:T(8,128)S(1)} %get-tuple-element.23.refs_5_), channel_id=1, source_target_pairs={{0,6},{1,7},{2,4},{3,5},{4,2},{5,3},{6,0},{7,1},{8,14},{9,15},{10,... | collective-permute-start | bytes 24584 | tf_op jit(solution)/shard_map/ppermute | solution.py:82
  11.5 0.0 collective-permute-done.3.refs_3_
  11.5 0.5 %interior.1 = (f32[19,4,16,128]{3,2,1,0:T(8,128)S(1)}, f32[7,4,16,128]{3,2,1,0:T(8,128)S(1)}, f32[10,16,128]{2,1,0:T(8,128)S(1)}) custom-call(s32[4,16,128]{2,1,0:T(8,128)S(1)} %copy-done.5, f32[3,4,16,128]{3,2,1,0:T(8,128)S(1)} %get-tuple-element.18.ue_in, f32[4,16,128]{2,1,0:T(8,128)S(1)} %get-tuple-element.19.refs_2_.ratio_in, ...), custom_call_target="tpu_custom_call" | custom-call | bytes 2097152 | tf_op jit(solution)/shard_map/interior/pallas_call | solution.py:519
  12.0 0.0 collective-permute-done.4.refs_0_
  12.0 1.4 %collective-permute-done.5.refs_1_ = f32[16,128]{1,0:T(8,128)S(1)} collective-permute-done((f32[16,128]{1,0:T(8,128)S(1)}, f32[16,128]{1,0:T(8,128)S(1)}, u32[]{:S(2)}, u32[]{:S(2)}) %collective-permute-start.5) | collective-permute-done | bytes 8224 | tf_op jit(solution)/shard_map/ppermute | solution.py:82
  13.4 1.3 %finish.1 = (f32[19,4,16,128]{3,2,1,0:T(8,128)}, f32[7,4,16,128]{3,2,1,0:T(8,128)}, f32[10,16,128]{2,1,0:T(8,128)}) custom-call(f32[4,16,128]{2,1,0:T(8,128)S(1)} %get-tuple-element.16.ends, s32[16,128]{1,0:T(8,128)S(1)} %get-tuple-element.17.kinds, f32[19,4,16,128]{3,2,1,0:T(8,128)S(1)} %get-tuple-element.24.main_flow, ...), custom_call_target="tpu_custom_call" | custom-call | tf_op jit(solution)/shard_map/finish/pallas_call | solution.py:527
  (10 shorter events, 0.0 us)
Async XLA Ops:
  0.6 3.8 %copy-start.5 = (s32[4,16,128]{2,1,0:T(8,128)S(1)}, s32[4,16,128]{2,1,0:T(8,128)}, u32[]{:S(2)}) copy-start(s32[4,16,128]{2,1,0:T(8,128)} %flags.3) | copy-start | bytes 98308
  0.6 3.8 %copy-start.4 = (f32[7,4,16,128]{3,2,1,0:T(8,128)S(1)}, f32[7,4,16,128]{3,2,1,0:T(8,128)}, u32[]{:S(2)}) copy-start(f32[7,4,16,128]{3,2,1,0:T(8,128)} %pop_heat.1) | copy-start | bytes 688132
  0.7 3.8 %copy-start.3 = (f32[19,4,16,128]{3,2,1,0:T(8,128)S(1)}, f32[19,4,16,128]{3,2,1,0:T(8,128)}, u32[]{:S(2)}) copy-start(f32[19,4,16,128]{3,2,1,0:T(8,128)} %pop_flow.1) | copy-start | bytes 1867780
  0.7 3.8 %copy-start.6 = (s32[16,128]{1,0:T(8,128)S(1)}, s32[16,128]{1,0:T(8,128)}, u32[]{:S(2)}) copy-start(s32[16,128]{1,0:T(8,128)} %nozzle.1) | copy-start | bytes 24580
  0.7 3.8 %copy-start.7 = (f32[3,64]{1,0:T(4,128)S(1)}, f32[3,64]{1,0:T(4,128)}, u32[]{:S(2)}) copy-start(f32[3,64]{1,0:T(4,128)} %jet_velocity.1) | copy-start | bytes 2308
  1.8 5.9 %copy-start = (f32[19,4,16,128]{3,2,1,0:T(8,128)S(1)}, f32[19,4,16,128]{3,2,1,0:T(8,128)}, u32[]{:S(2)}) copy-start(f32[19,4,16,128]{3,2,1,0:T(8,128)} %cot_flow.5) | copy-start | bytes 1867780
  1.8 5.8 %collective-permute-start.2 = (f32[96,128]{1,0:T(8,128)S(1)}, f32[96,128]{1,0:T(8,128)S(1)}, u32[]{:S(2)}, u32[]{:S(2)}) collective-permute-start(f32[96,128]{1,0:T(8,128)S(1)} %get-tuple-element.15.refs_0_), channel_id=1, source_target_pairs={{0,1},{1,0},{2,3},{3,2},{4,5},{5,4},{6,7},{7,6},{8,9},{9,8},{10,11... | collective-permute-start | bytes 147464 | tf_op jit(solution)/shard_map/ppermute | solution.py:82
  3.1 2.9 %collective-permute-start = (f32[40,128]{1,0:T(8,128)S(1)}, f32[40,128]{1,0:T(8,128)S(1)}, u32[]{:S(2)}, u32[]{:S(2)}) collective-permute-start(f32[40,128]{1,0:T(8,128)S(1)} %get-tuple-element.20), channel_id=1, source_target_pairs={{0,8},{1,9},{2,10},{3,11},{4,12},{5,13},{6,14},{7,15},{8,0},{9,1},... | collective-permute-start | bytes 61448 | tf_op jit(solution)/shard_map/ppermute | solution.py:82
  4.4 2.9 %copy-start.2 = (f32[10,16,128]{2,1,0:T(8,128)S(1)}, f32[10,16,128]{2,1,0:T(8,128)}, u32[]{:S(2)}) copy-start(f32[10,16,128]{2,1,0:T(8,128)} %cot_plate.7) | copy-start | bytes 245764
  4.4 2.9 %collective-permute-start.1 = (f32[40,128]{1,0:T(8,128)S(1)}, f32[40,128]{1,0:T(8,128)S(1)}, u32[]{:S(2)}, u32[]{:S(2)}) collective-permute-start(f32[40,128]{1,0:T(8,128)S(1)} %get-tuple-element.21), channel_id=1, source_target_pairs={{0,2},{1,3},{2,0},{3,1},{4,6},{5,7},{6,4},{7,5},{8,16},{9,17},{10,... | collective-permute-start | bytes 61448 | tf_op jit(solution)/shard_map/ppermute | solution.py:82
  4.4 3.2 %copy-start.1 = (f32[7,4,16,128]{3,2,1,0:T(8,128)S(1)}, f32[7,4,16,128]{3,2,1,0:T(8,128)}, u32[]{:S(2)}) copy-start(f32[7,4,16,128]{3,2,1,0:T(8,128)} %cot_heat.5) | copy-start | bytes 688132
  7.4 4.1 %collective-permute-start.3 = (f32[24,128]{1,0:T(8,128)S(1)}, f32[24,128]{1,0:T(8,128)S(1)}, u32[]{:S(2)}, u32[]{:S(2)}) collective-permute-start(f32[24,128]{1,0:T(8,128)S(1)} %rest.1.refs_3_), channel_id=1, source_target_pairs={{0,1},{1,0},{2,3},{3,2},{4,5},{5,4},{6,7},{7,6},{8,9},{9,8},{10,11... | collective-permute-start | bytes 36872 | tf_op jit(solution)/shard_map/ppermute | solution.py:82
  7.9 4.1 %collective-permute-start.4 = (f32[16,128]{1,0:T(8,128)S(1)}, f32[16,128]{1,0:T(8,128)S(1)}, u32[]{:S(2)}, u32[]{:S(2)}) collective-permute-start(f32[16,128]{1,0:T(8,128)S(1)} %get-tuple-element.22.refs_4_), channel_id=1, source_target_pairs={{0,2},{1,3},{2,0},{3,1},{4,6},{5,7},{6,4},{7,5},{8,10},{9,11},{10,... | collective-permute-start | bytes 24584 | tf_op jit(solution)/shard_map/ppermute | solution.py:82
  10.3 3.1 %collective-permute-start.5 = (f32[16,128]{1,0:T(8,128)S(1)}, f32[16,128]{1,0:T(8,128)S(1)}, u32[]{:S(2)}, u32[]{:S(2)}) collective-permute-start(f32[16,128]{1,0:T(8,128)S(1)} %get-tuple-element.23.refs_5_), channel_id=1, source_target_pairs={{0,6},{1,7},{2,4},{3,5},{4,2},{5,3},{6,0},{7,1},{8,14},{9,15},{10,... | collective-permute-start | bytes 24584 | tf_op jit(solution)/shard_map/ppermute | solution.py:82

commit v3 on v2

v3 whole, which is shorter than its diff:
```python
import functools

import jax
import jax.numpy as jnp
from jax import lax
from jax.experimental import pallas as pl
from jax.experimental.pallas import tpu as pltpu
from jax.sharding import PartitionSpec as P

VELOCITY = (
    (0, 0, 0),
    (1, 0, 0),
    (-1, 0, 0),
    (0, 1, 0),
    (0, -1, 0),
    (0, 0, 1),
    (0, 0, -1),
    (1, 1, 0),
    (-1, -1, 0),
    (1, -1, 0),
    (-1, 1, 0),
    (1, 0, 1),
    (-1, 0, -1),
    (1, 0, -1),
    (-1, 0, 1),
    (0, 1, 1),
    (0, -1, -1),
    (0, 1, -1),
    (0, -1, 1),
)
OPPOSITE = tuple((VELOCITY.index((-a, -b, -c)) for a, b, c in VELOCITY))
WEIGHTS_FLOW = (1.0 / 3.0,) + (1.0 / 18.0,) * 6 + (1.0 / 36.0,) * 12
WEIGHTS_HEAT = (0.25,) + (0.125,) * 6
FLOW = 19
HEAT = 7
DIRECTIONS = VELOCITY + VELOCITY[:HEAT]
tau_flow = 0.8
tau_heat = 0.9
diffusion = 0.12
coupling = 0.3

AXES = ("gx", "gy", "gz")
COMPONENT = {"gx": 0, "gy": 1, "gz": 2}
VMEM_LIMIT = 8 << 20
EDGE_ROWS = 48


def moving(component, sign):
    return [k for k, c in enumerate(DIRECTIONS) if c[component] == sign]


XP, XM = moving(0, 1), moving(0, -1)
YP, YM = moving(1, 1), moving(1, -1)
ZP, ZM = moving(2, 1), moving(2, -1)


def rounds(size):
    return 1 if size == 2 else 2


def swap(value, **turns):
    sizes = [lax.axis_size(name) for name in AXES]
    flat = lambda p: (p[0] * sizes[1] + p[1]) * sizes[2] + p[2]
    pairs = []
    for a in range(sizes[0]):
        for b in range(sizes[1]):
            for c in range(sizes[2]):
                here = [a, b, c]
                there = [a, b, c]
                for axis, turn in turns.items():
                    at = AXES.index(axis)
                    i = here[at]
                    there[at] = i ^ 1 if turn == 0 else (i + 1 if i % 2 else i - 1)
                if not all(0 <= t < n for t, n in zip(there, sizes)):
                    there = [a, sizes[1] - 1 - b if "gy" in turns else b ^ 1, c]
                pairs.append((flat(here), flat(there)))
    return lax.ppermute(value, AXES, pairs)


def place(axis):
    i = lax.axis_index(axis)
    return lax.rem(i, 2) == 0, i < lax.axis_size(axis) - 1, i > 0


def outgoing(axis, turn, to_higher, to_lower):
    even, _, _ = place(axis)
    return jnp.where(even, to_higher, to_lower) if turn == 0 else jnp.where(even, to_lower, to_higher)


def incoming(axis, turns):
    even, higher, lower = place(axis)
    first, last = turns[0], turns[-1]
    zero = jnp.zeros_like(first)
    above = jnp.where(higher, jnp.where(even, first, last), zero)
    below = jnp.where(lower, jnp.where(even, last, first), zero)
    return above, below


def slab(cot_flow, cot_heat, k, z):
    return cot_flow[k, z] if k < FLOW else cot_heat[k - FLOW, z]


def row_of(cot_flow, cot_heat, k, z, x):
    return cot_flow[k, z, x : x + 1, :] if k < FLOW else cot_heat[k - FLOW, z, x : x + 1, :]


def padded(rows):
    return -(-rows // 8) * 8


def turned(plane, by):
    by %= plane.shape[1]
    return pltpu.roll(plane, by, 1) if by else plane


def column_lane(n, z, depth):
    return n * depth + z


def plate_lane(l, depth):
    return column_lane(len(YM), 0, depth) + l


def shift_lanes(plane, sign, halo, lane):
    y = lax.broadcasted_iota(jnp.int32, plane.shape, 1)
    edge = plane.shape[1] - 1 if sign == 1 else 0
    return jnp.where(y == edge, turned(halo, edge - lane), turned(plane, -sign))


def shift_rows(plane, sign):
    width = plane.shape[0]
    x = lax.broadcasted_iota(jnp.int32, plane.shape, 0)
    edge = width - 1 if sign == 1 else 0
    return jnp.where(x == edge, 0.0, pltpu.roll(plane, -sign % width, 0))


def pack_faces(nzt, cot_flow, cot_heat, cot_plate, *refs):
    outs, sems = refs[:nzt], refs[nzt]
    depth, width = cot_flow.shape[1], cot_flow.shape[2]
    layers = cot_plate.shape[0]
    even, _, _ = place("gz")
    copies = []
    for turn in range(nzt):
        up = even if turn == 0 else jnp.logical_not(even)
        z = jnp.where(up, depth - 1, 0)
        sources = []
        for hi, lo in zip(ZM, ZP):
            ref, skip = (cot_flow, 0) if hi < FLOW else (cot_heat, FLOW)
            sources.append(ref.at[jnp.where(up, hi - skip, lo - skip), z])
        sources.append(cot_plate.at[jnp.where(up, layers - 1, 0)])
        for n, source in enumerate(sources):
            target = outs[turn].at[n * width : (n + 1) * width, :]
            copies.append(pltpu.make_async_copy(source, target, sems.at[turn, n]))
            copies[-1].start()
    for copy in copies:
        copy.wait()


def pack_columns(nyt, cot_flow, cot_heat, cot_plate, *refs):
    outs = refs[-nyt:]
    depth, width, length = cot_flow.shape[1:]
    layers = cot_plate.shape[0]
    y = lax.broadcasted_iota(jnp.int32, (width, length), 1)

    def put(packed, plane, source, lane):
        return jnp.where(y == lane, turned(plane, lane - source), packed)

    packs = []
    for side, source in ((YM, length - 1), (YP, 0)):
        packed = jnp.zeros((width, length), jnp.float32)
        for n, k in enumerate(side):
            for z in range(depth):
                packed = put(
                    packed, slab(cot_flow, cot_heat, k, z), source, column_lane(n, z, depth)
                )
        for l in range(layers):
            packed = put(packed, cot_plate[l], source, plate_lane(l, depth))
        packs.append(packed)
    for turn in range(nyt):
        outs[turn][...] = outgoing("gy", turn, packs[0], packs[1])


def pack_edges(nyt, nzt, depth, *refs):
    y_in, outs = refs[:nyt], refs[-nzt:]
    above, below = incoming("gy", [r[...] for r in y_in])
    width, length = above.shape
    y = lax.broadcasted_iota(jnp.int32, above.shape, 1)

    def edge(cz, z):
        down = column_lane(YM.index(DIRECTIONS.index((0, -1, cz))), z, depth)
        up = column_lane(YP.index(DIRECTIONS.index((0, 1, cz))), z, depth)
        up_plane = jnp.where(y == length - 1, turned(above, length - 1 - up), 0.0)
        return jnp.where(y == 0, turned(below, -down), up_plane)

    to_higher, to_lower = edge(-1, depth - 1), edge(1, 0)
    for turn in range(nzt):
        outs[turn][:width, :] = outgoing("gz", turn, to_higher, to_lower)
        if outs[turn].shape[0] > width:
            outs[turn][width:, :] = jnp.zeros((outs[turn].shape[0] - width, length), jnp.float32)


def face_rows(z_in, k, rows):
    up = DIRECTIONS[k][2] == 1
    at = (ZP if up else ZM).index(k) * ((z_in[0].shape[0]) // (len(ZP) + 1))
    above, below = incoming("gz", [r[at + rows.start : at + rows.stop, :] for r in z_in])
    return above if up else below


def pack_rows(nxt, nyt, nzt, cot_flow, cot_heat, cot_plate, *refs):
    z_in, y_in, outs = refs[:nzt], refs[nzt : nzt + nyt], refs[-nxt:]
    depth, width, length = cot_flow.shape[1:]
    layers = cot_plate.shape[0]
    y_above, y_below = incoming("gy", [r[...] for r in y_in])

    def row(k, z, x):
        _, cy, cz = DIRECTIONS[k]
        if 0 <= z + cz < depth:
            value = row_of(cot_flow, cot_heat, k, z + cz, x)
        else:
            value = face_rows(z_in, k, slice(x, x + 1))
        if cy == 0:
            return value
        halo, n = (y_above, YP.index(k)) if cy == 1 else (y_below, YM.index(k))
        return shift_lanes(value, cy, halo[x : x + 1, :], column_lane(n, z, depth))

    used = len(XM) * depth + layers
    for turn in range(nxt):
        if used < outs[turn].shape[0]:
            outs[turn][used:, :] = jnp.zeros((outs[turn].shape[0] - used, length), jnp.float32)
    for n, (hi, lo) in enumerate(zip(XM, XP)):
        for z in range(depth):
            r = n * depth + z
            to_higher, to_lower = row(hi, z, width - 1), row(lo, z, 0)
            for turn in range(nxt):
                outs[turn][r : r + 1, :] = outgoing("gx", turn, to_higher, to_lower)
    for l in range(layers):
        r = len(XM) * depth + l
        for turn in range(nxt):
            outs[turn][r : r + 1, :] = outgoing(
                "gx", turn, cot_plate[l, width - 1 : width, :], cot_plate[l, 0:1, :]
            )


def prepare(pop_flow, pop_heat, flags, nozzle, jet_velocity, *refs):
    ue_out, ratio_out, rows_out, kinds_out = refs[-4:]
    depth, width = flags.shape[:2]
    jets = [jnp.zeros(nozzle.shape, jnp.float32)] * 3
    which = nozzle[...]
    for n in range(jet_velocity.shape[1]):
        hit = which == n
        jets = [jnp.where(hit, jet_velocity[c, n], jets[c]) for c in range(3)]
    for z in range(depth):
        inlet = flags[z] == 2
        pops = [pop_flow[q, z] for q in range(FLOW)]
        rho = sum(pops[1:], pops[0])
        inverse = 1.0 / rho
        values = []
        for c in range(3):
            plus = [pops[q] for q in range(FLOW) if VELOCITY[q][c] == 1]
            minus = [pops[q] for q in range(FLOW) if VELOCITY[q][c] == -1]
            total = sum(plus[1:], plus[0]) - sum(minus[1:], minus[0])
            values.append(jnp.where(inlet, jets[c], total * inverse))
            ue_out[c, z] = values[c]
        heat = [pop_heat[q, z] for q in range(HEAT)]
        values.append(sum(heat[1:], heat[0]) * inverse)
        ratio_out[z] = values[3]
        for side, x in enumerate((0, width - 1)):
            r = side * depth + z
            for c in range(4):
                rows_out[c, r : r + 1, :] = values[c][x : x + 1, :]
            kinds_out[r : r + 1, :] = flags[z, x : x + 1, :]


def collide_back(s, t, ue, ratio, wall, inlet):
    add = lambda a, b: b if a is None else a + b
    zero_moment = WEIGHTS_FLOW[0] * s[0]
    first = [None] * 3
    second = {}
    for group, weight in ((range(1, 7), WEIGHTS_FLOW[1]), (range(7, 19), WEIGHTS_FLOW[7])):
        odd = [None] * 3
        even = {}
        total = None
        for q in group:
            o = OPPOSITE[q]
            if o < q:
                continue
            c = VELOCITY[q]
            plus, minus = s[q] + s[o], s[q] - s[o]
            total = add(total, plus)
            for i in range(3):
                if c[i]:
                    odd[i] = add(odd[i], minus if c[i] == 1 else -minus)
                for j in range(i, 3):
                    if c[i] * c[j]:
                        even[i, j] = add(even.get((i, j)), plus if c[i] * c[j] == 1 else -plus)
        zero_moment = zero_moment + weight * total
        for i in range(3):
            first[i] = add(first[i], weight * odd[i])
        for key, value in even.items():
            second[key] = add(second.get(key), weight * value)
    heat_first = [WEIGHTS_HEAT[1] * (t[2 * c + 1] - t[2 * c + 2]) for c in range(3)]
    heat_zero = WEIGHTS_HEAT[0] * t[0] + WEIGHTS_HEAT[1] * (
        (t[1] + t[2]) + (t[3] + t[4]) + (t[5] + t[6])
    )
    dot = lambda a, b: a[0] * b[0] + a[1] * b[1] + a[2] * b[2]
    bent = [sum(second[min(i, j), max(i, j)] * ue[j] for j in range(3)) for i in range(3)]
    gain = zero_moment * (1.0 - 1.5 * dot(ue, ue)) + 3.0 * dot(first, ue) + 4.5 * dot(bent, ue)
    pull = [
        (3.0 / tau_flow) * (first[i] + 3.0 * bent[i] - ue[i] * zero_moment)
        + (4.0 / tau_heat) * ratio * heat_first[i]
        for i in range(3)
    ]
    common = jnp.where(inlet, gain, (1.0 / tau_flow) * gain - dot(ue, pull))
    pull = [jnp.where(inlet, 0.0, p) for p in pull]
    keep = jnp.where(inlet, 0.0, 1.0 - 1.0 / tau_flow)
    flow = []
    for q in range(FLOW):
        value = keep * s[q] + common
        for i in range(3):
            if VELOCITY[q][i] == 1:
                value = value + pull[i]
            elif VELOCITY[q][i] == -1:
                value = value - pull[i]
        flow.append(jnp.where(wall, s[OPPOSITE[q]], value))
    heat_common = jnp.where(inlet, 0.0, (1.0 / tau_heat) * (heat_zero + 4.0 * dot(heat_first, ue)))
    heat_keep = jnp.where(inlet, 0.0, 1.0 - 1.0 / tau_heat)
    heat = [
        jnp.where(wall, t[OPPOSITE[q]], heat_keep * t[q] + heat_common) for q in range(HEAT)
    ]
    return flow, heat


def interior(nyt, nzt, flags, ue_in, ratio_in, cot_flow, cot_heat, cot_plate, *refs):
    z_in, y_in, yz_in = refs[:nzt], refs[nzt : nzt + nyt], refs[nzt + nyt : 2 * nzt + nyt]
    out_flow, out_heat, out_plate, rows_flow, rows_heat, rows_plate = refs[-10:-4]
    flow_buf, heat_buf, plate_buf, sems = refs[-4:]
    depth, width = cot_flow.shape[1], cot_flow.shape[2]
    layers = cot_plate.shape[0]
    base = lax.axis_index("gz") == 0
    y_above, y_below = incoming("gy", [r[...] for r in y_in])
    yz_above, yz_below = incoming("gz", [r[:width, :] for r in yz_in])
    copies = []

    def send(source, target):
        copies.append(pltpu.make_async_copy(source, target, sems.at[len(copies)]))
        copies[-1].start()

    z_above = z_below = None
    z_rows = slice(len(ZP) * width, (len(ZP) + 1) * width)
    z_above, z_below = incoming("gz", [r[z_rows, :] for r in z_in])
    for l in range(layers):
        own = cot_plate[l]
        up = cot_plate[l + 1] if l + 1 < layers else z_above
        down = cot_plate[l - 1] if l > 0 else z_below
        total = up + down + shift_rows(own, 1) + shift_rows(own, -1)
        total = total + shift_lanes(own, 1, y_above, plate_lane(l, depth))
        total = total + shift_lanes(own, -1, y_below, plate_lane(l, depth))
        value = own + diffusion * (total - 6.0 * own)
        if l == 0:
            value = value + jnp.where(base, 0.25 * cot_heat[5, 0] - coupling * own, 0.0)
        plate_buf[l] = value
        rows_plate[l : l + 1, :] = value[0:1, :]
        rows_plate[layers + l : layers + l + 1, :] = value[width - 1 : width, :]
    send(plate_buf, out_plate)

    for z in range(depth):
        star = []
        for k, (cx, cy, cz) in enumerate(DIRECTIONS):
            at = z + cz
            inside = 0 <= at < depth
            plane = slab(cot_flow, cot_heat, k, at) if inside else face_rows(z_in, k, slice(0, width))
            if cy:
                halo, n = (y_above, YP.index(k)) if cy == 1 else (y_below, YM.index(k))
                if inside:
                    plane = shift_lanes(plane, cy, halo, column_lane(n, at, depth))
                else:
                    lane = plane.shape[1] - 1 if cy == 1 else 0
                    plane = shift_lanes(plane, cy, yz_above if cz == 1 else yz_below, lane)
            if cx:
                plane = shift_rows(plane, cx)
            if cz == -1 and z == 0:
                if k < FLOW:
                    bounced = cot_flow[OPPOSITE[k], 0]
                else:
                    bounced = -cot_heat[OPPOSITE[k - FLOW], 0]
                plane = jnp.where(base, bounced, plane)
            star.append(plane)
        kind = flags[z]
        flow, heat = collide_back(
            star[:FLOW], star[FLOW:], [ue_in[c, z] for c in range(3)], ratio_in[z], kind == 1, kind == 2
        )
        if z == 0:
            source = jnp.where(base, coupling * cot_plate[0], 0.0)
            heat = [value + source for value in heat]
        for values, buf, rows in ((flow, flow_buf, rows_flow), (heat, heat_buf, rows_heat)):
            for q, value in enumerate(values):
                buf[q, z] = value
                rows[q, z : z + 1, :] = value[0:1, :]
                rows[q, depth + z : depth + z + 1, :] = value[width - 1 : width, :]
        send(flow_buf.at[:, z], out_flow.at[:, z])
        send(heat_buf.at[:, z], out_heat.at[:, z])
    for copy in copies:
        copy.wait()


def finish(nxt, rows_in, kinds, rows_flow, rows_heat, rows_plate, *refs):
    x_in, refs = refs[:nxt], refs[nxt + 3 :]
    out_flow, out_heat, out_plate, above_buf, below_buf, star_buf, flow_buf, heat_buf, plate_buf, sems = refs
    depth, width = out_flow.shape[1], out_flow.shape[2]
    layers = out_plate.shape[0]
    above, below = incoming("gx", [r[...] for r in x_in])
    above_buf[...] = above
    below_buf[...] = below
    zero = jnp.zeros((2 * depth, above.shape[1]), jnp.float32)
    star = []
    for k, c in enumerate(DIRECTIONS):
        if c[0] == 0:
            star.append(zero)
            continue
        star_buf[k] = zero
        if c[0] == 1:
            n = XP.index(k) * depth
            star_buf[k, depth:, :] = above_buf[n : n + depth, :]
        else:
            n = XM.index(k) * depth
            star_buf[k, :depth, :] = below_buf[n : n + depth, :]
        star.append(star_buf[k])
    kind = kinds[...]
    flow, heat = collide_back(
        star[:FLOW], star[FLOW:], [rows_in[c] for c in range(3)], rows_in[3], kind == 1, kind == 2
    )
    copies = []
    for values, rows, buf, out in (
        (flow, rows_flow, flow_buf, out_flow),
        (heat, rows_heat, heat_buf, out_heat),
    ):
        for q, value in enumerate(values):
            buf[q] = rows[q] + value
        for side, x in enumerate((0, width - 1)):
            source = buf.at[:, side * depth : (side + 1) * depth, :]
            copies.append(pltpu.make_async_copy(source, out.at[:, :, x, :], sems.at[len(copies)]))
            copies[-1].start()
    n = len(XP) * depth
    for side, (x, beside) in enumerate(((0, below_buf), (width - 1, above_buf))):
        rows = slice(side * layers, (side + 1) * layers)
        plate_buf[side] = rows_plate[rows, :] + diffusion * beside[n : n + layers, :]
        copies.append(pltpu.make_async_copy(plate_buf.at[side], out_plate.at[:, x, :], sems.at[len(copies)]))
        copies[-1].start()
    for copy in copies:
        copy.wait()


def kernel_call(body, outs, spaces, name, cost, out_spaces=None, scratch=(), aliases=None):
    return pl.pallas_call(
        body,
        out_shape=outs,
        in_specs=[pl.BlockSpec(memory_space=space) for space in spaces],
        out_specs=[
            pl.BlockSpec(memory_space=space) for space in (out_spaces or [pltpu.VMEM] * len(outs))
        ],
        scratch_shapes=scratch,
        input_output_aliases=aliases or {},
        compiler_params=pltpu.CompilerParams(vmem_limit_bytes=VMEM_LIMIT),
        cost_estimate=pl.CostEstimate(flops=0, bytes_accessed=cost, transcendentals=0),
        name=name,
    )


def local(pop_flow, pop_heat, flags, nozzle_id, jet_velocity, cot_flow, cot_heat, cot_plate):
    nxt, nyt, nzt = (rounds(lax.axis_size(a)) for a in AXES)
    _, depth, width, length = cot_flow.shape
    layers = cot_plate.shape[0]
    f32 = jnp.float32
    array = lambda *shape: jax.ShapeDtypeStruct(shape, f32)
    vmem, hbm = pltpu.VMEM, pltpu.HBM
    cots = (cot_flow, cot_heat, cot_plate)
    side = padded(len(XM) * depth + layers)

    faces = kernel_call(
        functools.partial(pack_faces, nzt),
        [array((len(ZM) + 1) * width, length)] * nzt,
        [hbm] * 3,
        "faces",
        1 << 20,
        scratch=[pltpu.SemaphoreType.DMA((nzt, len(ZM) + 1))],
    )(*(pltpu.with_memory_space_constraint(c, hbm) for c in cots))
    z_in = [swap(v, gz=t) for t, v in enumerate(faces)]
    columns = kernel_call(
        functools.partial(pack_columns, nyt),
        [array(width, length)] * nyt,
        [vmem] * (3 + nzt),
        "columns",
        1 << 18,
    )(*cots, *faces)
    y_in = [swap(v, gy=t) for t, v in enumerate(columns)]
    edges = kernel_call(
        functools.partial(pack_edges, nyt, nzt, depth),
        [array(EDGE_ROWS, length)] * nzt,
        [vmem] * nyt,
        "edges",
        1 << 16,
    )(*y_in)
    yz_in = [swap(v, gz=t) for t, v in enumerate(edges)]
    rows = kernel_call(
        functools.partial(pack_rows, nxt, nyt, nzt),
        [array(side, length)] * nxt,
        [vmem] * (3 + 2 * nzt + nyt),
        "rows",
        1 << 18,
    )(*cots, *z_in, *y_in, *edges)
    x_in = [swap(v, gx=t) for t, v in enumerate(rows)]
    ue, ratio, row_values, row_kinds = kernel_call(
        prepare,
        [
            array(3, depth, width, length),
            array(depth, width, length),
            array(4, 2 * depth, length),
            jax.ShapeDtypeStruct((2 * depth, length), jnp.int32),
        ],
        [vmem] * 4 + [pltpu.SMEM] + [vmem] * nxt,
        "prepare",
        2 << 20,
    )(pop_flow, pop_heat, flags, nozzle_id, jet_velocity, *rows)
    *grads, rows_flow, rows_heat, rows_plate = kernel_call(
        functools.partial(interior, nyt, nzt),
        [array(*c.shape) for c in cots]
        + [array(FLOW, 2 * depth, length), array(HEAT, 2 * depth, length), array(2 * layers, length)],
        [vmem] * (6 + 2 * nzt + nyt),
        "interior",
        4 << 20,
        out_spaces=[hbm] * 3 + [vmem] * 3,
        scratch=[pltpu.VMEM(c.shape, f32) for c in cots] + [pltpu.SemaphoreType.DMA((2 * depth + 1,))],
    )(flags, ue, ratio, *cots, *z_in, *y_in, *yz_in)
    return tuple(
        kernel_call(
            functools.partial(finish, nxt),
            [array(*c.shape) for c in cots],
            [vmem] * (5 + nxt) + [hbm] * 3,
            "finish",
            1 << 20,
            out_spaces=[hbm] * 3,
            scratch=[
                pltpu.VMEM((side, length), f32),
                pltpu.VMEM((side, length), f32),
                pltpu.VMEM((FLOW + HEAT, 2 * depth, length), f32),
                pltpu.VMEM((FLOW, 2 * depth, length), f32),
                pltpu.VMEM((HEAT, 2 * depth, length), f32),
                pltpu.VMEM((2, layers, length), f32),
                pltpu.SemaphoreType.DMA((6,)),
            ],
            aliases={5 + nxt + i: i for i in range(3)},
        )(row_values, row_kinds, rows_flow, rows_heat, rows_plate, *x_in, *grads)
    )


def solution(mesh):
    return jax.shard_map(
        local,
        mesh=mesh,
        in_specs=(
            P(None, "gz", "gx", "gy"),
            P(None, "gz", "gx", "gy"),
            P("gz", "gx", "gy"),
            P("gx", "gy"),
            P(),
            P(None, "gz", "gx", "gy"),
            P(None, "gz", "gx", "gy"),
            P("gz", "gx", "gy"),
        ),
        out_specs=(P(None, "gz", "gx", "gy"), P(None, "gz", "gx", "gy"), P("gz", "gx", "gy")),
        check_vma=False,
    )
```

time: 15 us -> 14.4 us (0.960)
  the two profiles are of different devices: /device:TPU:17 before, /device:TPU:0 now
where the time goes in v3:
time: 14.4 us; the launch traced here: 14.2 us
  starting transfers between devices  6.92 us (48%)
  Pallas kernels  4.25 us (30%)
  waiting for transfers between devices  2.24 us (16%)
  between operations  0.76 us (5%)
    ppermute x6, starting transfers between devices, swap(): return lax.ppermute(value, AXES, pairs)  6.92 us
    ppermute x6, waiting for transfers between devices, swap(): return lax.ppermute(value, AXES, pairs)  2.24 us
    pallas_call x1, Pallas kernels, local(): kernel_call(functools.partial(interior, nyt, nzt), [array(*c.shape) for c...  1.36 us
    pallas_call x1, Pallas kernels, local(): kernel_call(functools.partial(pack_faces, nzt), [array((len(ZM) + 1) * wi...  0.95 us
    pallas_call x1, Pallas kernels, local(): kernel_call(prepare, [array(3, depth, width, length), array(depth, width,...  0.78 us
    pallas_call x1, Pallas kernels, local(): kernel_call(functools.partial(finish, nxt), [array(*c.shape) for c in cot...  0.76 us
  transfers between devices with their start and end apart: 6, of which 2 were waited for; matrix products, arithmetic and copies ran while one was open for 0% of the time, Pallas kernels for 18%

profile of v3, /device:TPU:0, one launch (start us, length us, event | category | flops | bytes accessed | tf_op | source)
XLA Modules:
  0.0 14.2 jit_solution(4866156513345269543)
XLA Ops:
  0.6 0.0 copy-start.2
  0.6 0.0 copy-start.1
  0.7 0.0 copy-start
  0.7 0.9 %faces.1.refs_0_ = f32[112,128]{1,0:T(8,128)S(1)} custom-call(f32[19,4,16,128]{3,2,1,0:T(8,128)} %cot_flow.7, f32[7,4,16,128]{3,2,1,0:T(8,128)} %cot_heat.7, f32[10,16,128]{2,1,0:T(8,128)} %cot_plate.7), custom_call_target="tpu_custom_call" | custom-call | bytes 1048576 | tf_op jit(solution)/shard_map/faces/pallas_call | solution.py:479
  1.6 3.0 %collective-permute-start = (f32[112,128]{1,0:T(8,128)S(1)}, f32[112,128]{1,0:T(8,128)S(1)}, u32[]{:S(2)}, u32[]{:S(2)}) collective-permute-start(f32[112,128]{1,0:T(8,128)S(1)} %faces.1.refs_0_), channel_id=1, source_target_pairs={{0,1},{1,0},{2,3},{3,2},{4,5},{5,4},{6,7},{7,6},{8,9},{9,8},{10,11... | collective-permute-start | bytes 172040 | tf_op jit(solution)/shard_map/ppermute | solution.py:77
  4.7 0.2 %columns.1 = (f32[16,128]{1,0:T(8,128)S(1)}, f32[16,128]{1,0:T(8,128)S(1)}) custom-call(f32[19,4,16,128]{3,2,1,0:T(8,128)S(1)} %copy-done, f32[7,4,16,128]{3,2,1,0:T(8,128)S(1)} %copy-done.1, f32[10,16,128]{2,1,0:T(8,128)S(1)} %copy-done.2, f32[112,128]{1,0:T(8,128)S(1)} %faces.1.refs_0_), custom_call_target="tpu_custom_call" | custom-call | bytes 262144 | tf_op jit(solution)/shard_map/columns/pallas_call | solution.py:488
  4.9 0.0 copy-start.3
  4.9 0.1 collective-permute-start.1
  5.0 1.6 %collective-permute-start.2 = (f32[16,128]{1,0:T(8,128)S(1)}, f32[16,128]{1,0:T(8,128)S(1)}, u32[]{:S(2)}, u32[]{:S(2)}) collective-permute-start(f32[16,128]{1,0:T(8,128)S(1)} %get-tuple-element.18), channel_id=1, source_target_pairs={{0,6},{1,7},{2,4},{3,5},{4,2},{5,3},{6,0},{7,1},{8,14},{9,15},{10,... | collective-permute-start | bytes 24584 | tf_op jit(solution)/shard_map/ppermute | solution.py:77
  6.6 0.0 collective-permute-done.1.refs_0_.refs_1_
  6.6 1.5 %collective-permute-done.2.refs_1_.refs_2_ = f32[16,128]{1,0:T(8,128)S(1)} collective-permute-done((f32[16,128]{1,0:T(8,128)S(1)}, f32[16,128]{1,0:T(8,128)S(1)}, u32[]{:S(2)}, u32[]{:S(2)}) %collective-permute-start.2) | collective-permute-done | bytes 8224 | tf_op jit(solution)/shard_map/ppermute | solution.py:77
  8.1 0.1 edges.1.refs_3_
  8.2 0.4 %collective-permute-start.3 = (f32[48,128]{1,0:T(8,128)S(1)}, f32[48,128]{1,0:T(8,128)S(1)}, u32[]{:S(2)}, u32[]{:S(2)}) collective-permute-start(f32[48,128]{1,0:T(8,128)S(1)} %edges.1.refs_3_), channel_id=1, source_target_pairs={{0,1},{1,0},{2,3},{3,2},{4,5},{5,4},{6,7},{7,6},{8,9},{9,8},{10,11... | collective-permute-start | bytes 73736 | tf_op jit(solution)/shard_map/ppermute | solution.py:77
  8.6 0.0 collective-permute-done.refs_0_
  8.6 0.1 rows.1
  8.7 0.0 copy-start.7
  8.7 1.8 %collective-permute-start.4 = (f32[40,128]{1,0:T(8,128)S(1)}, f32[40,128]{1,0:T(8,128)S(1)}, u32[]{:S(2)}, u32[]{:S(2)}) collective-permute-start(f32[40,128]{1,0:T(8,128)S(1)} %get-tuple-element.19.refs_0_), channel_id=1, source_target_pairs={{0,8},{1,9},{2,10},{3,11},{4,12},{5,13},{6,14},{7,15},{8,0},{9,1},... | collective-permute-start | bytes 61448 | tf_op jit(solution)/shard_map/ppermute | solution.py:77
  10.5 0.0 collective-permute-start.5
  10.6 0.8 %prepare.1 = (f32[3,4,16,128]{3,2,1,0:T(8,128)S(1)}, f32[4,16,128]{2,1,0:T(8,128)S(1)}, f32[4,8,128]{2,1,0:T(8,128)S(1)}, s32[8,128]{1,0:T(8,128)S(1)}) custom-call(f32[19,4,16,128]{3,2,1,0:T(8,128)S(1)} %copy-done.3, f32[7,4,16,128]{3,2,1,0:T(8,128)S(1)} %copy-done.4, s32[4,16,128]{2,1,0:T(8,128)S(1)} %copy-done.5, s32[16,128]{1,0:T(8,128)S(1)} %copy-done.6, ...), custom_call_target="tpu_custom_call" | custom-call | bytes 2097152 | tf_op jit(solution)/shard_map/prepare/pallas_call | solution.py:512
  11.4 0.7 %collective-permute-done.3.refs_3_ = f32[48,128]{1,0:T(8,128)S(1)} collective-permute-done((f32[48,128]{1,0:T(8,128)S(1)}, f32[48,128]{1,0:T(8,128)S(1)}, u32[]{:S(2)}, u32[]{:S(2)}) %collective-permute-start.3) | collective-permute-done | bytes 24608 | tf_op jit(solution)/shard_map/ppermute | solution.py:77
  12.1 1.4 %interior.1 = (f32[19,4,16,128]{3,2,1,0:T(8,128)}, f32[7,4,16,128]{3,2,1,0:T(8,128)}, f32[10,16,128]{2,1,0:T(8,128)}, f32[19,8,128]{2,1,0:T(8,128)S(1)}, f32[7,8...) custom-call(s32[4,16,128]{2,1,0:T(8,128)S(1)} %copy-done.5, f32[3,4,16,128]{3,2,1,0:T(8,128)S(1)} %get-tuple-element.23.ue_in, ...), custom_call_target="tpu_custom_call" | custom-call | bytes 4194304 | tf_op jit(solution)/shard_map/interior/pallas_call | solution.py:524
  13.4 0.0 collective-permute-done.4.refs_0_
  13.4 0.0 collective-permute-done.5.refs_1_
  13.5 0.8 %finish.1 = (f32[19,4,16,128]{3,2,1,0:T(8,128)}, f32[7,4,16,128]{3,2,1,0:T(8,128)}, f32[10,16,128]{2,1,0:T(8,128)}) custom-call(f32[4,8,128]{2,1,0:T(8,128)S(1)} %get-tuple-element.21.rows_in, s32[8,128]{1,0:T(8,128)S(1)} %get-tuple-element.22.kinds, ...), custom_call_target="tpu_custom_call", output_to_operand_aliasing={{0}: (7, {}), {1}: (8, {}), {2}: (9, {})} | custom-call | bytes 1048576 | tf_op jit(solution)/shard_map/finish/pallas_call | solution.py:535
  (11 shorter events, 0.0 us)
Async XLA Ops:
  0.6 4.0 %copy-start.2 = (f32[10,16,128]{2,1,0:T(8,128)S(1)}, f32[10,16,128]{2,1,0:T(8,128)}, u32[]{:S(2)}) copy-start(f32[10,16,128]{2,1,0:T(8,128)} %cot_plate.7) | copy-start | bytes 245764
  0.6 4.0 %copy-start.1 = (f32[7,4,16,128]{3,2,1,0:T(8,128)S(1)}, f32[7,4,16,128]{3,2,1,0:T(8,128)}, u32[]{:S(2)}) copy-start(f32[7,4,16,128]{3,2,1,0:T(8,128)} %cot_heat.7) | copy-start | bytes 688132
  0.7 4.0 %copy-start = (f32[19,4,16,128]{3,2,1,0:T(8,128)S(1)}, f32[19,4,16,128]{3,2,1,0:T(8,128)}, u32[]{:S(2)}) copy-start(f32[19,4,16,128]{3,2,1,0:T(8,128)} %cot_flow.7) | copy-start | bytes 1867780
  1.6 7.0 %collective-permute-start = (f32[112,128]{1,0:T(8,128)S(1)}, f32[112,128]{1,0:T(8,128)S(1)}, u32[]{:S(2)}, u32[]{:S(2)}) collective-permute-start(f32[112,128]{1,0:T(8,128)S(1)} %faces.1.refs_0_), channel_id=1, source_target_pairs={{0,1},{1,0},{2,3},{3,2},{4,5},{5,4},{6,7},{7,6},{8,9},{9,8},{10,11... | collective-permute-start | bytes 172040 | tf_op jit(solution)/shard_map/ppermute | solution.py:77
  4.9 5.7 %copy-start.3 = (f32[19,4,16,128]{3,2,1,0:T(8,128)S(1)}, f32[19,4,16,128]{3,2,1,0:T(8,128)}, u32[]{:S(2)}) copy-start(f32[19,4,16,128]{3,2,1,0:T(8,128)} %pop_flow.1) | copy-start | bytes 1867780
  4.9 1.7 %collective-permute-start.1 = (f32[16,128]{1,0:T(8,128)S(1)}, f32[16,128]{1,0:T(8,128)S(1)}, u32[]{:S(2)}, u32[]{:S(2)}) collective-permute-start(f32[16,128]{1,0:T(8,128)S(1)} %get-tuple-element.17), channel_id=1, source_target_pairs={{0,2},{1,3},{2,0},{3,1},{4,6},{5,7},{6,4},{7,5},{8,10},{9,11},{10,... | collective-permute-start | bytes 24584 | tf_op jit(solution)/shard_map/ppermute | solution.py:77
  5.0 3.1 %collective-permute-start.2 = (f32[16,128]{1,0:T(8,128)S(1)}, f32[16,128]{1,0:T(8,128)S(1)}, u32[]{:S(2)}, u32[]{:S(2)}) collective-permute-start(f32[16,128]{1,0:T(8,128)S(1)} %get-tuple-element.18), channel_id=1, source_target_pairs={{0,6},{1,7},{2,4},{3,5},{4,2},{5,3},{6,0},{7,1},{8,14},{9,15},{10,... | collective-permute-start | bytes 24584 | tf_op jit(solution)/shard_map/ppermute | solution.py:77
  8.2 2.4 %copy-start.4 = (f32[7,4,16,128]{3,2,1,0:T(8,128)S(1)}, f32[7,4,16,128]{3,2,1,0:T(8,128)}, u32[]{:S(2)}) copy-start(f32[7,4,16,128]{3,2,1,0:T(8,128)} %pop_heat.1) | copy-start | bytes 688132
  8.2 2.4 %copy-start.5 = (s32[4,16,128]{2,1,0:T(8,128)S(1)}, s32[4,16,128]{2,1,0:T(8,128)}, u32[]{:S(2)}) copy-start(s32[4,16,128]{2,1,0:T(8,128)} %flags.3) | copy-start | bytes 98308
  8.2 3.9 %collective-permute-start.3 = (f32[48,128]{1,0:T(8,128)S(1)}, f32[48,128]{1,0:T(8,128)S(1)}, u32[]{:S(2)}, u32[]{:S(2)}) collective-permute-start(f32[48,128]{1,0:T(8,128)S(1)} %edges.1.refs_3_), channel_id=1, source_target_pairs={{0,1},{1,0},{2,3},{3,2},{4,5},{5,4},{6,7},{7,6},{8,9},{9,8},{10,11... | collective-permute-start | bytes 73736 | tf_op jit(solution)/shard_map/ppermute | solution.py:77
  8.6 2.0 %copy-start.6 = (s32[16,128]{1,0:T(8,128)S(1)}, s32[16,128]{1,0:T(8,128)}, u32[]{:S(2)}) copy-start(s32[16,128]{1,0:T(8,128)} %nozzle.1) | copy-start | bytes 24580
  8.7 1.9 %copy-start.7 = (f32[3,64]{1,0:T(4,128)S(1)}, f32[3,64]{1,0:T(4,128)}, u32[]{:S(2)}) copy-start(f32[3,64]{1,0:T(4,128)} %jet_velocity.1) | copy-start | bytes 2308
  8.7 4.7 %collective-permute-start.4 = (f32[40,128]{1,0:T(8,128)S(1)}, f32[40,128]{1,0:T(8,128)S(1)}, u32[]{:S(2)}, u32[]{:S(2)}) collective-permute-start(f32[40,128]{1,0:T(8,128)S(1)} %get-tuple-element.19.refs_0_), channel_id=1, source_target_pairs={{0,8},{1,9},{2,10},{3,11},{4,12},{5,13},{6,14},{7,15},{8,0},{9,1},... | collective-permute-start | bytes 61448 | tf_op jit(solution)/shard_map/ppermute | solution.py:77
  10.5 2.9 %collective-permute-start.5 = (f32[40,128]{1,0:T(8,128)S(1)}, f32[40,128]{1,0:T(8,128)S(1)}, u32[]{:S(2)}, u32[]{:S(2)}) collective-permute-start(f32[40,128]{1,0:T(8,128)S(1)} %get-tuple-element.20.refs_1_), channel_id=1, source_target_pairs={{0,2},{1,3},{2,0},{3,1},{4,6},{5,7},{6,4},{7,5},{8,16},{9,17},{10,... | collective-permute-start | bytes 61448 | tf_op jit(solution)/shard_map/ppermute | solution.py:77

commit v4 on v3

--- a/solution.py
+++ b/solution.py
@@ -43,6 +43,8 @@
 COMPONENT = {"gx": 0, "gy": 1, "gz": 2}
 VMEM_LIMIT = 8 << 20
 EDGE_ROWS = 48
+YPAD = (0, 0)
+XPAD = (0, 0)
 
 
 def moving(component, sign):
@@ -177,13 +179,15 @@
             packed = put(packed, cot_plate[l], source, plate_lane(l, depth))
         packs.append(packed)
     for turn in range(nyt):
-        outs[turn][...] = outgoing("gy", turn, packs[0], packs[1])
-
-
-def pack_edges(nyt, nzt, depth, *refs):
+        outs[turn][:width, :] = outgoing("gy", turn, packs[0], packs[1])
+        if outs[turn].shape[0] > width:
+            outs[turn][width:, :] = jnp.zeros((outs[turn].shape[0] - width, length), jnp.float32)
+
+
+def pack_edges(nyt, nzt, depth, width, *refs):
     y_in, outs = refs[:nyt], refs[-nzt:]
-    above, below = incoming("gy", [r[...] for r in y_in])
-    width, length = above.shape
+    above, below = incoming("gy", [r[:width, :] for r in y_in])
+    length = above.shape[1]
     y = lax.broadcasted_iota(jnp.int32, above.shape, 1)
 
     def edge(cz, z):
@@ -210,7 +214,7 @@
     z_in, y_in, outs = refs[:nzt], refs[nzt : nzt + nyt], refs[-nxt:]
     depth, width, length = cot_flow.shape[1:]
     layers = cot_plate.shape[0]
-    y_above, y_below = incoming("gy", [r[...] for r in y_in])
+    y_above, y_below = incoming("gy", [r[:width, :] for r in y_in])
 
     def row(k, z, x):
         _, cy, cz = DIRECTIONS[k]
@@ -330,40 +334,49 @@
     return flow, heat
 
 
-def interior(nyt, nzt, flags, ue_in, ratio_in, cot_flow, cot_heat, cot_plate, *refs):
-    z_in, y_in, yz_in = refs[:nzt], refs[nzt : nzt + nyt], refs[nzt + nyt : 2 * nzt + nyt]
-    out_flow, out_heat, out_plate, rows_flow, rows_heat, rows_plate = refs[-10:-4]
-    flow_buf, heat_buf, plate_buf, sems = refs[-4:]
+def interior(outer, nyt, nzt, flags, ue_in, ratio_in, cot_flow, cot_heat, cot_plate, *refs):
+    z_in, y_in, refs = refs[:nzt], refs[nzt : nzt + nyt], refs[nzt + nyt :]
     depth, width = cot_flow.shape[1], cot_flow.shape[2]
     layers = cot_plate.shape[0]
     base = lax.axis_index("gz") == 0
-    y_above, y_below = incoming("gy", [r[...] for r in y_in])
-    yz_above, yz_below = incoming("gz", [r[:width, :] for r in yz_in])
+    y_above, y_below = incoming("gy", [r[:width, :] for r in y_in])
     copies = []
+    if outer:
+        yz_above, yz_below = incoming("gz", [r[:width, :] for r in refs[:nzt]])
+        out_flow, out_heat, rows_flow, rows_heat, flow_buf, heat_buf, sems = refs[-7:]
+        zs = (0, depth - 1)
+    else:
+        out_flow, out_heat, out_plate, rows_flow, rows_heat, rows_plate = refs[-10:-4]
+        flow_buf, heat_buf, plate_buf, sems = refs[-4:]
+        zs = range(1, depth - 1)
 
     def send(source, target):
         copies.append(pltpu.make_async_copy(source, target, sems.at[len(copies)]))
         copies[-1].start()
 
-    z_above = z_below = None
-    z_rows = slice(len(ZP) * width, (len(ZP) + 1) * width)
-    z_above, z_below = incoming("gz", [r[z_rows, :] for r in z_in])
-    for l in range(layers):
-        own = cot_plate[l]
-        up = cot_plate[l + 1] if l + 1 < layers else z_above
-        down = cot_plate[l - 1] if l > 0 else z_below
-        total = up + down + shift_rows(own, 1) + shift_rows(own, -1)
-        total = total + shift_lanes(own, 1, y_above, plate_lane(l, depth))
-        total = total + shift_lanes(own, -1, y_below, plate_lane(l, depth))
-        value = own + diffusion * (total - 6.0 * own)
-        if l == 0:
-            value = value + jnp.where(base, 0.25 * cot_heat[5, 0] - coupling * own, 0.0)
-        plate_buf[l] = value
-        rows_plate[l : l + 1, :] = value[0:1, :]
-        rows_plate[layers + l : layers + l + 1, :] = value[width - 1 : width, :]
-    send(plate_buf, out_plate)
-
-    for z in range(depth):
+    def plate():
+        z_rows = slice(len(ZP) * width, (len(ZP) + 1) * width)
+        z_above, z_below = incoming("gz", [r[z_rows, :] for r in z_in])
+        for l in range(layers):
+            own = cot_plate[l]
+            up = cot_plate[l + 1] if l + 1 < layers else z_above
+            down = cot_plate[l - 1] if l > 0 else z_below
+            total = up + down + shift_rows(own, 1) + shift_rows(own, -1)
+            total = total + shift_lanes(own, 1, y_above, plate_lane(l, depth))
+            total = total + shift_lanes(own, -1, y_below, plate_lane(l, depth))
+            value = own + diffusion * (total - 6.0 * own)
+            if l == 0:
+                value = value + jnp.where(base, 0.25 * cot_heat[5, 0] - coupling * own, 0.0)
+            plate_buf[l] = value
+            rows_plate[l : l + 1, :] = value[0:1, :]
+            rows_plate[layers + l : layers + l + 1, :] = value[width - 1 : width, :]
+        send(plate_buf, out_plate)
+
+    if not outer:
+        plate()
+    rows_flow[...] = jnp.zeros_like(rows_flow)
+    rows_heat[...] = jnp.zeros_like(rows_heat)
+    for slot, z in enumerate(zs):
         star = []
         for k, (cx, cy, cz) in enumerate(DIRECTIONS):
             at = z + cz
@@ -394,21 +407,22 @@
             heat = [value + source for value in heat]
         for values, buf, rows in ((flow, flow_buf, rows_flow), (heat, heat_buf, rows_heat)):
             for q, value in enumerate(values):
-                buf[q, z] = value
+                buf[q, slot] = value
                 rows[q, z : z + 1, :] = value[0:1, :]
                 rows[q, depth + z : depth + z + 1, :] = value[width - 1 : width, :]
-        send(flow_buf.at[:, z], out_flow.at[:, z])
-        send(heat_buf.at[:, z], out_heat.at[:, z])
+        send(flow_buf.at[:, slot], out_flow.at[:, z])
+        send(heat_buf.at[:, slot], out_heat.at[:, z])
     for copy in copies:
         copy.wait()
 
 
-def finish(nxt, rows_in, kinds, rows_flow, rows_heat, rows_plate, *refs):
+def finish(nxt, rows_in, kinds, rows_flow, rows_heat, rows_plate, outer_flow, outer_heat, *refs):
     x_in, refs = refs[:nxt], refs[nxt + 3 :]
     out_flow, out_heat, out_plate, above_buf, below_buf, star_buf, flow_buf, heat_buf, plate_buf, sems = refs
     depth, width = out_flow.shape[1], out_flow.shape[2]
     layers = out_plate.shape[0]
-    above, below = incoming("gx", [r[...] for r in x_in])
+    used = above_buf.shape[0]
+    above, below = incoming("gx", [r[:used, :] for r in x_in])
     above_buf[...] = above
     below_buf[...] = below
     zero = jnp.zeros((2 * depth, above.shape[1]), jnp.float32)
@@ -430,12 +444,12 @@
         star[:FLOW], star[FLOW:], [rows_in[c] for c in range(3)], rows_in[3], kind == 1, kind == 2
     )
     copies = []
-    for values, rows, buf, out in (
-        (flow, rows_flow, flow_buf, out_flow),
-        (heat, rows_heat, heat_buf, out_heat),
+    for values, rows, outer_rows, buf, out in (
+        (flow, rows_flow, outer_flow, flow_buf, out_flow),
+        (heat, rows_heat, outer_heat, heat_buf, out_heat),
     ):
         for q, value in enumerate(values):
-            buf[q] = rows[q] + value
+            buf[q] = rows[q] + outer_rows[q] + value
         for side, x in enumerate((0, width - 1)):
             source = buf.at[:, side * depth : (side + 1) * depth, :]
             copies.append(pltpu.make_async_copy(source, out.at[:, :, x, :], sems.at[len(copies)]))
@@ -487,28 +501,12 @@
     z_in = [swap(v, gz=t) for t, v in enumerate(faces)]
     columns = kernel_call(
         functools.partial(pack_columns, nyt),
-        [array(width, length)] * nyt,
+        [array(width + YPAD[t], length) for t in range(nyt)],
         [vmem] * (3 + nzt),
         "columns",
         1 << 18,
     )(*cots, *faces)
     y_in = [swap(v, gy=t) for t, v in enumerate(columns)]
-    edges = kernel_call(
-        functools.partial(pack_edges, nyt, nzt, depth),
-        [array(EDGE_ROWS, length)] * nzt,
-        [vmem] * nyt,
-        "edges",
-        1 << 16,
-    )(*y_in)
-    yz_in = [swap(v, gz=t) for t, v in enumerate(edges)]
-    rows = kernel_call(
-        functools.partial(pack_rows, nxt, nyt, nzt),
-        [array(side, length)] * nxt,
-        [vmem] * (3 + 2 * nzt + nyt),
-        "rows",
-        1 << 18,
-    )(*cots, *z_in, *y_in, *edges)
-    x_in = [swap(v, gx=t) for t, v in enumerate(rows)]
     ue, ratio, row_values, row_kinds = kernel_call(
         prepare,
         [
@@ -517,25 +515,62 @@
             array(4, 2 * depth, length),
             jax.ShapeDtypeStruct((2 * depth, length), jnp.int32),
         ],
-        [vmem] * 4 + [pltpu.SMEM] + [vmem] * nxt,
+        [vmem] * 4 + [pltpu.SMEM] + [vmem] * nyt,
         "prepare",
         2 << 20,
-    )(pop_flow, pop_heat, flags, nozzle_id, jet_velocity, *rows)
+    )(pop_flow, pop_heat, flags, nozzle_id, jet_velocity, *columns)
+    edges = kernel_call(
+        functools.partial(pack_edges, nyt, nzt, depth, width),
+        [array(EDGE_ROWS, length)] * nzt,
+        [vmem] * (nyt + 1),
+        "edges",
+        1 << 16,
+    )(*y_in, ratio)
+    yz_in = [swap(v, gz=t) for t, v in enumerate(edges)]
+    rows = kernel_call(
+        functools.partial(pack_rows, nxt, nyt, nzt),
+        [array(side + XPAD[t], length) for t in range(nxt)],
+        [vmem] * (3 + 2 * nzt + nyt),
+        "rows",
+        1 << 18,
+    )(*cots, *z_in, *y_in, *edges)
+    x_in = [swap(v, gx=t) for t, v in enumerate(rows)]
+    ends = [array(FLOW, 2 * depth, length), array(HEAT, 2 * depth, length)]
+    inner = max(depth - 2, 1)
     *grads, rows_flow, rows_heat, rows_plate = kernel_call(
-        functools.partial(interior, nyt, nzt),
-        [array(*c.shape) for c in cots]
-        + [array(FLOW, 2 * depth, length), array(HEAT, 2 * depth, length), array(2 * layers, length)],
-        [vmem] * (6 + 2 * nzt + nyt),
-        "interior",
-        4 << 20,
+        functools.partial(interior, False, nyt, nzt),
+        [array(*c.shape) for c in cots] + ends + [array(2 * layers, length)],
+        [vmem] * (6 + nzt + nyt + nxt),
+        "inner",
+        2 << 20,
         out_spaces=[hbm] * 3 + [vmem] * 3,
-        scratch=[pltpu.VMEM(c.shape, f32) for c in cots] + [pltpu.SemaphoreType.DMA((2 * depth + 1,))],
-    )(flags, ue, ratio, *cots, *z_in, *y_in, *yz_in)
+        scratch=[
+            pltpu.VMEM((FLOW, inner, width, length), f32),
+            pltpu.VMEM((HEAT, inner, width, length), f32),
+            pltpu.VMEM(cot_plate.shape, f32),
+            pltpu.SemaphoreType.DMA((2 * depth + 1,)),
+        ],
+    )(flags, ue, ratio, *cots, *z_in, *y_in, *rows)
+    given = 6 + 2 * nzt + nyt
+    flow, heat, outer_flow, outer_heat = kernel_call(
+        functools.partial(interior, True, nyt, nzt),
+        [array(*c.shape) for c in cots[:2]] + ends,
+        [vmem] * given + [hbm] * 2,
+        "outer",
+        2 << 20,
+        out_spaces=[hbm] * 2 + [vmem] * 2,
+        scratch=[
+            pltpu.VMEM((FLOW, 2, width, length), f32),
+            pltpu.VMEM((HEAT, 2, width, length), f32),
+            pltpu.SemaphoreType.DMA((4,)),
+        ],
+        aliases={given: 0, given + 1: 1},
+    )(flags, ue, ratio, *cots, *z_in, *y_in, *yz_in, *grads[:2])
     return tuple(
         kernel_call(
             functools.partial(finish, nxt),
             [array(*c.shape) for c in cots],
-            [vmem] * (5 + nxt) + [hbm] * 3,
+            [vmem] * (7 + nxt) + [hbm] * 3,
             "finish",
             1 << 20,
             out_spaces=[hbm] * 3,
@@ -548,8 +583,8 @@
                 pltpu.VMEM((2, layers, length), f32),
                 pltpu.SemaphoreType.DMA((6,)),
             ],
-            aliases={5 + nxt + i: i for i in range(3)},
-        )(row_values, row_kinds, rows_flow, rows_heat, rows_plate, *x_in, *grads)
+            aliases={7 + nxt + i: i for i in range(3)},
+        )(row_values, row_kinds, rows_flow, rows_heat, rows_plate, outer_flow, outer_heat, *x_in, flow, heat, grads[2])
     )
 
 

time: 14.4 us -> 14.1 us (0.979)
  waiting for transfers between devices: 2.24 us -> 1.11 us
  Pallas kernels: 4.25 us -> 5.06 us
    ppermute x6, waiting for transfers between devices: 2.24 us -> 1.11 us  [swap(): return lax.ppermute(value, AXES, pairs)]
    pallas_call x4 -> x5, Pallas kernels: 1.76 us -> 2.57 us  [the longest x1 1.15 us: local(): kernel_call(functools.partial(interior, False, nyt, nzt), [array(*c.shape...]
  transfers between devices with their start and end apart: 6 -> 6, of which waited for: 2 -> 2; matrix products, arithmetic and copies ran while one was open for 0% -> 0% of each run, Pallas kernels for 18% -> 24%
where the time goes in v4:
time: 14.1 us; the launch traced here: 13.9 us
  starting transfers between devices  6.87 us (49%)
  Pallas kernels  5.06 us (36%)
  waiting for transfers between devices  1.11 us (8%)
  between operations  0.78 us (6%)
    ppermute x6, starting transfers between devices, swap(): return lax.ppermute(value, AXES, pairs)  6.87 us
    pallas_call x1, Pallas kernels, local(): kernel_call(functools.partial(interior, False, nyt, nzt), [array(*c.shape...  1.15 us
    ppermute x6, waiting for transfers between devices, swap(): return lax.ppermute(value, AXES, pairs)  1.11 us
    pallas_call x1, Pallas kernels, local(): kernel_call(functools.partial(interior, True, nyt, nzt), [array(*c.shape)...  1.01 us
    pallas_call x1, Pallas kernels, local(): kernel_call(functools.partial(pack_faces, nzt), [array((len(ZM) + 1) * wi...  0.95 us
    pallas_call x1, Pallas kernels, local(): kernel_call(prepare, [array(3, depth, width, length), array(depth, width,...  0.78 us
    pallas_call x1, Pallas kernels, local(): kernel_call(functools.partial(finish, nxt), [array(*c.shape) for c in cot...  0.76 us
  transfers between devices with their start and end apart: 6, of which 2 were waited for; matrix products, arithmetic and copies ran while one was open for 0% of the time, Pallas kernels for 24%

profile of v4, /device:TPU:0, one launch (start us, length us, event | category | flops | bytes accessed | tf_op | source)
XLA Modules:
  0.0 13.9 jit_solution(4956847658740017684)
XLA Ops:
  0.7 0.9 %faces.1.refs_0_ = f32[112,128]{1,0:T(8,128)S(1)} custom-call(f32[19,4,16,128]{3,2,1,0:T(8,128)} %cot_flow.9, f32[7,4,16,128]{3,2,1,0:T(8,128)} %cot_heat.9, f32[10,16,128]{2,1,0:T(8,128)} %cot_plate.9), custom_call_target="tpu_custom_call" | custom-call | bytes 1048576 | tf_op jit(solution)/shard_map/faces/pallas_call | solution.py:493
  1.6 0.0 copy-start.3
  1.6 0.0 copy-start.4
  1.6 0.0 copy-start.5
  1.7 3.0 %collective-permute-start = (f32[112,128]{1,0:T(8,128)S(1)}, f32[112,128]{1,0:T(8,128)S(1)}, u32[]{:S(2)}, u32[]{:S(2)}) collective-permute-start(f32[112,128]{1,0:T(8,128)S(1)} %faces.1.refs_0_), channel_id=1, source_target_pairs={{0,1},{1,0},{2,3},{3,2},{4,5},{5,4},{6,7},{7,6},{8,9},{9,8},{10,11... | collective-permute-start | bytes 172040 | tf_op jit(solution)/shard_map/ppermute | solution.py:79
  4.7 0.2 %columns.1 = (f32[16,128]{1,0:T(8,128)S(1)}, f32[16,128]{1,0:T(8,128)S(1)}) custom-call(f32[19,4,16,128]{3,2,1,0:T(8,128)S(1)} %copy-done, f32[7,4,16,128]{3,2,1,0:T(8,128)S(1)} %copy-done.1, f32[10,16,128]{2,1,0:T(8,128)S(1)} %copy-done.2, f32[112,128]{1,0:T(8,128)S(1)} %faces.1.refs_0_), custom_call_target="tpu_custom_call" | custom-call | bytes 262144 | tf_op jit(solution)/shard_map/columns/pallas_call | solution.py:502
  4.9 0.0 copy-start.7
  4.9 0.1 collective-permute-start.1
  5.0 1.6 %collective-permute-start.2 = (f32[16,128]{1,0:T(8,128)S(1)}, f32[16,128]{1,0:T(8,128)S(1)}, u32[]{:S(2)}, u32[]{:S(2)}) collective-permute-start(f32[16,128]{1,0:T(8,128)S(1)} %get-tuple-element.22.refs_1_), channel_id=1, source_target_pairs={{0,6},{1,7},{2,4},{3,5},{4,2},{5,3},{6,0},{7,1},{8,14},{9,15},{10,... | collective-permute-start | bytes 24584 | tf_op jit(solution)/shard_map/ppermute | solution.py:79
  6.6 0.8 %prepare.1 = (f32[3,4,16,128]{3,2,1,0:T(8,128)S(1)}, f32[4,16,128]{2,1,0:T(8,128)S(1)}, f32[4,8,128]{2,1,0:T(8,128)S(1)}, s32[8,128]{1,0:T(8,128)S(1)}) custom-call(f32[19,4,16,128]{3,2,1,0:T(8,128)S(1)} %copy-done.3, f32[7,4,16,128]{3,2,1,0:T(8,128)S(1)} %copy-done.5, s32[4,16,128]{2,1,0:T(8,128)S(1)} %copy-done.4, s32[16,128]{1,0:T(8,128)S(1)} %copy-done.6, ...), custom_call_target="tpu_custom_call" | custom-call | bytes 2097152 | tf_op jit(solution)/shard_map/prepare/pallas_call | solution.py:510
  7.4 0.0 collective-permute-done.1.refs_0_.refs_1_
  7.4 0.7 %collective-permute-done.2.refs_1_.refs_2_ = f32[16,128]{1,0:T(8,128)S(1)} collective-permute-done((f32[16,128]{1,0:T(8,128)S(1)}, f32[16,128]{1,0:T(8,128)S(1)}, u32[]{:S(2)}, u32[]{:S(2)}) %collective-permute-start.2) | collective-permute-done | bytes 8224 | tf_op jit(solution)/shard_map/ppermute | solution.py:79
  8.1 0.1 edges.1.refs_3_
  8.2 0.3 %collective-permute-start.3 = (f32[48,128]{1,0:T(8,128)S(1)}, f32[48,128]{1,0:T(8,128)S(1)}, u32[]{:S(2)}, u32[]{:S(2)}) collective-permute-start(f32[48,128]{1,0:T(8,128)S(1)} %edges.1.refs_3_), channel_id=1, source_target_pairs={{0,1},{1,0},{2,3},{3,2},{4,5},{5,4},{6,7},{7,6},{8,9},{9,8},{10,11... | collective-permute-start | bytes 73736 | tf_op jit(solution)/shard_map/ppermute | solution.py:79
  8.6 0.0 collective-permute-done.refs_0_
  8.6 0.1 rows.1
  8.7 1.8 %collective-permute-start.4 = (f32[40,128]{1,0:T(8,128)S(1)}, f32[40,128]{1,0:T(8,128)S(1)}, u32[]{:S(2)}, u32[]{:S(2)}) collective-permute-start(f32[40,128]{1,0:T(8,128)S(1)} %get-tuple-element.27.refs_3_), channel_id=1, source_target_pairs={{0,8},{1,9},{2,10},{3,11},{4,12},{5,13},{6,14},{7,15},{8,0},{9,1},... | collective-permute-start | bytes 61448 | tf_op jit(solution)/shard_map/ppermute | solution.py:79
  10.5 0.0 collective-permute-start.5
  10.5 1.1 %inner.1 = (f32[19,4,16,128]{3,2,1,0:T(8,128)}, f32[7,4,16,128]{3,2,1,0:T(8,128)}, f32[10,16,128]{2,1,0:T(8,128)}, f32[19,8,128]{2,1,0:T(8,128)S(1)}, f32[7,8,128]{2,1,0:T(8,128)S(1)}, /*index=5*/f32[20,128]{1,0:T(8,128)S(1)}) custom-call(s32[4,16,128]{2,1,0:T(8,128)S(1)} %copy-done.4, f32[3,4,16,128]{3,2,1,0:T(8,128)S(1)} %get-tuple-element.25.ue_in, ...), custom_call_target="tpu_custom_call" | custom-call | bytes 2097152 | tf_op jit(solution)/shard_map/inner/pallas_call | solution.py:540
  11.7 0.4 %collective-permute-done.3.refs_3_ = f32[48,128]{1,0:T(8,128)S(1)} collective-permute-done((f32[48,128]{1,0:T(8,128)S(1)}, f32[48,128]{1,0:T(8,128)S(1)}, u32[]{:S(2)}, u32[]{:S(2)}) %collective-permute-start.3) | collective-permute-done | bytes 24608 | tf_op jit(solution)/shard_map/ppermute | solution.py:79
  12.1 1.0 %outer.1 = (f32[19,4,16,128]{3,2,1,0:T(8,128)}, f32[7,4,16,128]{3,2,1,0:T(8,128)}, f32[19,8,128]{2,1,0:T(8,128)S(1)}, f32[7,8,128]{2,1,0:T(8,128)S(1)}) custom-call(s32[4,16,128]{2,1,0:T(8,128)S(1)} %copy-done.4, f32[3,4,16,128]{3,2,1,0:T(8,128)S(1)} %get-tuple-element.25.ue_in, ...), custom_call_target="tpu_custom_call", output_to_operand_aliasing={{0}: (10, {}), {1}: (11, {})} | custom-call | bytes 2097152 | tf_op jit(solution)/shard_map/outer/pallas_call | solution.py:555
  13.1 0.0 collective-permute-done.4.refs_0_
  13.1 0.0 collective-permute-done.5.refs_1_
  13.1 0.8 %finish.1 = (f32[19,4,16,128]{3,2,1,0:T(8,128)}, f32[7,4,16,128]{3,2,1,0:T(8,128)}, f32[10,16,128]{2,1,0:T(8,128)}) custom-call(f32[4,8,128]{2,1,0:T(8,128)S(1)} %get-tuple-element.23.rows_in, s32[8,128]{1,0:T(8,128)S(1)} %get-tuple-element.24.kinds, ...), custom_call_target="tpu_custom_call", output_to_operand_aliasing={{0}: (9, {}), {1}: (10, {}), {2}: (11, {})} | custom-call | bytes 1048576 | tf_op jit(solution)/shard_map/finish/pallas_call | solution.py:570
  (12 shorter events, 0.0 us)
Async XLA Ops:
  0.6 4.1 %copy-start.2 = (f32[10,16,128]{2,1,0:T(8,128)S(1)}, f32[10,16,128]{2,1,0:T(8,128)}, u32[]{:S(2)}) copy-start(f32[10,16,128]{2,1,0:T(8,128)} %cot_plate.9) | copy-start | bytes 245764
  0.6 4.0 %copy-start.1 = (f32[7,4,16,128]{3,2,1,0:T(8,128)S(1)}, f32[7,4,16,128]{3,2,1,0:T(8,128)}, u32[]{:S(2)}) copy-start(f32[7,4,16,128]{3,2,1,0:T(8,128)} %cot_heat.9) | copy-start | bytes 688132
  0.7 4.0 %copy-start = (f32[19,4,16,128]{3,2,1,0:T(8,128)S(1)}, f32[19,4,16,128]{3,2,1,0:T(8,128)}, u32[]{:S(2)}) copy-start(f32[19,4,16,128]{3,2,1,0:T(8,128)} %cot_flow.9) | copy-start | bytes 1867780
  1.6 5.0 %copy-start.3 = (f32[19,4,16,128]{3,2,1,0:T(8,128)S(1)}, f32[19,4,16,128]{3,2,1,0:T(8,128)}, u32[]{:S(2)}) copy-start(f32[19,4,16,128]{3,2,1,0:T(8,128)} %pop_flow.1) | copy-start | bytes 1867780
  1.6 5.0 %copy-start.4 = (s32[4,16,128]{2,1,0:T(8,128)S(1)}, s32[4,16,128]{2,1,0:T(8,128)}, u32[]{:S(2)}) copy-start(s32[4,16,128]{2,1,0:T(8,128)} %flags.5) | copy-start | bytes 98308
  1.6 5.0 %copy-start.5 = (f32[7,4,16,128]{3,2,1,0:T(8,128)S(1)}, f32[7,4,16,128]{3,2,1,0:T(8,128)}, u32[]{:S(2)}) copy-start(f32[7,4,16,128]{3,2,1,0:T(8,128)} %pop_heat.1) | copy-start | bytes 688132
  1.7 6.9 %collective-permute-start = (f32[112,128]{1,0:T(8,128)S(1)}, f32[112,128]{1,0:T(8,128)S(1)}, u32[]{:S(2)}, u32[]{:S(2)}) collective-permute-start(f32[112,128]{1,0:T(8,128)S(1)} %faces.1.refs_0_), channel_id=1, source_target_pairs={{0,1},{1,0},{2,3},{3,2},{4,5},{5,4},{6,7},{7,6},{8,9},{9,8},{10,11... | collective-permute-start | bytes 172040 | tf_op jit(solution)/shard_map/ppermute | solution.py:79
  4.7 1.9 %copy-start.6 = (s32[16,128]{1,0:T(8,128)S(1)}, s32[16,128]{1,0:T(8,128)}, u32[]{:S(2)}) copy-start(s32[16,128]{1,0:T(8,128)} %nozzle.1) | copy-start | bytes 24580
  4.9 1.7 %copy-start.7 = (f32[3,64]{1,0:T(4,128)S(1)}, f32[3,64]{1,0:T(4,128)}, u32[]{:S(2)}) copy-start(f32[3,64]{1,0:T(4,128)} %jet_velocity.1) | copy-start | bytes 2308
  4.9 2.5 %collective-permute-start.1 = (f32[16,128]{1,0:T(8,128)S(1)}, f32[16,128]{1,0:T(8,128)S(1)}, u32[]{:S(2)}, u32[]{:S(2)}) collective-permute-start(f32[16,128]{1,0:T(8,128)S(1)} %get-tuple-element.21.refs_0_), channel_id=1, source_target_pairs={{0,2},{1,3},{2,0},{3,1},{4,6},{5,7},{6,4},{7,5},{8,10},{9,11},{10,... | collective-permute-start | bytes 24584 | tf_op jit(solution)/shard_map/ppermute | solution.py:79
  5.0 3.1 %collective-permute-start.2 = (f32[16,128]{1,0:T(8,128)S(1)}, f32[16,128]{1,0:T(8,128)S(1)}, u32[]{:S(2)}, u32[]{:S(2)}) collective-permute-start(f32[16,128]{1,0:T(8,128)S(1)} %get-tuple-element.22.refs_1_), channel_id=1, source_target_pairs={{0,6},{1,7},{2,4},{3,5},{4,2},{5,3},{6,0},{7,1},{8,14},{9,15},{10,... | collective-permute-start | bytes 24584 | tf_op jit(solution)/shard_map/ppermute | solution.py:79
  8.2 3.8 %collective-permute-start.3 = (f32[48,128]{1,0:T(8,128)S(1)}, f32[48,128]{1,0:T(8,128)S(1)}, u32[]{:S(2)}, u32[]{:S(2)}) collective-permute-start(f32[48,128]{1,0:T(8,128)S(1)} %edges.1.refs_3_), channel_id=1, source_target_pairs={{0,1},{1,0},{2,3},{3,2},{4,5},{5,4},{6,7},{7,6},{8,9},{9,8},{10,11... | collective-permute-start | bytes 73736 | tf_op jit(solution)/shard_map/ppermute | solution.py:79
  8.7 4.4 %collective-permute-start.4 = (f32[40,128]{1,0:T(8,128)S(1)}, f32[40,128]{1,0:T(8,128)S(1)}, u32[]{:S(2)}, u32[]{:S(2)}) collective-permute-start(f32[40,128]{1,0:T(8,128)S(1)} %get-tuple-element.27.refs_3_), channel_id=1, source_target_pairs={{0,8},{1,9},{2,10},{3,11},{4,12},{5,13},{6,14},{7,15},{8,0},{9,1},... | collective-permute-start | bytes 61448 | tf_op jit(solution)/shard_map/ppermute | solution.py:79
  10.5 2.6 %collective-permute-start.5 = (f32[40,128]{1,0:T(8,128)S(1)}, f32[40,128]{1,0:T(8,128)S(1)}, u32[]{:S(2)}, u32[]{:S(2)}) collective-permute-start(f32[40,128]{1,0:T(8,128)S(1)} %get-tuple-element.28.refs_4_), channel_id=1, source_target_pairs={{0,2},{1,3},{2,0},{3,1},{4,6},{5,7},{6,4},{7,5},{8,16},{9,17},{10,... | collective-permute-start | bytes 61448 | tf_op jit(solution)/shard_map/ppermute | solution.py:79

commit v5 on v3

--- a/solution.py
+++ b/solution.py
@@ -42,7 +42,9 @@
 AXES = ("gx", "gy", "gz")
 COMPONENT = {"gx": 0, "gy": 1, "gz": 2}
 VMEM_LIMIT = 8 << 20
-EDGE_ROWS = 48
+YZ_ROWS = 48
+YPAD = (0, 0)
+XPAD = (0, 0)
 
 
 def moving(component, sign):
@@ -156,8 +158,8 @@
         copy.wait()
 
 
-def pack_columns(nyt, cot_flow, cot_heat, cot_plate, *refs):
-    outs = refs[-nyt:]
+def pack_columns(nyt, nzt, cot_flow, cot_heat, cot_plate, *refs):
+    outs, yz_outs = refs[-nyt * (nzt + 1) : -nyt * nzt], refs[-nyt * nzt :]
     depth, width, length = cot_flow.shape[1:]
     layers = cot_plate.shape[0]
     y = lax.broadcasted_iota(jnp.int32, (width, length), 1)
@@ -177,26 +179,25 @@
             packed = put(packed, cot_plate[l], source, plate_lane(l, depth))
         packs.append(packed)
     for turn in range(nyt):
-        outs[turn][...] = outgoing("gy", turn, packs[0], packs[1])
-
-
-def pack_edges(nyt, nzt, depth, *refs):
-    y_in, outs = refs[:nyt], refs[-nzt:]
-    above, below = incoming("gy", [r[...] for r in y_in])
-    width, length = above.shape
-    y = lax.broadcasted_iota(jnp.int32, above.shape, 1)
-
-    def edge(cz, z):
-        down = column_lane(YM.index(DIRECTIONS.index((0, -1, cz))), z, depth)
-        up = column_lane(YP.index(DIRECTIONS.index((0, 1, cz))), z, depth)
-        up_plane = jnp.where(y == length - 1, turned(above, length - 1 - up), 0.0)
-        return jnp.where(y == 0, turned(below, -down), up_plane)
-
-    to_higher, to_lower = edge(-1, depth - 1), edge(1, 0)
-    for turn in range(nzt):
-        outs[turn][:width, :] = outgoing("gz", turn, to_higher, to_lower)
+        outs[turn][:width, :] = outgoing("gy", turn, packs[0], packs[1])
         if outs[turn].shape[0] > width:
             outs[turn][width:, :] = jnp.zeros((outs[turn].shape[0] - width, length), jnp.float32)
+
+    def plane(cy, cz):
+        k = DIRECTIONS.index((0, cy, cz))
+        return slab(cot_flow, cot_heat, k, depth - 1 if cz == -1 else 0)
+
+    for ty in range(nyt):
+        for tz in range(nzt):
+            out = yz_outs[ty * nzt + tz]
+            out[:width, :] = outgoing(
+                "gy",
+                ty,
+                outgoing("gz", tz, plane(-1, -1), plane(-1, 1)),
+                outgoing("gz", tz, plane(1, -1), plane(1, 1)),
+            )
+            if out.shape[0] > width:
+                out[width:, :] = jnp.zeros((out.shape[0] - width, length), jnp.float32)
 
 
 def face_rows(z_in, k, rows):
@@ -210,7 +211,7 @@
     z_in, y_in, outs = refs[:nzt], refs[nzt : nzt + nyt], refs[-nxt:]
     depth, width, length = cot_flow.shape[1:]
     layers = cot_plate.shape[0]
-    y_above, y_below = incoming("gy", [r[...] for r in y_in])
+    y_above, y_below = incoming("gy", [r[:width, :] for r in y_in])
 
     def row(k, z, x):
         _, cy, cz = DIRECTIONS[k]
@@ -331,14 +332,15 @@
 
 
 def interior(nyt, nzt, flags, ue_in, ratio_in, cot_flow, cot_heat, cot_plate, *refs):
-    z_in, y_in, yz_in = refs[:nzt], refs[nzt : nzt + nyt], refs[nzt + nyt : 2 * nzt + nyt]
+    z_in, y_in, yz_in = refs[:nzt], refs[nzt : nzt + nyt], refs[nzt + nyt : nzt + nyt + nyt * nzt]
     out_flow, out_heat, out_plate, rows_flow, rows_heat, rows_plate = refs[-10:-4]
     flow_buf, heat_buf, plate_buf, sems = refs[-4:]
     depth, width = cot_flow.shape[1], cot_flow.shape[2]
     layers = cot_plate.shape[0]
     base = lax.axis_index("gz") == 0
-    y_above, y_below = incoming("gy", [r[...] for r in y_in])
-    yz_above, yz_below = incoming("gz", [r[:width, :] for r in yz_in])
+    y_above, y_below = incoming("gy", [r[:width, :] for r in y_in])
+    sides = [incoming("gy", [r[:width, :] for r in yz_in[tz::nzt]]) for tz in range(nzt)]
+    yz = {1: incoming("gz", [side[0] for side in sides]), -1: incoming("gz", [side[1] for side in sides])}
     copies = []
 
     def send(source, target):
@@ -374,8 +376,8 @@
                 if inside:
                     plane = shift_lanes(plane, cy, halo, column_lane(n, at, depth))
                 else:
-                    lane = plane.shape[1] - 1 if cy == 1 else 0
-                    plane = shift_lanes(plane, cy, yz_above if cz == 1 else yz_below, lane)
+                    lane = 0 if cy == 1 else plane.shape[1] - 1
+                    plane = shift_lanes(plane, cy, yz[cy][0 if cz == 1 else 1], lane)
             if cx:
                 plane = shift_rows(plane, cx)
             if cz == -1 and z == 0:
@@ -408,7 +410,8 @@
     out_flow, out_heat, out_plate, above_buf, below_buf, star_buf, flow_buf, heat_buf, plate_buf, sems = refs
     depth, width = out_flow.shape[1], out_flow.shape[2]
     layers = out_plate.shape[0]
-    above, below = incoming("gx", [r[...] for r in x_in])
+    used = above_buf.shape[0]
+    above, below = incoming("gx", [r[:used, :] for r in x_in])
     above_buf[...] = above
     below_buf[...] = below
     zero = jnp.zeros((2 * depth, above.shape[1]), jnp.float32)
@@ -486,28 +489,21 @@
     )(*(pltpu.with_memory_space_constraint(c, hbm) for c in cots))
     z_in = [swap(v, gz=t) for t, v in enumerate(faces)]
     columns = kernel_call(
-        functools.partial(pack_columns, nyt),
-        [array(width, length)] * nyt,
+        functools.partial(pack_columns, nyt, nzt),
+        [array(width + YPAD[t], length) for t in range(nyt)] + [array(YZ_ROWS, length)] * (nyt * nzt),
         [vmem] * (3 + nzt),
         "columns",
         1 << 18,
     )(*cots, *faces)
-    y_in = [swap(v, gy=t) for t, v in enumerate(columns)]
-    edges = kernel_call(
-        functools.partial(pack_edges, nyt, nzt, depth),
-        [array(EDGE_ROWS, length)] * nzt,
-        [vmem] * nyt,
-        "edges",
-        1 << 16,
-    )(*y_in)
-    yz_in = [swap(v, gz=t) for t, v in enumerate(edges)]
+    y_in = [swap(v, gy=t) for t, v in enumerate(columns[:nyt])]
+    yz_in = [swap(columns[nyt + ty * nzt + tz], gy=ty, gz=tz) for ty in range(nyt) for tz in range(nzt)]
     rows = kernel_call(
         functools.partial(pack_rows, nxt, nyt, nzt),
-        [array(side, length)] * nxt,
-        [vmem] * (3 + 2 * nzt + nyt),
+        [array(side + XPAD[t], length) for t in range(nxt)],
+        [vmem] * (3 + nzt + nyt),
         "rows",
         1 << 18,
-    )(*cots, *z_in, *y_in, *edges)
+    )(*cots, *z_in, *y_in)
     x_in = [swap(v, gx=t) for t, v in enumerate(rows)]
     ue, ratio, row_values, row_kinds = kernel_call(
         prepare,
@@ -525,7 +521,7 @@
         functools.partial(interior, nyt, nzt),
         [array(*c.shape) for c in cots]
         + [array(FLOW, 2 * depth, length), array(HEAT, 2 * depth, length), array(2 * layers, length)],
-        [vmem] * (6 + 2 * nzt + nyt),
+        [vmem] * (6 + nzt + nyt + nyt * nzt),
         "interior",
         4 << 20,
         out_spaces=[hbm] * 3 + [vmem] * 3,

time: 14.4 us -> 13.5 us (0.938)
  the two profiles are of different devices: /device:TPU:0 before, /device:TPU:11 now
where the time goes in v5:
time: 13.5 us; the launch traced here: 13.3 us
  starting transfers between devices  6.92 us (51%)
  Pallas kernels  4.17 us (31%)
  waiting for transfers between devices  1.46 us (11%)
  between operations  0.75 us (6%)
    ppermute x7, starting transfers between devices, swap(): return lax.ppermute(value, AXES, pairs)  6.92 us
    ppermute x7, waiting for transfers between devices, swap(): return lax.ppermute(value, AXES, pairs)  1.46 us
    pallas_call x1, Pallas kernels, local(): kernel_call(functools.partial(interior, nyt, nzt), [array(*c.shape) for c...  1.36 us
    pallas_call x1, Pallas kernels, local(): kernel_call(functools.partial(pack_faces, nzt), [array((len(ZM) + 1) * wi...  0.95 us
    pallas_call x1, Pallas kernels, local(): kernel_call(prepare, [array(3, depth, width, length), array(depth, width,...  0.78 us
    pallas_call x1, Pallas kernels, local(): kernel_call(functools.partial(finish, nxt), [array(*c.shape) for c in cot...  0.76 us
  transfers between devices with their start and end apart: 7, of which 1 were waited for; matrix products, arithmetic and copies ran while one was open for 0% of the time, Pallas kernels for 19%

profile of v5, /device:TPU:11, one launch (start us, length us, event | category | flops | bytes accessed | tf_op | source)
XLA Modules:
  0.0 13.3 jit_solution(17515242848154544576)
XLA Ops:
  0.6 0.0 copy-start.2
  0.6 0.0 copy-start.1
  0.7 0.9 %faces.1.refs_0_ = f32[112,128]{1,0:T(8,128)S(1)} custom-call(f32[19,4,16,128]{3,2,1,0:T(8,128)} %cot_flow.7, f32[7,4,16,128]{3,2,1,0:T(8,128)} %cot_heat.7, f32[10,16,128]{2,1,0:T(8,128)} %cot_plate.7), custom_call_target="tpu_custom_call" | custom-call | bytes 1048576 | tf_op jit(solution)/shard_map/faces/pallas_call | solution.py:482
  1.6 1.3 %collective-permute-start = (f32[112,128]{1,0:T(8,128)S(1)}, f32[112,128]{1,0:T(8,128)S(1)}, u32[]{:S(2)}, u32[]{:S(2)}) collective-permute-start(f32[112,128]{1,0:T(8,128)S(1)} %faces.1.refs_0_), channel_id=1, source_target_pairs={{0,1},{1,0},{2,3},{3,2},{4,5},{5,4},{6,7},{7,6},{8,9},{9,8},{10,11... | collective-permute-start | bytes 172040 | tf_op jit(solution)/shard_map/ppermute | solution.py:79
  2.9 0.2 %columns.1 = (f32[16,128]{1,0:T(8,128)S(1)}, f32[16,128]{1,0:T(8,128)S(1)}, f32[48,128]{1,0:T(8,128)S(1)}, f32[48,128]{1,0:T(8,128)S(1)}) custom-call(f32[19,4,16,128]{3,2,1,0:T(8,128)S(1)} %copy-done, f32[7,4,16,128]{3,2,1,0:T(8,128)S(1)} %copy-done.1, f32[10,16,128]{2,1,0:T(8,128)S(1)} %copy-done.2, f32[112,128]{1,0:T(8,128)S(1)} %faces.1.refs_0_), custom_call_target="tpu_custom_call" | custom-call | bytes 262144 | tf_op jit(solution)/shard_map/columns/pallas_call | solution.py:491
  3.1 0.0 copy-start.3
  3.1 1.0 %collective-permute-start.1 = (f32[16,128]{1,0:T(8,128)S(1)}, f32[16,128]{1,0:T(8,128)S(1)}, u32[]{:S(2)}, u32[]{:S(2)}) collective-permute-start(f32[16,128]{1,0:T(8,128)S(1)} %get-tuple-element.19), channel_id=1, source_target_pairs={{0,2},{1,3},{2,0},{3,1},{4,6},{5,7},{6,4},{7,5},{8,10},{9,11},{10,... | collective-permute-start | bytes 24584 | tf_op jit(solution)/shard_map/ppermute | solution.py:79
  4.2 0.2 %collective-permute-start.2 = (f32[16,128]{1,0:T(8,128)S(1)}, f32[16,128]{1,0:T(8,128)S(1)}, u32[]{:S(2)}, u32[]{:S(2)}) collective-permute-start(f32[16,128]{1,0:T(8,128)S(1)} %get-tuple-element.20), channel_id=1, source_target_pairs={{0,6},{1,7},{2,4},{3,5},{4,2},{5,3},{6,0},{7,1},{8,14},{9,15},{10,... | collective-permute-start | bytes 24584 | tf_op jit(solution)/shard_map/ppermute | solution.py:79
  4.4 0.6 %collective-permute-start.3 = (f32[48,128]{1,0:T(8,128)S(1)}, f32[48,128]{1,0:T(8,128)S(1)}, u32[]{:S(2)}, u32[]{:S(2)}) collective-permute-start(f32[48,128]{1,0:T(8,128)S(1)} %get-tuple-element.27), channel_id=1, source_target_pairs={{0,3},{1,2},{2,1},{3,0},{4,7},{5,6},{6,5},{7,4},{8,11},{9,10},{10,... | collective-permute-start | bytes 73736 | tf_op jit(solution)/shard_map/ppermute | solution.py:79
  4.9 1.2 %collective-permute-start.4 = (f32[48,128]{1,0:T(8,128)S(1)}, f32[48,128]{1,0:T(8,128)S(1)}, u32[]{:S(2)}, u32[]{:S(2)}) collective-permute-start(f32[48,128]{1,0:T(8,128)S(1)} %get-tuple-element.28), channel_id=1, source_target_pairs={{0,6},{1,7},{2,5},{3,4},{4,3},{5,2},{6,0},{7,1},{8,14},{9,15},{10,... | collective-permute-start | bytes 73736 | tf_op jit(solution)/shard_map/ppermute | solution.py:79
  6.1 0.0 collective-permute-done.1.refs_1_
  6.1 1.4 %collective-permute-done.2.refs_2_ = f32[16,128]{1,0:T(8,128)S(1)} collective-permute-done((f32[16,128]{1,0:T(8,128)S(1)}, f32[16,128]{1,0:T(8,128)S(1)}, u32[]{:S(2)}, u32[]{:S(2)}) %collective-permute-start.2) | collective-permute-done | bytes 8224 | tf_op jit(solution)/shard_map/ppermute | solution.py:79
  7.6 0.0 collective-permute-done.refs_0_
  7.6 0.1 rows.1
  7.7 0.0 copy-start.7
  7.7 0.2 %collective-permute-start.5 = (f32[40,128]{1,0:T(8,128)S(1)}, f32[40,128]{1,0:T(8,128)S(1)}, u32[]{:S(2)}, u32[]{:S(2)}) collective-permute-start(f32[40,128]{1,0:T(8,128)S(1)} %get-tuple-element.21.refs_0_), channel_id=1, source_target_pairs={{0,8},{1,9},{2,10},{3,11},{4,12},{5,13},{6,14},{7,15},{8,0},{9,1},... | collective-permute-start | bytes 61448 | tf_op jit(solution)/shard_map/ppermute | solution.py:79
  7.9 2.4 %collective-permute-start.6 = (f32[40,128]{1,0:T(8,128)S(1)}, f32[40,128]{1,0:T(8,128)S(1)}, u32[]{:S(2)}, u32[]{:S(2)}) collective-permute-start(f32[40,128]{1,0:T(8,128)S(1)} %get-tuple-element.22.refs_1_), channel_id=1, source_target_pairs={{0,2},{1,3},{2,0},{3,1},{4,6},{5,7},{6,4},{7,5},{8,16},{9,17},{10,... | collective-permute-start | bytes 61448 | tf_op jit(solution)/shard_map/ppermute | solution.py:79
  10.4 0.8 %prepare.1 = (f32[3,4,16,128]{3,2,1,0:T(8,128)S(1)}, f32[4,16,128]{2,1,0:T(8,128)S(1)}, f32[4,8,128]{2,1,0:T(8,128)S(1)}, s32[8,128]{1,0:T(8,128)S(1)}) custom-call(f32[19,4,16,128]{3,2,1,0:T(8,128)S(1)} %copy-done.3, f32[7,4,16,128]{3,2,1,0:T(8,128)S(1)} %copy-done.4, s32[4,16,128]{2,1,0:T(8,128)S(1)} %copy-done.5, s32[16,128]{1,0:T(8,128)S(1)} %copy-done.6, ...), custom_call_target="tpu_custom_call" | custom-call | bytes 2097152 | tf_op jit(solution)/shard_map/prepare/pallas_call | solution.py:508
  11.2 0.0 collective-permute-done.3.refs_3_
  11.2 0.0 collective-permute-done.4.refs_4_
  11.2 1.4 %interior.1 = (f32[19,4,16,128]{3,2,1,0:T(8,128)}, f32[7,4,16,128]{3,2,1,0:T(8,128)}, f32[10,16,128]{2,1,0:T(8,128)}, f32[19,8,128]{2,1,0:T(8,128)S(1)}, f32[7,8...) custom-call(s32[4,16,128]{2,1,0:T(8,128)S(1)} %copy-done.5, f32[3,4,16,128]{3,2,1,0:T(8,128)S(1)} %get-tuple-element.25.ue_in, ...), custom_call_target="tpu_custom_call" | custom-call | bytes 4194304 | tf_op jit(solution)/shard_map/interior/pallas_call | solution.py:520
  12.6 0.0 collective-permute-done.5.refs_0_
  12.6 0.0 collective-permute-done.6.refs_1_
  12.6 0.8 %finish.1 = (f32[19,4,16,128]{3,2,1,0:T(8,128)}, f32[7,4,16,128]{3,2,1,0:T(8,128)}, f32[10,16,128]{2,1,0:T(8,128)}) custom-call(f32[4,8,128]{2,1,0:T(8,128)S(1)} %get-tuple-element.23.rows_in, s32[8,128]{1,0:T(8,128)S(1)} %get-tuple-element.24.kinds, ...), custom_call_target="tpu_custom_call", output_to_operand_aliasing={{0}: (7, {}), {1}: (8, {}), {2}: (9, {})} | custom-call | bytes 1048576 | tf_op jit(solution)/shard_map/finish/pallas_call | solution.py:531
  (12 shorter events, 0.0 us)
Async XLA Ops:
  0.6 2.3 %copy-start.2 = (f32[10,16,128]{2,1,0:T(8,128)S(1)}, f32[10,16,128]{2,1,0:T(8,128)}, u32[]{:S(2)}) copy-start(f32[10,16,128]{2,1,0:T(8,128)} %cot_plate.7) | copy-start | bytes 245764
  0.6 2.3 %copy-start.1 = (f32[7,4,16,128]{3,2,1,0:T(8,128)S(1)}, f32[7,4,16,128]{3,2,1,0:T(8,128)}, u32[]{:S(2)}) copy-start(f32[7,4,16,128]{3,2,1,0:T(8,128)} %cot_heat.7) | copy-start | bytes 688132
  0.7 2.3 %copy-start = (f32[19,4,16,128]{3,2,1,0:T(8,128)S(1)}, f32[19,4,16,128]{3,2,1,0:T(8,128)}, u32[]{:S(2)}) copy-start(f32[19,4,16,128]{3,2,1,0:T(8,128)} %cot_flow.7) | copy-start | bytes 1867780
  1.6 5.9 %collective-permute-start = (f32[112,128]{1,0:T(8,128)S(1)}, f32[112,128]{1,0:T(8,128)S(1)}, u32[]{:S(2)}, u32[]{:S(2)}) collective-permute-start(f32[112,128]{1,0:T(8,128)S(1)} %faces.1.refs_0_), channel_id=1, source_target_pairs={{0,1},{1,0},{2,3},{3,2},{4,5},{5,4},{6,7},{7,6},{8,9},{9,8},{10,11... | collective-permute-start | bytes 172040 | tf_op jit(solution)/shard_map/ppermute | solution.py:79
  3.1 7.2 %copy-start.3 = (f32[19,4,16,128]{3,2,1,0:T(8,128)S(1)}, f32[19,4,16,128]{3,2,1,0:T(8,128)}, u32[]{:S(2)}) copy-start(f32[19,4,16,128]{3,2,1,0:T(8,128)} %pop_flow.1) | copy-start | bytes 1867780
  3.1 3.0 %collective-permute-start.1 = (f32[16,128]{1,0:T(8,128)S(1)}, f32[16,128]{1,0:T(8,128)S(1)}, u32[]{:S(2)}, u32[]{:S(2)}) collective-permute-start(f32[16,128]{1,0:T(8,128)S(1)} %get-tuple-element.19), channel_id=1, source_target_pairs={{0,2},{1,3},{2,0},{3,1},{4,6},{5,7},{6,4},{7,5},{8,10},{9,11},{10,... | collective-permute-start | bytes 24584 | tf_op jit(solution)/shard_map/ppermute | solution.py:79
  4.2 3.4 %collective-permute-start.2 = (f32[16,128]{1,0:T(8,128)S(1)}, f32[16,128]{1,0:T(8,128)S(1)}, u32[]{:S(2)}, u32[]{:S(2)}) collective-permute-start(f32[16,128]{1,0:T(8,128)S(1)} %get-tuple-element.20), channel_id=1, source_target_pairs={{0,6},{1,7},{2,4},{3,5},{4,2},{5,3},{6,0},{7,1},{8,14},{9,15},{10,... | collective-permute-start | bytes 24584 | tf_op jit(solution)/shard_map/ppermute | solution.py:79
  4.4 6.8 %collective-permute-start.3 = (f32[48,128]{1,0:T(8,128)S(1)}, f32[48,128]{1,0:T(8,128)S(1)}, u32[]{:S(2)}, u32[]{:S(2)}) collective-permute-start(f32[48,128]{1,0:T(8,128)S(1)} %get-tuple-element.27), channel_id=1, source_target_pairs={{0,3},{1,2},{2,1},{3,0},{4,7},{5,6},{6,5},{7,4},{8,11},{9,10},{10,... | collective-permute-start | bytes 73736 | tf_op jit(solution)/shard_map/ppermute | solution.py:79
  4.9 5.4 %copy-start.4 = (f32[7,4,16,128]{3,2,1,0:T(8,128)S(1)}, f32[7,4,16,128]{3,2,1,0:T(8,128)}, u32[]{:S(2)}) copy-start(f32[7,4,16,128]{3,2,1,0:T(8,128)} %pop_heat.1) | copy-start | bytes 688132
  4.9 5.4 %copy-start.5 = (s32[4,16,128]{2,1,0:T(8,128)S(1)}, s32[4,16,128]{2,1,0:T(8,128)}, u32[]{:S(2)}) copy-start(s32[4,16,128]{2,1,0:T(8,128)} %flags.3) | copy-start | bytes 98308
  4.9 6.2 %collective-permute-start.4 = (f32[48,128]{1,0:T(8,128)S(1)}, f32[48,128]{1,0:T(8,128)S(1)}, u32[]{:S(2)}, u32[]{:S(2)}) collective-permute-start(f32[48,128]{1,0:T(8,128)S(1)} %get-tuple-element.28), channel_id=1, source_target_pairs={{0,6},{1,7},{2,5},{3,4},{4,3},{5,2},{6,0},{7,1},{8,14},{9,15},{10,... | collective-permute-start | bytes 73736 | tf_op jit(solution)/shard_map/ppermute | solution.py:79
  7.6 2.8 %copy-start.6 = (s32[16,128]{1,0:T(8,128)S(1)}, s32[16,128]{1,0:T(8,128)}, u32[]{:S(2)}) copy-start(s32[16,128]{1,0:T(8,128)} %nozzle.1) | copy-start | bytes 24580
  7.7 2.7 %copy-start.7 = (f32[3,64]{1,0:T(4,128)S(1)}, f32[3,64]{1,0:T(4,128)}, u32[]{:S(2)}) copy-start(f32[3,64]{1,0:T(4,128)} %jet_velocity.1) | copy-start | bytes 2308
  7.7 4.9 %collective-permute-start.5 = (f32[40,128]{1,0:T(8,128)S(1)}, f32[40,128]{1,0:T(8,128)S(1)}, u32[]{:S(2)}, u32[]{:S(2)}) collective-permute-start(f32[40,128]{1,0:T(8,128)S(1)} %get-tuple-element.21.refs_0_), channel_id=1, source_target_pairs={{0,8},{1,9},{2,10},{3,11},{4,12},{5,13},{6,14},{7,15},{8,0},{9,1},... | collective-permute-start | bytes 61448 | tf_op jit(solution)/shard_map/ppermute | solution.py:79
  7.9 4.6 %collective-permute-start.6 = (f32[40,128]{1,0:T(8,128)S(1)}, f32[40,128]{1,0:T(8,128)S(1)}, u32[]{:S(2)}, u32[]{:S(2)}) collective-permute-start(f32[40,128]{1,0:T(8,128)S(1)} %get-tuple-element.22.refs_1_), channel_id=1, source_target_pairs={{0,2},{1,3},{2,0},{3,1},{4,6},{5,7},{6,4},{7,5},{8,16},{9,17},{10,... | collective-permute-start | bytes 61448 | tf_op jit(solution)/shard_map/ppermute | solution.py:79

commit v6 on v5

--- a/solution.py
+++ b/solution.py
@@ -43,8 +43,7 @@
 COMPONENT = {"gx": 0, "gy": 1, "gz": 2}
 VMEM_LIMIT = 8 << 20
 YZ_ROWS = 48
-YPAD = (0, 0)
-XPAD = (0, 0)
+YPAD = (0, 8)
 
 
 def moving(component, sign):
@@ -245,11 +244,22 @@
 def prepare(pop_flow, pop_heat, flags, nozzle, jet_velocity, *refs):
     ue_out, ratio_out, rows_out, kinds_out = refs[-4:]
     depth, width = flags.shape[:2]
-    jets = [jnp.zeros(nozzle.shape, jnp.float32)] * 3
     which = nozzle[...]
-    for n in range(jet_velocity.shape[1]):
-        hit = which == n
-        jets = [jnp.where(hit, jet_velocity[c, n], jets[c]) for c in range(3)]
+    table = jet_velocity[...]
+    fill = jnp.zeros((3, which.shape[1] - table.shape[1]), jnp.float32)
+    table = jnp.concatenate([table, fill], axis=1)
+    jets = [
+        jnp.concatenate(
+            [
+                jnp.take_along_axis(
+                    jnp.broadcast_to(table[c : c + 1, :], (8, which.shape[1])), which[x : x + 8, :], axis=1
+                )
+                for x in range(0, width, 8)
+            ],
+            axis=0,
+        )
+        for c in range(3)
+    ]
     for z in range(depth):
         inlet = flags[z] == 2
         pops = [pop_flow[q, z] for q in range(FLOW)]
@@ -499,7 +509,7 @@
     yz_in = [swap(columns[nyt + ty * nzt + tz], gy=ty, gz=tz) for ty in range(nyt) for tz in range(nzt)]
     rows = kernel_call(
         functools.partial(pack_rows, nxt, nyt, nzt),
-        [array(side + XPAD[t], length) for t in range(nxt)],
+        [array(side, length)] * nxt,
         [vmem] * (3 + nzt + nyt),
         "rows",
         1 << 18,
@@ -513,7 +523,7 @@
             array(4, 2 * depth, length),
             jax.ShapeDtypeStruct((2 * depth, length), jnp.int32),
         ],
-        [vmem] * 4 + [pltpu.SMEM] + [vmem] * nxt,
+        [vmem] * (5 + nxt),
         "prepare",
         2 << 20,
     )(pop_flow, pop_heat, flags, nozzle_id, jet_velocity, *rows)

time: 13.5 us -> 13.4 us (level)
  the two profiles are of different devices: /device:TPU:11 before, /device:TPU:18 now
where the time goes in v6:
time: 13.4 us; the launch traced here: 13.2 us
  starting transfers between devices  6.61 us (49%)
  Pallas kernels  3.47 us (26%)
  waiting for transfers between devices  2.28 us (17%)
  between operations  0.77 us (6%)
    ppermute x7, starting transfers between devices, swap(): return lax.ppermute(value, AXES, pairs)  6.61 us
    ppermute x7, waiting for transfers between devices, swap(): return lax.ppermute(value, AXES, pairs)  2.28 us
    pallas_call x1, Pallas kernels, local(): kernel_call(functools.partial(interior, nyt, nzt), [array(*c.shape) for c...  1.35 us
    pallas_call x1, Pallas kernels, local(): kernel_call(functools.partial(pack_faces, nzt), [array((len(ZM) + 1) * wi...  0.95 us
    pallas_call x1, Pallas kernels, local(): kernel_call(functools.partial(finish, nxt), [array(*c.shape) for c in cot...  0.75 us
  transfers between devices with their start and end apart: 7, of which 2 were waited for; matrix products, arithmetic and copies ran while one was open for 0% of the time, Pallas kernels for 13%

profile of v6, /device:TPU:18, one launch (start us, length us, event | category | flops | bytes accessed | tf_op | source)
XLA Modules:
  0.0 13.2 jit_solution(2092438608318879056)
XLA Ops:
  0.7 0.9 %faces.1.refs_0_ = f32[112,128]{1,0:T(8,128)S(1)} custom-call(f32[19,4,16,128]{3,2,1,0:T(8,128)} %cot_flow.7, f32[7,4,16,128]{3,2,1,0:T(8,128)} %cot_heat.7, f32[10,16,128]{2,1,0:T(8,128)} %cot_plate.7), custom_call_target="tpu_custom_call" | custom-call | bytes 1048576 | tf_op jit(solution)/shard_map/faces/pallas_call | solution.py:492
  1.6 1.6 %collective-permute-start = (f32[112,128]{1,0:T(8,128)S(1)}, f32[112,128]{1,0:T(8,128)S(1)}, u32[]{:S(2)}, u32[]{:S(2)}) collective-permute-start(f32[112,128]{1,0:T(8,128)S(1)} %faces.1.refs_0_), channel_id=1, source_target_pairs={{0,1},{1,0},{2,3},{3,2},{4,5},{5,4},{6,7},{7,6},{8,9},{9,8},{10,11... | collective-permute-start | bytes 172040 | tf_op jit(solution)/shard_map/ppermute | solution.py:78
  3.2 0.0 copy-done.1
  3.2 0.2 %columns.1 = (f32[16,128]{1,0:T(8,128)S(1)}, f32[24,128]{1,0:T(8,128)S(1)}, f32[48,128]{1,0:T(8,128)S(1)}, f32[48,128]{1,0:T(8,128)S(1)}) custom-call(f32[19,4,16,128]{3,2,1,0:T(8,128)S(1)} %copy-done, f32[7,4,16,128]{3,2,1,0:T(8,128)S(1)} %copy-done.1, f32[10,16,128]{2,1,0:T(8,128)S(1)} %copy-done.2, f32[112,128]{1,0:T(8,128)S(1)} %faces.1.refs_0_), custom_call_target="tpu_custom_call" | custom-call | bytes 262144 | tf_op jit(solution)/shard_map/columns/pallas_call | solution.py:501
  3.4 0.0 copy-start.3
  3.4 0.1 collective-permute-start.2
  3.5 0.6 %collective-permute-start.1 = (f32[16,128]{1,0:T(8,128)S(1)}, f32[16,128]{1,0:T(8,128)S(1)}, u32[]{:S(2)}, u32[]{:S(2)}) collective-permute-start(f32[16,128]{1,0:T(8,128)S(1)} %get-tuple-element.19), channel_id=1, source_target_pairs={{0,2},{1,3},{2,0},{3,1},{4,6},{5,7},{6,4},{7,5},{8,10},{9,11},{10,... | collective-permute-start | bytes 24584 | tf_op jit(solution)/shard_map/ppermute | solution.py:78
  4.1 0.1 collective-permute-start.3
  4.3 2.6 %collective-permute-start.4 = (f32[48,128]{1,0:T(8,128)S(1)}, f32[48,128]{1,0:T(8,128)S(1)}, u32[]{:S(2)}, u32[]{:S(2)}) collective-permute-start(f32[48,128]{1,0:T(8,128)S(1)} %get-tuple-element.28), channel_id=1, source_target_pairs={{0,6},{1,7},{2,5},{3,4},{4,3},{5,2},{6,0},{7,1},{8,14},{9,15},{10,... | collective-permute-start | bytes 73736 | tf_op jit(solution)/shard_map/ppermute | solution.py:78
  6.8 0.0 collective-permute-done.1.refs_1_
  6.8 0.0 collective-permute-done.2.refs_2_
  6.8 0.0 collective-permute-done.refs_0_
  6.8 0.0 copy-start.6
  6.8 0.1 rows.1
  7.0 0.0 copy-start.7
  7.0 1.6 %collective-permute-start.5 = (f32[40,128]{1,0:T(8,128)S(1)}, f32[40,128]{1,0:T(8,128)S(1)}, u32[]{:S(2)}, u32[]{:S(2)}) collective-permute-start(f32[40,128]{1,0:T(8,128)S(1)} %get-tuple-element.21.refs_0_), channel_id=1, source_target_pairs={{0,8},{1,9},{2,10},{3,11},{4,12},{5,13},{6,14},{7,15},{8,0},{9,1},... | collective-permute-start | bytes 61448 | tf_op jit(solution)/shard_map/ppermute | solution.py:78
  8.6 0.0 collective-permute-start.6
  8.7 0.1 prepare.1
  8.8 0.0 collective-permute-done.3.refs_3_
  8.8 0.0 collective-permute-done.4.refs_4_
  8.8 1.4 %interior.1 = (f32[19,4,16,128]{3,2,1,0:T(8,128)}, f32[7,4,16,128]{3,2,1,0:T(8,128)}, f32[10,16,128]{2,1,0:T(8,128)}, f32[19,8,128]{2,1,0:T(8,128)S(1)}, f32[7,8...) custom-call(s32[4,16,128]{2,1,0:T(8,128)S(1)} %copy-done.5, f32[3,4,16,128]{3,2,1,0:T(8,128)S(1)} %get-tuple-element.25.ue_in, ...), custom_call_target="tpu_custom_call" | custom-call | bytes 4194304 | tf_op jit(solution)/shard_map/interior/pallas_call | solution.py:530
  10.1 0.7 %collective-permute-done.5.refs_0_ = f32[40,128]{1,0:T(8,128)S(1)} collective-permute-done((f32[40,128]{1,0:T(8,128)S(1)}, f32[40,128]{1,0:T(8,128)S(1)}, u32[]{:S(2)}, u32[]{:S(2)}) %collective-permute-start.5) | collective-permute-done | bytes 20512 | tf_op jit(solution)/shard_map/ppermute | solution.py:78
  10.8 1.6 %collective-permute-done.6.refs_1_ = f32[40,128]{1,0:T(8,128)S(1)} collective-permute-done((f32[40,128]{1,0:T(8,128)S(1)}, f32[40,128]{1,0:T(8,128)S(1)}, u32[]{:S(2)}, u32[]{:S(2)}) %collective-permute-start.6) | collective-permute-done | bytes 20512 | tf_op jit(solution)/shard_map/ppermute | solution.py:78
  12.4 0.7 %finish.1 = (f32[19,4,16,128]{3,2,1,0:T(8,128)}, f32[7,4,16,128]{3,2,1,0:T(8,128)}, f32[10,16,128]{2,1,0:T(8,128)}) custom-call(f32[4,8,128]{2,1,0:T(8,128)S(1)} %get-tuple-element.23.rows_in, s32[8,128]{1,0:T(8,128)S(1)} %get-tuple-element.24.kinds, ...), custom_call_target="tpu_custom_call", output_to_operand_aliasing={{0}: (7, {}), {1}: (8, {}), {2}: (9, {})} | custom-call | bytes 1048576 | tf_op jit(solution)/shard_map/finish/pallas_call | solution.py:541
  (12 shorter events, 0.0 us)
Async XLA Ops:
  0.6 2.6 %copy-start.2 = (f32[10,16,128]{2,1,0:T(8,128)S(1)}, f32[10,16,128]{2,1,0:T(8,128)}, u32[]{:S(2)}) copy-start(f32[10,16,128]{2,1,0:T(8,128)} %cot_plate.7) | copy-start | bytes 245764
  0.6 2.6 %copy-start.1 = (f32[7,4,16,128]{3,2,1,0:T(8,128)S(1)}, f32[7,4,16,128]{3,2,1,0:T(8,128)}, u32[]{:S(2)}) copy-start(f32[7,4,16,128]{3,2,1,0:T(8,128)} %cot_heat.7) | copy-start | bytes 688132
  0.7 2.6 %copy-start = (f32[19,4,16,128]{3,2,1,0:T(8,128)S(1)}, f32[19,4,16,128]{3,2,1,0:T(8,128)}, u32[]{:S(2)}) copy-start(f32[19,4,16,128]{3,2,1,0:T(8,128)} %cot_flow.7) | copy-start | bytes 1867780
  1.6 5.2 %collective-permute-start = (f32[112,128]{1,0:T(8,128)S(1)}, f32[112,128]{1,0:T(8,128)S(1)}, u32[]{:S(2)}, u32[]{:S(2)}) collective-permute-start(f32[112,128]{1,0:T(8,128)S(1)} %faces.1.refs_0_), channel_id=1, source_target_pairs={{0,1},{1,0},{2,3},{3,2},{4,5},{5,4},{6,7},{7,6},{8,9},{9,8},{10,11... | collective-permute-start | bytes 172040 | tf_op jit(solution)/shard_map/ppermute | solution.py:78
  3.4 5.2 %copy-start.3 = (f32[19,4,16,128]{3,2,1,0:T(8,128)S(1)}, f32[19,4,16,128]{3,2,1,0:T(8,128)}, u32[]{:S(2)}) copy-start(f32[19,4,16,128]{3,2,1,0:T(8,128)} %pop_flow.1) | copy-start | bytes 1867780
  3.4 3.4 %collective-permute-start.2 = (f32[24,128]{1,0:T(8,128)S(1)}, f32[24,128]{1,0:T(8,128)S(1)}, u32[]{:S(2)}, u32[]{:S(2)}) collective-permute-start(f32[24,128]{1,0:T(8,128)S(1)} %get-tuple-element.20), channel_id=1, source_target_pairs={{0,6},{1,7},{2,4},{3,5},{4,2},{5,3},{6,0},{7,1},{8,14},{9,15},{10,... | collective-permute-start | bytes 36872 | tf_op jit(solution)/shard_map/ppermute | solution.py:78
  3.5 3.3 %collective-permute-start.1 = (f32[16,128]{1,0:T(8,128)S(1)}, f32[16,128]{1,0:T(8,128)S(1)}, u32[]{:S(2)}, u32[]{:S(2)}) collective-permute-start(f32[16,128]{1,0:T(8,128)S(1)} %get-tuple-element.19), channel_id=1, source_target_pairs={{0,2},{1,3},{2,0},{3,1},{4,6},{5,7},{6,4},{7,5},{8,10},{9,11},{10,... | collective-permute-start | bytes 24584 | tf_op jit(solution)/shard_map/ppermute | solution.py:78
  4.1 4.6 %collective-permute-start.3 = (f32[48,128]{1,0:T(8,128)S(1)}, f32[48,128]{1,0:T(8,128)S(1)}, u32[]{:S(2)}, u32[]{:S(2)}) collective-permute-start(f32[48,128]{1,0:T(8,128)S(1)} %get-tuple-element.27), channel_id=1, source_target_pairs={{0,3},{1,2},{2,1},{3,0},{4,7},{5,6},{6,5},{7,4},{8,11},{9,10},{10,... | collective-permute-start | bytes 73736 | tf_op jit(solution)/shard_map/ppermute | solution.py:78
  4.3 4.4 %copy-start.4 = (f32[7,4,16,128]{3,2,1,0:T(8,128)S(1)}, f32[7,4,16,128]{3,2,1,0:T(8,128)}, u32[]{:S(2)}) copy-start(f32[7,4,16,128]{3,2,1,0:T(8,128)} %pop_heat.1) | copy-start | bytes 688132
  4.3 4.4 %copy-start.5 = (s32[4,16,128]{2,1,0:T(8,128)S(1)}, s32[4,16,128]{2,1,0:T(8,128)}, u32[]{:S(2)}) copy-start(s32[4,16,128]{2,1,0:T(8,128)} %flags.3) | copy-start | bytes 98308
  4.3 4.5 %collective-permute-start.4 = (f32[48,128]{1,0:T(8,128)S(1)}, f32[48,128]{1,0:T(8,128)S(1)}, u32[]{:S(2)}, u32[]{:S(2)}) collective-permute-start(f32[48,128]{1,0:T(8,128)S(1)} %get-tuple-element.28), channel_id=1, source_target_pairs={{0,6},{1,7},{2,5},{3,4},{4,3},{5,2},{6,0},{7,1},{8,14},{9,15},{10,... | collective-permute-start | bytes 73736 | tf_op jit(solution)/shard_map/ppermute | solution.py:78
  6.8 1.8 %copy-start.6 = (s32[16,128]{1,0:T(8,128)S(1)}, s32[16,128]{1,0:T(8,128)}, u32[]{:S(2)}) copy-start(s32[16,128]{1,0:T(8,128)} %nozzle.1) | copy-start | bytes 24580
  7.0 1.7 %copy-start.7 = (f32[3,64]{1,0:T(4,128)S(1)}, f32[3,64]{1,0:T(4,128)}, u32[]{:S(2)}) copy-start(f32[3,64]{1,0:T(4,128)} %jet_velocity.1) | copy-start | bytes 2308
  7.0 3.8 %collective-permute-start.5 = (f32[40,128]{1,0:T(8,128)S(1)}, f32[40,128]{1,0:T(8,128)S(1)}, u32[]{:S(2)}, u32[]{:S(2)}) collective-permute-start(f32[40,128]{1,0:T(8,128)S(1)} %get-tuple-element.21.refs_0_), channel_id=1, source_target_pairs={{0,8},{1,9},{2,10},{3,11},{4,12},{5,13},{6,14},{7,15},{8,0},{9,1},... | collective-permute-start | bytes 61448 | tf_op jit(solution)/shard_map/ppermute | solution.py:78
  8.6 3.8 %collective-permute-start.6 = (f32[40,128]{1,0:T(8,128)S(1)}, f32[40,128]{1,0:T(8,128)S(1)}, u32[]{:S(2)}, u32[]{:S(2)}) collective-permute-start(f32[40,128]{1,0:T(8,128)S(1)} %get-tuple-element.22.refs_1_), channel_id=1, source_target_pairs={{0,2},{1,3},{2,0},{3,1},{4,6},{5,7},{6,4},{7,5},{8,16},{9,17},{10,... | collective-permute-start | bytes 61448 | tf_op jit(solution)/shard_map/ppermute | solution.py:78

commit v7 on v6

--- a/solution.py
+++ b/solution.py
@@ -43,7 +43,7 @@
 COMPONENT = {"gx": 0, "gy": 1, "gz": 2}
 VMEM_LIMIT = 8 << 20
 YZ_ROWS = 48
-YPAD = (0, 8)
+YPAD = (0, 0)
 
 
 def moving(component, sign):
@@ -55,8 +55,17 @@
 ZP, ZM = moving(2, 1), moving(2, -1)
 
 
-def rounds(size):
-    return 1 if size == 2 else 2
+def rounds(axis):
+    if lax.axis_size(axis) == 2:
+        return 1
+    return 3 if axis == "gx" else 2
+
+
+def partner(axis, i, turn):
+    period = 3 if axis == "gx" else 2
+    if i % period == turn:
+        return i + 1
+    return i - 1 if (i - 1) % period == turn else -1
 
 
 def swap(value, **turns):
@@ -71,7 +80,7 @@
                 for axis, turn in turns.items():
                     at = AXES.index(axis)
                     i = here[at]
-                    there[at] = i ^ 1 if turn == 0 else (i + 1 if i % 2 else i - 1)
+                    there[at] = partner(axis, i, turn)
                 if not all(0 <= t < n for t, n in zip(there, sizes)):
                     there = [a, sizes[1] - 1 - b if "gy" in turns else b ^ 1, c]
                 pairs.append((flat(here), flat(there)))
@@ -80,21 +89,24 @@
 
 def place(axis):
     i = lax.axis_index(axis)
-    return lax.rem(i, 2) == 0, i < lax.axis_size(axis) - 1, i > 0
+    period = 3 if axis == "gx" else 2
+    return lax.rem(i, period), lax.rem(i + period - 1, period), i < lax.axis_size(axis) - 1, i > 0
 
 
 def outgoing(axis, turn, to_higher, to_lower):
-    even, _, _ = place(axis)
-    return jnp.where(even, to_higher, to_lower) if turn == 0 else jnp.where(even, to_lower, to_higher)
+    return jnp.where(place(axis)[0] == turn, to_higher, to_lower)
 
 
 def incoming(axis, turns):
-    even, higher, lower = place(axis)
-    first, last = turns[0], turns[-1]
-    zero = jnp.zeros_like(first)
-    above = jnp.where(higher, jnp.where(even, first, last), zero)
-    below = jnp.where(lower, jnp.where(even, last, first), zero)
-    return above, below
+    first, second, higher, lower = place(axis)
+
+    def pick(turn, there):
+        value = turns[0]
+        for t in range(1, len(turns)):
+            value = jnp.where(turn == t, turns[t], value)
+        return jnp.where(there, value, jnp.zeros_like(value))
+
+    return pick(first, higher), pick(second, lower)
 
 
 def slab(cot_flow, cot_heat, k, z):
@@ -139,10 +151,9 @@
     outs, sems = refs[:nzt], refs[nzt]
     depth, width = cot_flow.shape[1], cot_flow.shape[2]
     layers = cot_plate.shape[0]
-    even, _, _ = place("gz")
     copies = []
     for turn in range(nzt):
-        up = even if turn == 0 else jnp.logical_not(even)
+        up = place("gz")[0] == turn
         z = jnp.where(up, depth - 1, 0)
         sources = []
         for hi, lo in zip(ZM, ZP):
@@ -480,7 +491,7 @@
 
 
 def local(pop_flow, pop_heat, flags, nozzle_id, jet_velocity, cot_flow, cot_heat, cot_plate):
-    nxt, nyt, nzt = (rounds(lax.axis_size(a)) for a in AXES)
+    nxt, nyt, nzt = (rounds(a) for a in AXES)
     _, depth, width, length = cot_flow.shape
     layers = cot_plate.shape[0]
     f32 = jnp.float32

time: 13.4 us -> 13.2 us (0.985)
  the two profiles are of different devices: /device:TPU:18 before, /device:TPU:1 now
where the time goes in v7:
time: 13.2 us; the launch traced here: 13 us
  starting transfers between devices  7.92 us (60%)
  Pallas kernels  3.49 us (26%)
  waiting for transfers between devices  0.84 us (6%)
  between operations  0.75 us (6%)
    ppermute x8, starting transfers between devices, swap(): return lax.ppermute(value, AXES, pairs)  7.92 us
    pallas_call x1, Pallas kernels, local(): kernel_call(functools.partial(interior, nyt, nzt), [array(*c.shape) for c...  1.35 us
    pallas_call x1, Pallas kernels, local(): kernel_call(functools.partial(pack_faces, nzt), [array((len(ZM) + 1) * wi...  0.95 us
    ppermute x8, waiting for transfers between devices, swap(): return lax.ppermute(value, AXES, pairs)  0.84 us
    pallas_call x1, Pallas kernels, local(): kernel_call(functools.partial(finish, nxt), [array(*c.shape) for c in cot...  0.76 us
  transfers between devices with their start and end apart: 8, of which 2 were waited for; matrix products, arithmetic and copies ran while one was open for 0% of the time, Pallas kernels for 14%

profile of v7, /device:TPU:1, one launch (start us, length us, event | category | flops | bytes accessed | tf_op | source)
XLA Modules:
  0.0 13.0 jit_solution(11676327461677697379)
XLA Ops:
  0.7 0.9 %faces.1.refs_0_ = f32[112,128]{1,0:T(8,128)S(1)} custom-call(f32[19,4,16,128]{3,2,1,0:T(8,128)} %cot_flow.7, f32[7,4,16,128]{3,2,1,0:T(8,128)} %cot_heat.7, f32[10,16,128]{2,1,0:T(8,128)} %cot_plate.7), custom_call_target="tpu_custom_call" | custom-call | bytes 1048576 | tf_op jit(solution)/shard_map/faces/pallas_call | solution.py:503
  1.6 2.1 %collective-permute-start = (f32[112,128]{1,0:T(8,128)S(1)}, f32[112,128]{1,0:T(8,128)S(1)}, u32[]{:S(2)}, u32[]{:S(2)}) collective-permute-start(f32[112,128]{1,0:T(8,128)S(1)} %faces.1.refs_0_), channel_id=1, source_target_pairs={{0,1},{1,0},{2,3},{3,2},{4,5},{5,4},{6,7},{7,6},{8,9},{9,8},{10,11... | collective-permute-start | bytes 172040 | tf_op jit(solution)/shard_map/ppermute | solution.py:87
  3.8 0.2 %columns.1 = (f32[16,128]{1,0:T(8,128)S(1)}, f32[16,128]{1,0:T(8,128)S(1)}, f32[48,128]{1,0:T(8,128)S(1)}, f32[48,128]{1,0:T(8,128)S(1)}) custom-call(f32[19,4,16,128]{3,2,1,0:T(8,128)S(1)} %copy-done, f32[7,4,16,128]{3,2,1,0:T(8,128)S(1)} %copy-done.1, f32[10,16,128]{2,1,0:T(8,128)S(1)} %copy-done.2, f32[112,128]{1,0:T(8,128)S(1)} %faces.1.refs_0_), custom_call_target="tpu_custom_call" | custom-call | bytes 262144 | tf_op jit(solution)/shard_map/columns/pallas_call | solution.py:512
  4.0 0.0 copy-start.3
  4.0 1.0 %collective-permute-start.1 = (f32[16,128]{1,0:T(8,128)S(1)}, f32[16,128]{1,0:T(8,128)S(1)}, u32[]{:S(2)}, u32[]{:S(2)}) collective-permute-start(f32[16,128]{1,0:T(8,128)S(1)} %get-tuple-element.20), channel_id=1, source_target_pairs={{0,2},{1,3},{2,0},{3,1},{4,6},{5,7},{6,4},{7,5},{8,10},{9,11},{10,... | collective-permute-start | bytes 24584 | tf_op jit(solution)/shard_map/ppermute | solution.py:87
  5.0 1.2 %collective-permute-start.2 = (f32[16,128]{1,0:T(8,128)S(1)}, f32[16,128]{1,0:T(8,128)S(1)}, u32[]{:S(2)}, u32[]{:S(2)}) collective-permute-start(f32[16,128]{1,0:T(8,128)S(1)} %get-tuple-element.21), channel_id=1, source_target_pairs={{0,6},{1,7},{2,4},{3,5},{4,2},{5,3},{6,0},{7,1},{8,14},{9,15},{10,... | collective-permute-start | bytes 24584 | tf_op jit(solution)/shard_map/ppermute | solution.py:87
  6.2 0.6 %collective-permute-start.3 = (f32[48,128]{1,0:T(8,128)S(1)}, f32[48,128]{1,0:T(8,128)S(1)}, u32[]{:S(2)}, u32[]{:S(2)}) collective-permute-start(f32[48,128]{1,0:T(8,128)S(1)} %get-tuple-element.29), channel_id=1, source_target_pairs={{0,3},{1,2},{2,1},{3,0},{4,7},{5,6},{6,5},{7,4},{8,11},{9,10},{10,... | collective-permute-start | bytes 73736 | tf_op jit(solution)/shard_map/ppermute | solution.py:87
  6.7 1.2 %collective-permute-start.4 = (f32[48,128]{1,0:T(8,128)S(1)}, f32[48,128]{1,0:T(8,128)S(1)}, u32[]{:S(2)}, u32[]{:S(2)}) collective-permute-start(f32[48,128]{1,0:T(8,128)S(1)} %get-tuple-element.30), channel_id=1, source_target_pairs={{0,6},{1,7},{2,5},{3,4},{4,3},{5,2},{6,0},{7,1},{8,14},{9,15},{10,... | collective-permute-start | bytes 73736 | tf_op jit(solution)/shard_map/ppermute | solution.py:87
  7.9 0.0 collective-permute-done.1.refs_1_
  7.9 0.2 %collective-permute-done.2.refs_2_ = f32[16,128]{1,0:T(8,128)S(1)} collective-permute-done((f32[16,128]{1,0:T(8,128)S(1)}, f32[16,128]{1,0:T(8,128)S(1)}, u32[]{:S(2)}, u32[]{:S(2)}) %collective-permute-start.2) | collective-permute-done | bytes 8224 | tf_op jit(solution)/shard_map/ppermute | solution.py:87
  8.1 0.0 collective-permute-done.refs_0_
  8.1 0.1 %rows.1 = (f32[40,128]{1,0:T(8,128)S(1)}, f32[40,128]{1,0:T(8,128)S(1)}, f32[40,128]{1,0:T(8,128)S(1)}) custom-call(f32[19,4,16,128]{3,2,1,0:T(8,128)S(1)} %copy-done, f32[7,4,16,128]{3,2,1,0:T(8,128)S(1)} %copy-done.1, f32[10,16,128]{2,1,0:T(8,128)S(1)} %copy-done.2, f32[112,128]{1,0:T(8,128)S(1)} %collective-permute-done.refs_0_, ...), custom_call_target="tpu_custom_call" | custom-call | bytes 262144 | tf_op jit(solution)/shard_map/rows/pallas_call | solution.py:521
  8.2 0.0 copy-start.7
  8.2 1.4 %collective-permute-start.5 = (f32[40,128]{1,0:T(8,128)S(1)}, f32[40,128]{1,0:T(8,128)S(1)}, u32[]{:S(2)}, u32[]{:S(2)}) collective-permute-start(f32[40,128]{1,0:T(8,128)S(1)} %get-tuple-element.22.refs_0_), channel_id=1, source_target_pairs={{0,8},{1,9},{2,10},{3,11},{4,12},{5,13},{6,14},{7,15},{8,0},{9,1},... | collective-permute-start | bytes 61448 | tf_op jit(solution)/shard_map/ppermute | solution.py:87
  9.6 0.3 %collective-permute-start.6 = (f32[40,128]{1,0:T(8,128)S(1)}, f32[40,128]{1,0:T(8,128)S(1)}, u32[]{:S(2)}, u32[]{:S(2)}) collective-permute-start(f32[40,128]{1,0:T(8,128)S(1)} %get-tuple-element.23.refs_1_), channel_id=1, source_target_pairs={{0,2},{1,3},{2,0},{3,1},{4,6},{5,7},{6,4},{7,5},{8,16},{9,17},{10,... | collective-permute-start | bytes 61448 | tf_op jit(solution)/shard_map/ppermute | solution.py:87
  10.0 0.2 %collective-permute-start.7 = (f32[40,128]{1,0:T(8,128)S(1)}, f32[40,128]{1,0:T(8,128)S(1)}, u32[]{:S(2)}, u32[]{:S(2)}) collective-permute-start(f32[40,128]{1,0:T(8,128)S(1)} %get-tuple-element.24.refs_2_), channel_id=1, source_target_pairs={{0,2},{1,3},{2,0},{3,1},{4,6},{5,7},{6,4},{7,5},{8,10},{9,11},{10,... | collective-permute-start | bytes 61448 | tf_op jit(solution)/shard_map/ppermute | solution.py:87
  10.1 0.1 prepare.1
  10.2 0.0 collective-permute-done.3.refs_3_
  10.3 0.6 %collective-permute-done.4.refs_4_ = f32[48,128]{1,0:T(8,128)S(1)} collective-permute-done((f32[48,128]{1,0:T(8,128)S(1)}, f32[48,128]{1,0:T(8,128)S(1)}, u32[]{:S(2)}, u32[]{:S(2)}) %collective-permute-start.4) | collective-permute-done | bytes 24608 | tf_op jit(solution)/shard_map/ppermute | solution.py:87
  10.9 1.3 %interior.1 = (f32[19,4,16,128]{3,2,1,0:T(8,128)}, f32[7,4,16,128]{3,2,1,0:T(8,128)}, f32[10,16,128]{2,1,0:T(8,128)}, f32[19,8,128]{2,1,0:T(8,128)S(1)}, f32[7,8...) custom-call(s32[4,16,128]{2,1,0:T(8,128)S(1)} %copy-done.5, f32[3,4,16,128]{3,2,1,0:T(8,128)S(1)} %get-tuple-element.27.ue_in, ...), custom_call_target="tpu_custom_call" | custom-call | bytes 4194304 | tf_op jit(solution)/shard_map/interior/pallas_call | solution.py:541
  12.2 0.0 collective-permute-done.5.refs_0_
  12.3 0.0 collective-permute-done.6.refs_1_
  12.3 0.0 collective-permute-done.7.refs_2_
  12.3 0.8 %finish.1 = (f32[19,4,16,128]{3,2,1,0:T(8,128)}, f32[7,4,16,128]{3,2,1,0:T(8,128)}, f32[10,16,128]{2,1,0:T(8,128)}) custom-call(f32[4,8,128]{2,1,0:T(8,128)S(1)} %get-tuple-element.25.rows_in, s32[8,128]{1,0:T(8,128)S(1)} %get-tuple-element.26.kinds, ...), custom_call_target="tpu_custom_call", output_to_operand_aliasing={{0}: (8, {}), {1}: (9, {}), {2}: (10, {})} | custom-call | bytes 1048576 | tf_op jit(solution)/shard_map/finish/pallas_call | solution.py:552
  (14 shorter events, 0.0 us)
Async XLA Ops:
  0.6 3.1 %copy-start.2 = (f32[10,16,128]{2,1,0:T(8,128)S(1)}, f32[10,16,128]{2,1,0:T(8,128)}, u32[]{:S(2)}) copy-start(f32[10,16,128]{2,1,0:T(8,128)} %cot_plate.7) | copy-start | bytes 245764
  0.6 3.1 %copy-start.1 = (f32[7,4,16,128]{3,2,1,0:T(8,128)S(1)}, f32[7,4,16,128]{3,2,1,0:T(8,128)}, u32[]{:S(2)}) copy-start(f32[7,4,16,128]{3,2,1,0:T(8,128)} %cot_heat.7) | copy-start | bytes 688132
  0.7 3.1 %copy-start = (f32[19,4,16,128]{3,2,1,0:T(8,128)S(1)}, f32[19,4,16,128]{3,2,1,0:T(8,128)}, u32[]{:S(2)}) copy-start(f32[19,4,16,128]{3,2,1,0:T(8,128)} %cot_flow.7) | copy-start | bytes 1867780
  1.6 6.5 %collective-permute-start = (f32[112,128]{1,0:T(8,128)S(1)}, f32[112,128]{1,0:T(8,128)S(1)}, u32[]{:S(2)}, u32[]{:S(2)}) collective-permute-start(f32[112,128]{1,0:T(8,128)S(1)} %faces.1.refs_0_), channel_id=1, source_target_pairs={{0,1},{1,0},{2,3},{3,2},{4,5},{5,4},{6,7},{7,6},{8,9},{9,8},{10,11... | collective-permute-start | bytes 172040 | tf_op jit(solution)/shard_map/ppermute | solution.py:87
  4.0 6.2 %copy-start.3 = (f32[19,4,16,128]{3,2,1,0:T(8,128)S(1)}, f32[19,4,16,128]{3,2,1,0:T(8,128)}, u32[]{:S(2)}) copy-start(f32[19,4,16,128]{3,2,1,0:T(8,128)} %pop_flow.1) | copy-start | bytes 1867780
  4.0 3.9 %collective-permute-start.1 = (f32[16,128]{1,0:T(8,128)S(1)}, f32[16,128]{1,0:T(8,128)S(1)}, u32[]{:S(2)}, u32[]{:S(2)}) collective-permute-start(f32[16,128]{1,0:T(8,128)S(1)} %get-tuple-element.20), channel_id=1, source_target_pairs={{0,2},{1,3},{2,0},{3,1},{4,6},{5,7},{6,4},{7,5},{8,10},{9,11},{10,... | collective-permute-start | bytes 24584 | tf_op jit(solution)/shard_map/ppermute | solution.py:87
  5.0 3.1 %collective-permute-start.2 = (f32[16,128]{1,0:T(8,128)S(1)}, f32[16,128]{1,0:T(8,128)S(1)}, u32[]{:S(2)}, u32[]{:S(2)}) collective-permute-start(f32[16,128]{1,0:T(8,128)S(1)} %get-tuple-element.21), channel_id=1, source_target_pairs={{0,6},{1,7},{2,4},{3,5},{4,2},{5,3},{6,0},{7,1},{8,14},{9,15},{10,... | collective-permute-start | bytes 24584 | tf_op jit(solution)/shard_map/ppermute | solution.py:87
  6.2 4.1 %collective-permute-start.3 = (f32[48,128]{1,0:T(8,128)S(1)}, f32[48,128]{1,0:T(8,128)S(1)}, u32[]{:S(2)}, u32[]{:S(2)}) collective-permute-start(f32[48,128]{1,0:T(8,128)S(1)} %get-tuple-element.29), channel_id=1, source_target_pairs={{0,3},{1,2},{2,1},{3,0},{4,7},{5,6},{6,5},{7,4},{8,11},{9,10},{10,... | collective-permute-start | bytes 73736 | tf_op jit(solution)/shard_map/ppermute | solution.py:87
  6.7 3.4 %copy-start.4 = (f32[7,4,16,128]{3,2,1,0:T(8,128)S(1)}, f32[7,4,16,128]{3,2,1,0:T(8,128)}, u32[]{:S(2)}) copy-start(f32[7,4,16,128]{3,2,1,0:T(8,128)} %pop_heat.1) | copy-start | bytes 688132
  6.7 3.4 %copy-start.5 = (s32[4,16,128]{2,1,0:T(8,128)S(1)}, s32[4,16,128]{2,1,0:T(8,128)}, u32[]{:S(2)}) copy-start(s32[4,16,128]{2,1,0:T(8,128)} %flags.3) | copy-start | bytes 98308
  6.7 4.2 %collective-permute-start.4 = (f32[48,128]{1,0:T(8,128)S(1)}, f32[48,128]{1,0:T(8,128)S(1)}, u32[]{:S(2)}, u32[]{:S(2)}) collective-permute-start(f32[48,128]{1,0:T(8,128)S(1)} %get-tuple-element.30), channel_id=1, source_target_pairs={{0,6},{1,7},{2,5},{3,4},{4,3},{5,2},{6,0},{7,1},{8,14},{9,15},{10,... | collective-permute-start | bytes 73736 | tf_op jit(solution)/shard_map/ppermute | solution.py:87
  8.1 2.0 %copy-start.6 = (s32[16,128]{1,0:T(8,128)S(1)}, s32[16,128]{1,0:T(8,128)}, u32[]{:S(2)}) copy-start(s32[16,128]{1,0:T(8,128)} %nozzle.1) | copy-start | bytes 24580
  8.2 1.9 %copy-start.7 = (f32[3,64]{1,0:T(4,128)S(1)}, f32[3,64]{1,0:T(4,128)}, u32[]{:S(2)}) copy-start(f32[3,64]{1,0:T(4,128)} %jet_velocity.1) | copy-start | bytes 2308
  8.2 4.0 %collective-permute-start.5 = (f32[40,128]{1,0:T(8,128)S(1)}, f32[40,128]{1,0:T(8,128)S(1)}, u32[]{:S(2)}, u32[]{:S(2)}) collective-permute-start(f32[40,128]{1,0:T(8,128)S(1)} %get-tuple-element.22.refs_0_), channel_id=1, source_target_pairs={{0,8},{1,9},{2,10},{3,11},{4,12},{5,13},{6,14},{7,15},{8,0},{9,1},... | collective-permute-start | bytes 61448 | tf_op jit(solution)/shard_map/ppermute | solution.py:87
  9.6 2.6 %collective-permute-start.6 = (f32[40,128]{1,0:T(8,128)S(1)}, f32[40,128]{1,0:T(8,128)S(1)}, u32[]{:S(2)}, u32[]{:S(2)}) collective-permute-start(f32[40,128]{1,0:T(8,128)S(1)} %get-tuple-element.23.refs_1_), channel_id=1, source_target_pairs={{0,2},{1,3},{2,0},{3,1},{4,6},{5,7},{6,4},{7,5},{8,16},{9,17},{10,... | collective-permute-start | bytes 61448 | tf_op jit(solution)/shard_map/ppermute | solution.py:87
  10.0 2.3 %collective-permute-start.7 = (f32[40,128]{1,0:T(8,128)S(1)}, f32[40,128]{1,0:T(8,128)S(1)}, u32[]{:S(2)}, u32[]{:S(2)}) collective-permute-start(f32[40,128]{1,0:T(8,128)S(1)} %get-tuple-element.24.refs_2_), channel_id=1, source_target_pairs={{0,2},{1,3},{2,0},{3,1},{4,6},{5,7},{6,4},{7,5},{8,10},{9,11},{10,... | collective-permute-start | bytes 61448 | tf_op jit(solution)/shard_map/ppermute | solution.py:87

commit v8 on v7

--- a/solution.py
+++ b/solution.py
@@ -511,7 +511,7 @@
     z_in = [swap(v, gz=t) for t, v in enumerate(faces)]
     columns = kernel_call(
         functools.partial(pack_columns, nyt, nzt),
-        [array(width + YPAD[t], length) for t in range(nyt)] + [array(YZ_ROWS, length)] * (nyt * nzt),
+        [array(width + YPAD[t], length) for t in range(nyt)] + [array(YZ_ROWS + 8 * ty, length) for ty in range(nyt) for tz in range(nzt)],
         [vmem] * (3 + nzt),
         "columns",
         1 << 18,

time: 13.2 us -> 13.3 us (level)
  the two profiles are of different devices: /device:TPU:1 before, /device:TPU:0 now
where the time goes in v8:
time: 13.3 us; the launch traced here: 13.1 us
  starting transfers between devices  8.58 us (65%)
  Pallas kernels  3.49 us (26%)
  between operations  0.75 us (6%)
  waiting for transfers between devices  0.21 us (2%)
    ppermute x8, starting transfers between devices, swap(): return lax.ppermute(value, AXES, pairs)  8.58 us
    pallas_call x1, Pallas kernels, local(): kernel_call(functools.partial(interior, nyt, nzt), [array(*c.shape) for c...  1.35 us
    pallas_call x1, Pallas kernels, local(): kernel_call(functools.partial(pack_faces, nzt), [array((len(ZM) + 1) * wi...  0.95 us
    pallas_call x1, Pallas kernels, local(): kernel_call(functools.partial(finish, nxt), [array(*c.shape) for c in cot...  0.75 us
  transfers between devices with their start and end apart: 8, of which 1 were waited for; matrix products, arithmetic and copies ran while one was open for 0% of the time, Pallas kernels for 14%

profile of v8, /device:TPU:0, one launch (start us, length us, event | category | flops | bytes accessed | tf_op | source)
XLA Modules:
  0.0 13.1 jit_solution(17595262658631077280)
XLA Ops:
  0.7 0.9 %faces.1.refs_0_ = f32[112,128]{1,0:T(8,128)S(1)} custom-call(f32[19,4,16,128]{3,2,1,0:T(8,128)} %cot_flow.7, f32[7,4,16,128]{3,2,1,0:T(8,128)} %cot_heat.7, f32[10,16,128]{2,1,0:T(8,128)} %cot_plate.7), custom_call_target="tpu_custom_call" | custom-call | bytes 1048576 | tf_op jit(solution)/shard_map/faces/pallas_call | solution.py:503
  1.6 3.0 %collective-permute-start = (f32[112,128]{1,0:T(8,128)S(1)}, f32[112,128]{1,0:T(8,128)S(1)}, u32[]{:S(2)}, u32[]{:S(2)}) collective-permute-start(f32[112,128]{1,0:T(8,128)S(1)} %faces.1.refs_0_), channel_id=1, source_target_pairs={{0,1},{1,0},{2,3},{3,2},{4,5},{5,4},{6,7},{7,6},{8,9},{9,8},{10,11... | collective-permute-start | bytes 172040 | tf_op jit(solution)/shard_map/ppermute | solution.py:87
  4.7 0.2 %columns.1 = (f32[16,128]{1,0:T(8,128)S(1)}, f32[16,128]{1,0:T(8,128)S(1)}, f32[48,128]{1,0:T(8,128)S(1)}, f32[56,128]{1,0:T(8,128)S(1)}) custom-call(f32[19,4,16,128]{3,2,1,0:T(8,128)S(1)} %copy-done, f32[7,4,16,128]{3,2,1,0:T(8,128)S(1)} %copy-done.1, f32[10,16,128]{2,1,0:T(8,128)S(1)} %copy-done.2, f32[112,128]{1,0:T(8,128)S(1)} %faces.1.refs_0_), custom_call_target="tpu_custom_call" | custom-call | bytes 262144 | tf_op jit(solution)/shard_map/columns/pallas_call | solution.py:512
  4.9 0.0 copy-start.3
  4.9 0.1 collective-permute-start.1
  5.0 1.6 %collective-permute-start.2 = (f32[16,128]{1,0:T(8,128)S(1)}, f32[16,128]{1,0:T(8,128)S(1)}, u32[]{:S(2)}, u32[]{:S(2)}) collective-permute-start(f32[16,128]{1,0:T(8,128)S(1)} %get-tuple-element.21), channel_id=1, source_target_pairs={{0,6},{1,7},{2,4},{3,5},{4,2},{5,3},{6,0},{7,1},{8,14},{9,15},{10,... | collective-permute-start | bytes 24584 | tf_op jit(solution)/shard_map/ppermute | solution.py:87
  6.6 0.2 %collective-permute-start.4 = (f32[56,128]{1,0:T(8,128)S(1)}, f32[56,128]{1,0:T(8,128)S(1)}, u32[]{:S(2)}, u32[]{:S(2)}) collective-permute-start(f32[56,128]{1,0:T(8,128)S(1)} %get-tuple-element.30), channel_id=1, source_target_pairs={{0,6},{1,7},{2,5},{3,4},{4,3},{5,2},{6,0},{7,1},{8,14},{9,15},{10,... | collective-permute-start | bytes 86024 | tf_op jit(solution)/shard_map/ppermute | solution.py:87
  6.8 1.5 %collective-permute-start.3 = (f32[48,128]{1,0:T(8,128)S(1)}, f32[48,128]{1,0:T(8,128)S(1)}, u32[]{:S(2)}, u32[]{:S(2)}) collective-permute-start(f32[48,128]{1,0:T(8,128)S(1)} %get-tuple-element.29), channel_id=1, source_target_pairs={{0,3},{1,2},{2,1},{3,0},{4,7},{5,6},{6,5},{7,4},{8,11},{9,10},{10,... | collective-permute-start | bytes 73736 | tf_op jit(solution)/shard_map/ppermute | solution.py:87
  8.3 0.0 collective-permute-done.1.refs_1_
  8.3 0.0 collective-permute-done.2.refs_2_
  8.3 0.0 collective-permute-done.refs_0_
  8.3 0.0 copy-start.6
  8.3 0.1 %rows.1 = (f32[40,128]{1,0:T(8,128)S(1)}, f32[40,128]{1,0:T(8,128)S(1)}, f32[40,128]{1,0:T(8,128)S(1)}) custom-call(f32[19,4,16,128]{3,2,1,0:T(8,128)S(1)} %copy-done, f32[7,4,16,128]{3,2,1,0:T(8,128)S(1)} %copy-done.1, f32[10,16,128]{2,1,0:T(8,128)S(1)} %copy-done.2, f32[112,128]{1,0:T(8,128)S(1)} %collective-permute-done.refs_0_, ...), custom_call_target="tpu_custom_call" | custom-call | bytes 262144 | tf_op jit(solution)/shard_map/rows/pallas_call | solution.py:521
  8.4 0.0 copy-start.7
  8.5 1.6 %collective-permute-start.5 = (f32[40,128]{1,0:T(8,128)S(1)}, f32[40,128]{1,0:T(8,128)S(1)}, u32[]{:S(2)}, u32[]{:S(2)}) collective-permute-start(f32[40,128]{1,0:T(8,128)S(1)} %get-tuple-element.22.refs_0_), channel_id=1, source_target_pairs={{0,8},{1,9},{2,10},{3,11},{4,12},{5,13},{6,14},{7,15},{8,0},{9,1},... | collective-permute-start | bytes 61448 | tf_op jit(solution)/shard_map/ppermute | solution.py:87
  10.1 0.0 collective-permute-start.6
  10.1 0.5 %collective-permute-start.7 = (f32[40,128]{1,0:T(8,128)S(1)}, f32[40,128]{1,0:T(8,128)S(1)}, u32[]{:S(2)}, u32[]{:S(2)}) collective-permute-start(f32[40,128]{1,0:T(8,128)S(1)} %get-tuple-element.24.refs_2_), channel_id=1, source_target_pairs={{0,2},{1,3},{2,0},{3,1},{4,6},{5,7},{6,4},{7,5},{8,10},{9,11},{10,... | collective-permute-start | bytes 61448 | tf_op jit(solution)/shard_map/ppermute | solution.py:87
  10.6 0.1 prepare.1
  10.7 0.0 collective-permute-done.3.refs_3_
  10.7 0.0 collective-permute-done.4.refs_4_
  10.8 1.4 %interior.1 = (f32[19,4,16,128]{3,2,1,0:T(8,128)}, f32[7,4,16,128]{3,2,1,0:T(8,128)}, f32[10,16,128]{2,1,0:T(8,128)}, f32[19,8,128]{2,1,0:T(8,128)S(1)}, f32[7,8...) custom-call(s32[4,16,128]{2,1,0:T(8,128)S(1)} %copy-done.5, f32[3,4,16,128]{3,2,1,0:T(8,128)S(1)} %get-tuple-element.27.ue_in, ...), custom_call_target="tpu_custom_call" | custom-call | bytes 4194304 | tf_op jit(solution)/shard_map/interior/pallas_call | solution.py:541
  12.1 0.2 %collective-permute-done.5.refs_0_ = f32[40,128]{1,0:T(8,128)S(1)} collective-permute-done((f32[40,128]{1,0:T(8,128)S(1)}, f32[40,128]{1,0:T(8,128)S(1)}, u32[]{:S(2)}, u32[]{:S(2)}) %collective-permute-start.5) | collective-permute-done | bytes 20512 | tf_op jit(solution)/shard_map/ppermute | solution.py:87
  12.3 0.0 collective-permute-done.6.refs_1_
  12.3 0.8 %finish.1 = (f32[19,4,16,128]{3,2,1,0:T(8,128)}, f32[7,4,16,128]{3,2,1,0:T(8,128)}, f32[10,16,128]{2,1,0:T(8,128)}) custom-call(f32[4,8,128]{2,1,0:T(8,128)S(1)} %get-tuple-element.25.rows_in, s32[8,128]{1,0:T(8,128)S(1)} %get-tuple-element.26.kinds, ...), custom_call_target="tpu_custom_call", output_to_operand_aliasing={{0}: (8, {}), {1}: (9, {}), {2}: (10, {})} | custom-call | bytes 1048576 | tf_op jit(solution)/shard_map/finish/pallas_call | solution.py:552
  (14 shorter events, 0.0 us)
Async XLA Ops:
  0.6 4.0 %copy-start.2 = (f32[10,16,128]{2,1,0:T(8,128)S(1)}, f32[10,16,128]{2,1,0:T(8,128)}, u32[]{:S(2)}) copy-start(f32[10,16,128]{2,1,0:T(8,128)} %cot_plate.7) | copy-start | bytes 245764
  0.6 4.0 %copy-start.1 = (f32[7,4,16,128]{3,2,1,0:T(8,128)S(1)}, f32[7,4,16,128]{3,2,1,0:T(8,128)}, u32[]{:S(2)}) copy-start(f32[7,4,16,128]{3,2,1,0:T(8,128)} %cot_heat.7) | copy-start | bytes 688132
  0.7 4.0 %copy-start = (f32[19,4,16,128]{3,2,1,0:T(8,128)S(1)}, f32[19,4,16,128]{3,2,1,0:T(8,128)}, u32[]{:S(2)}) copy-start(f32[19,4,16,128]{3,2,1,0:T(8,128)} %cot_flow.7) | copy-start | bytes 1867780
  1.6 6.7 %collective-permute-start = (f32[112,128]{1,0:T(8,128)S(1)}, f32[112,128]{1,0:T(8,128)S(1)}, u32[]{:S(2)}, u32[]{:S(2)}) collective-permute-start(f32[112,128]{1,0:T(8,128)S(1)} %faces.1.refs_0_), channel_id=1, source_target_pairs={{0,1},{1,0},{2,3},{3,2},{4,5},{5,4},{6,7},{7,6},{8,9},{9,8},{10,11... | collective-permute-start | bytes 172040 | tf_op jit(solution)/shard_map/ppermute | solution.py:87
  4.9 5.8 %copy-start.3 = (f32[19,4,16,128]{3,2,1,0:T(8,128)S(1)}, f32[19,4,16,128]{3,2,1,0:T(8,128)}, u32[]{:S(2)}) copy-start(f32[19,4,16,128]{3,2,1,0:T(8,128)} %pop_flow.1) | copy-start | bytes 1867780
  4.9 3.4 %collective-permute-start.1 = (f32[16,128]{1,0:T(8,128)S(1)}, f32[16,128]{1,0:T(8,128)S(1)}, u32[]{:S(2)}, u32[]{:S(2)}) collective-permute-start(f32[16,128]{1,0:T(8,128)S(1)} %get-tuple-element.20), channel_id=1, source_target_pairs={{0,2},{1,3},{2,0},{3,1},{4,6},{5,7},{6,4},{7,5},{8,10},{9,11},{10,... | collective-permute-start | bytes 24584 | tf_op jit(solution)/shard_map/ppermute | solution.py:87
  5.0 3.3 %collective-permute-start.2 = (f32[16,128]{1,0:T(8,128)S(1)}, f32[16,128]{1,0:T(8,128)S(1)}, u32[]{:S(2)}, u32[]{:S(2)}) collective-permute-start(f32[16,128]{1,0:T(8,128)S(1)} %get-tuple-element.21), channel_id=1, source_target_pairs={{0,6},{1,7},{2,4},{3,5},{4,2},{5,3},{6,0},{7,1},{8,14},{9,15},{10,... | collective-permute-start | bytes 24584 | tf_op jit(solution)/shard_map/ppermute | solution.py:87
  6.6 4.2 %collective-permute-start.4 = (f32[56,128]{1,0:T(8,128)S(1)}, f32[56,128]{1,0:T(8,128)S(1)}, u32[]{:S(2)}, u32[]{:S(2)}) collective-permute-start(f32[56,128]{1,0:T(8,128)S(1)} %get-tuple-element.30), channel_id=1, source_target_pairs={{0,6},{1,7},{2,5},{3,4},{4,3},{5,2},{6,0},{7,1},{8,14},{9,15},{10,... | collective-permute-start | bytes 86024 | tf_op jit(solution)/shard_map/ppermute | solution.py:87
  6.8 3.9 %copy-start.4 = (f32[7,4,16,128]{3,2,1,0:T(8,128)S(1)}, f32[7,4,16,128]{3,2,1,0:T(8,128)}, u32[]{:S(2)}) copy-start(f32[7,4,16,128]{3,2,1,0:T(8,128)} %pop_heat.1) | copy-start | bytes 688132
  6.8 3.9 %copy-start.5 = (s32[4,16,128]{2,1,0:T(8,128)S(1)}, s32[4,16,128]{2,1,0:T(8,128)}, u32[]{:S(2)}) copy-start(s32[4,16,128]{2,1,0:T(8,128)} %flags.3) | copy-start | bytes 98308
  6.8 4.0 %collective-permute-start.3 = (f32[48,128]{1,0:T(8,128)S(1)}, f32[48,128]{1,0:T(8,128)S(1)}, u32[]{:S(2)}, u32[]{:S(2)}) collective-permute-start(f32[48,128]{1,0:T(8,128)S(1)} %get-tuple-element.29), channel_id=1, source_target_pairs={{0,3},{1,2},{2,1},{3,0},{4,7},{5,6},{6,5},{7,4},{8,11},{9,10},{10,... | collective-permute-start | bytes 73736 | tf_op jit(solution)/shard_map/ppermute | solution.py:87
  8.3 2.3 %copy-start.6 = (s32[16,128]{1,0:T(8,128)S(1)}, s32[16,128]{1,0:T(8,128)}, u32[]{:S(2)}) copy-start(s32[16,128]{1,0:T(8,128)} %nozzle.1) | copy-start | bytes 24580
  8.4 2.2 %copy-start.7 = (f32[3,64]{1,0:T(4,128)S(1)}, f32[3,64]{1,0:T(4,128)}, u32[]{:S(2)}) copy-start(f32[3,64]{1,0:T(4,128)} %jet_velocity.1) | copy-start | bytes 2308
  8.5 3.8 %collective-permute-start.5 = (f32[40,128]{1,0:T(8,128)S(1)}, f32[40,128]{1,0:T(8,128)S(1)}, u32[]{:S(2)}, u32[]{:S(2)}) collective-permute-start(f32[40,128]{1,0:T(8,128)S(1)} %get-tuple-element.22.refs_0_), channel_id=1, source_target_pairs={{0,8},{1,9},{2,10},{3,11},{4,12},{5,13},{6,14},{7,15},{8,0},{9,1},... | collective-permute-start | bytes 61448 | tf_op jit(solution)/shard_map/ppermute | solution.py:87
  10.1 2.2 %collective-permute-start.6 = (f32[40,128]{1,0:T(8,128)S(1)}, f32[40,128]{1,0:T(8,128)S(1)}, u32[]{:S(2)}, u32[]{:S(2)}) collective-permute-start(f32[40,128]{1,0:T(8,128)S(1)} %get-tuple-element.23.refs_1_), channel_id=1, source_target_pairs={{0,2},{1,3},{2,0},{3,1},{4,6},{5,7},{6,4},{7,5},{8,16},{9,17},{10,... | collective-permute-start | bytes 61448 | tf_op jit(solution)/shard_map/ppermute | solution.py:87
  10.1 2.2 %collective-permute-start.7 = (f32[40,128]{1,0:T(8,128)S(1)}, f32[40,128]{1,0:T(8,128)S(1)}, u32[]{:S(2)}, u32[]{:S(2)}) collective-permute-start(f32[40,128]{1,0:T(8,128)S(1)} %get-tuple-element.24.refs_2_), channel_id=1, source_target_pairs={{0,2},{1,3},{2,0},{3,1},{4,6},{5,7},{6,4},{7,5},{8,10},{9,11},{10,... | collective-permute-start | bytes 61448 | tf_op jit(solution)/shard_map/ppermute | solution.py:87

commit v9 on v8

--- a/solution.py
+++ b/solution.py
@@ -435,6 +435,13 @@
     above, below = incoming("gx", [r[:used, :] for r in x_in])
     above_buf[...] = above
     below_buf[...] = below
+    copies = []
+    n = len(XP) * depth
+    for side, (x, beside) in enumerate(((0, below_buf), (width - 1, above_buf))):
+        rows = slice(side * layers, (side + 1) * layers)
+        plate_buf[side] = rows_plate[rows, :] + diffusion * beside[n : n + layers, :]
+        copies.append(pltpu.make_async_copy(plate_buf.at[side], out_plate.at[:, x, :], sems.at[len(copies)]))
+        copies[-1].start()
     zero = jnp.zeros((2 * depth, above.shape[1]), jnp.float32)
     star = []
     for k, c in enumerate(DIRECTIONS):
@@ -453,7 +460,6 @@
     flow, heat = collide_back(
         star[:FLOW], star[FLOW:], [rows_in[c] for c in range(3)], rows_in[3], kind == 1, kind == 2
     )
-    copies = []
     for values, rows, buf, out in (
         (flow, rows_flow, flow_buf, out_flow),
         (heat, rows_heat, heat_buf, out_heat),
@@ -464,12 +470,6 @@
             source = buf.at[:, side * depth : (side + 1) * depth, :]
             copies.append(pltpu.make_async_copy(source, out.at[:, :, x, :], sems.at[len(copies)]))
             copies[-1].start()
-    n = len(XP) * depth
-    for side, (x, beside) in enumerate(((0, below_buf), (width - 1, above_buf))):
-        rows = slice(side * layers, (side + 1) * layers)
-        plate_buf[side] = rows_plate[rows, :] + diffusion * beside[n : n + layers, :]
-        copies.append(pltpu.make_async_copy(plate_buf.at[side], out_plate.at[:, x, :], sems.at[len(copies)]))
-        copies[-1].start()
     for copy in copies:
         copy.wait()
 

time: 13.3 us -> 13.3 us (level)
  no operation moved by 1% of the time
where the time goes in v9:
time: 13.3 us; the launch traced here: 13.1 us
  starting transfers between devices  8.58 us (65%)
  Pallas kernels  3.49 us (26%)
  between operations  0.75 us (6%)
  waiting for transfers between devices  0.21 us (2%)
    ppermute x8, starting transfers between devices, swap(): return lax.ppermute(value, AXES, pairs)  8.58 us
    pallas_call x1, Pallas kernels, local(): kernel_call(functools.partial(interior, nyt, nzt), [array(*c.shape) for c...  1.35 us
    pallas_call x1, Pallas kernels, local(): kernel_call(functools.partial(pack_faces, nzt), [array((len(ZM) + 1) * wi...  0.95 us
    pallas_call x1, Pallas kernels, local(): kernel_call(functools.partial(finish, nxt), [array(*c.shape) for c in cot...  0.75 us
  transfers between devices with their start and end apart: 8, of which 1 were waited for; matrix products, arithmetic and copies ran while one was open for 0% of the time, Pallas kernels for 14%

profile of v9, /device:TPU:0, one launch (start us, length us, event | category | flops | bytes accessed | tf_op | source)
XLA Modules:
  0.0 13.1 jit_solution(11284140847719155007)
XLA Ops:
  0.7 0.9 %faces.1.refs_0_ = f32[112,128]{1,0:T(8,128)S(1)} custom-call(f32[19,4,16,128]{3,2,1,0:T(8,128)} %cot_flow.7, f32[7,4,16,128]{3,2,1,0:T(8,128)} %cot_heat.7, f32[10,16,128]{2,1,0:T(8,128)} %cot_plate.7), custom_call_target="tpu_custom_call" | custom-call | bytes 1048576 | tf_op jit(solution)/shard_map/faces/pallas_call | solution.py:503
  1.6 3.0 %collective-permute-start = (f32[112,128]{1,0:T(8,128)S(1)}, f32[112,128]{1,0:T(8,128)S(1)}, u32[]{:S(2)}, u32[]{:S(2)}) collective-permute-start(f32[112,128]{1,0:T(8,128)S(1)} %faces.1.refs_0_), channel_id=1, source_target_pairs={{0,1},{1,0},{2,3},{3,2},{4,5},{5,4},{6,7},{7,6},{8,9},{9,8},{10,11... | collective-permute-start | bytes 172040 | tf_op jit(solution)/shard_map/ppermute | solution.py:87
  4.7 0.2 %columns.1 = (f32[16,128]{1,0:T(8,128)S(1)}, f32[16,128]{1,0:T(8,128)S(1)}, f32[48,128]{1,0:T(8,128)S(1)}, f32[56,128]{1,0:T(8,128)S(1)}) custom-call(f32[19,4,16,128]{3,2,1,0:T(8,128)S(1)} %copy-done, f32[7,4,16,128]{3,2,1,0:T(8,128)S(1)} %copy-done.1, f32[10,16,128]{2,1,0:T(8,128)S(1)} %copy-done.2, f32[112,128]{1,0:T(8,128)S(1)} %faces.1.refs_0_), custom_call_target="tpu_custom_call" | custom-call | bytes 262144 | tf_op jit(solution)/shard_map/columns/pallas_call | solution.py:512
  4.9 0.0 copy-start.3
  4.9 0.1 collective-permute-start.1
  5.0 1.6 %collective-permute-start.2 = (f32[16,128]{1,0:T(8,128)S(1)}, f32[16,128]{1,0:T(8,128)S(1)}, u32[]{:S(2)}, u32[]{:S(2)}) collective-permute-start(f32[16,128]{1,0:T(8,128)S(1)} %get-tuple-element.21), channel_id=1, source_target_pairs={{0,6},{1,7},{2,4},{3,5},{4,2},{5,3},{6,0},{7,1},{8,14},{9,15},{10,... | collective-permute-start | bytes 24584 | tf_op jit(solution)/shard_map/ppermute | solution.py:87
  6.6 0.2 %collective-permute-start.4 = (f32[56,128]{1,0:T(8,128)S(1)}, f32[56,128]{1,0:T(8,128)S(1)}, u32[]{:S(2)}, u32[]{:S(2)}) collective-permute-start(f32[56,128]{1,0:T(8,128)S(1)} %get-tuple-element.30), channel_id=1, source_target_pairs={{0,6},{1,7},{2,5},{3,4},{4,3},{5,2},{6,0},{7,1},{8,14},{9,15},{10,... | collective-permute-start | bytes 86024 | tf_op jit(solution)/shard_map/ppermute | solution.py:87
  6.8 1.5 %collective-permute-start.3 = (f32[48,128]{1,0:T(8,128)S(1)}, f32[48,128]{1,0:T(8,128)S(1)}, u32[]{:S(2)}, u32[]{:S(2)}) collective-permute-start(f32[48,128]{1,0:T(8,128)S(1)} %get-tuple-element.29), channel_id=1, source_target_pairs={{0,3},{1,2},{2,1},{3,0},{4,7},{5,6},{6,5},{7,4},{8,11},{9,10},{10,... | collective-permute-start | bytes 73736 | tf_op jit(solution)/shard_map/ppermute | solution.py:87
  8.3 0.0 collective-permute-done.1.refs_1_
  8.3 0.0 collective-permute-done.2.refs_2_
  8.3 0.0 collective-permute-done.refs_0_
  8.3 0.0 copy-start.6
  8.3 0.1 %rows.1 = (f32[40,128]{1,0:T(8,128)S(1)}, f32[40,128]{1,0:T(8,128)S(1)}, f32[40,128]{1,0:T(8,128)S(1)}) custom-call(f32[19,4,16,128]{3,2,1,0:T(8,128)S(1)} %copy-done, f32[7,4,16,128]{3,2,1,0:T(8,128)S(1)} %copy-done.1, f32[10,16,128]{2,1,0:T(8,128)S(1)} %copy-done.2, f32[112,128]{1,0:T(8,128)S(1)} %collective-permute-done.refs_0_, ...), custom_call_target="tpu_custom_call" | custom-call | bytes 262144 | tf_op jit(solution)/shard_map/rows/pallas_call | solution.py:521
  8.4 0.0 copy-start.7
  8.5 1.6 %collective-permute-start.5 = (f32[40,128]{1,0:T(8,128)S(1)}, f32[40,128]{1,0:T(8,128)S(1)}, u32[]{:S(2)}, u32[]{:S(2)}) collective-permute-start(f32[40,128]{1,0:T(8,128)S(1)} %get-tuple-element.22.refs_0_), channel_id=1, source_target_pairs={{0,8},{1,9},{2,10},{3,11},{4,12},{5,13},{6,14},{7,15},{8,0},{9,1},... | collective-permute-start | bytes 61448 | tf_op jit(solution)/shard_map/ppermute | solution.py:87
  10.1 0.0 collective-permute-start.6
  10.1 0.5 %collective-permute-start.7 = (f32[40,128]{1,0:T(8,128)S(1)}, f32[40,128]{1,0:T(8,128)S(1)}, u32[]{:S(2)}, u32[]{:S(2)}) collective-permute-start(f32[40,128]{1,0:T(8,128)S(1)} %get-tuple-element.24.refs_2_), channel_id=1, source_target_pairs={{0,2},{1,3},{2,0},{3,1},{4,6},{5,7},{6,4},{7,5},{8,10},{9,11},{10,... | collective-permute-start | bytes 61448 | tf_op jit(solution)/shard_map/ppermute | solution.py:87
  10.6 0.1 prepare.1
  10.7 0.0 collective-permute-done.4.refs_4_
  10.8 1.4 %interior.1 = (f32[19,4,16,128]{3,2,1,0:T(8,128)}, f32[7,4,16,128]{3,2,1,0:T(8,128)}, f32[10,16,128]{2,1,0:T(8,128)}, f32[19,8,128]{2,1,0:T(8,128)S(1)}, f32[7,8...) custom-call(s32[4,16,128]{2,1,0:T(8,128)S(1)} %copy-done.5, f32[3,4,16,128]{3,2,1,0:T(8,128)S(1)} %get-tuple-element.27.ue_in, ...), custom_call_target="tpu_custom_call" | custom-call | bytes 4194304 | tf_op jit(solution)/shard_map/interior/pallas_call | solution.py:541
  12.1 0.2 %collective-permute-done.5.refs_0_ = f32[40,128]{1,0:T(8,128)S(1)} collective-permute-done((f32[40,128]{1,0:T(8,128)S(1)}, f32[40,128]{1,0:T(8,128)S(1)}, u32[]{:S(2)}, u32[]{:S(2)}) %collective-permute-start.5) | collective-permute-done | bytes 20512 | tf_op jit(solution)/shard_map/ppermute | solution.py:87
  12.3 0.0 collective-permute-done.6.refs_1_
  12.3 0.0 collective-permute-done.7.refs_2_
  12.3 0.8 %finish.1 = (f32[19,4,16,128]{3,2,1,0:T(8,128)}, f32[7,4,16,128]{3,2,1,0:T(8,128)}, f32[10,16,128]{2,1,0:T(8,128)}) custom-call(f32[4,8,128]{2,1,0:T(8,128)S(1)} %get-tuple-element.25.rows_in, s32[8,128]{1,0:T(8,128)S(1)} %get-tuple-element.26.kinds, ...), custom_call_target="tpu_custom_call", output_to_operand_aliasing={{0}: (8, {}), {1}: (9, {}), {2}: (10, {})} | custom-call | bytes 1048576 | tf_op jit(solution)/shard_map/finish/pallas_call | solution.py:552
  (14 shorter events, 0.0 us)
Async XLA Ops:
  0.6 4.0 %copy-start.2 = (f32[10,16,128]{2,1,0:T(8,128)S(1)}, f32[10,16,128]{2,1,0:T(8,128)}, u32[]{:S(2)}) copy-start(f32[10,16,128]{2,1,0:T(8,128)} %cot_plate.7) | copy-start | bytes 245764
  0.6 4.0 %copy-start.1 = (f32[7,4,16,128]{3,2,1,0:T(8,128)S(1)}, f32[7,4,16,128]{3,2,1,0:T(8,128)}, u32[]{:S(2)}) copy-start(f32[7,4,16,128]{3,2,1,0:T(8,128)} %cot_heat.7) | copy-start | bytes 688132
  0.7 4.0 %copy-start = (f32[19,4,16,128]{3,2,1,0:T(8,128)S(1)}, f32[19,4,16,128]{3,2,1,0:T(8,128)}, u32[]{:S(2)}) copy-start(f32[19,4,16,128]{3,2,1,0:T(8,128)} %cot_flow.7) | copy-start | bytes 1867780
  1.6 6.7 %collective-permute-start = (f32[112,128]{1,0:T(8,128)S(1)}, f32[112,128]{1,0:T(8,128)S(1)}, u32[]{:S(2)}, u32[]{:S(2)}) collective-permute-start(f32[112,128]{1,0:T(8,128)S(1)} %faces.1.refs_0_), channel_id=1, source_target_pairs={{0,1},{1,0},{2,3},{3,2},{4,5},{5,4},{6,7},{7,6},{8,9},{9,8},{10,11... | collective-permute-start | bytes 172040 | tf_op jit(solution)/shard_map/ppermute | solution.py:87
  4.9 5.8 %copy-start.3 = (f32[19,4,16,128]{3,2,1,0:T(8,128)S(1)}, f32[19,4,16,128]{3,2,1,0:T(8,128)}, u32[]{:S(2)}) copy-start(f32[19,4,16,128]{3,2,1,0:T(8,128)} %pop_flow.1) | copy-start | bytes 1867780
  4.9 3.4 %collective-permute-start.1 = (f32[16,128]{1,0:T(8,128)S(1)}, f32[16,128]{1,0:T(8,128)S(1)}, u32[]{:S(2)}, u32[]{:S(2)}) collective-permute-start(f32[16,128]{1,0:T(8,128)S(1)} %get-tuple-element.20), channel_id=1, source_target_pairs={{0,2},{1,3},{2,0},{3,1},{4,6},{5,7},{6,4},{7,5},{8,10},{9,11},{10,... | collective-permute-start | bytes 24584 | tf_op jit(solution)/shard_map/ppermute | solution.py:87
  5.0 3.3 %collective-permute-start.2 = (f32[16,128]{1,0:T(8,128)S(1)}, f32[16,128]{1,0:T(8,128)S(1)}, u32[]{:S(2)}, u32[]{:S(2)}) collective-permute-start(f32[16,128]{1,0:T(8,128)S(1)} %get-tuple-element.21), channel_id=1, source_target_pairs={{0,6},{1,7},{2,4},{3,5},{4,2},{5,3},{6,0},{7,1},{8,14},{9,15},{10,... | collective-permute-start | bytes 24584 | tf_op jit(solution)/shard_map/ppermute | solution.py:87
  6.6 4.2 %collective-permute-start.4 = (f32[56,128]{1,0:T(8,128)S(1)}, f32[56,128]{1,0:T(8,128)S(1)}, u32[]{:S(2)}, u32[]{:S(2)}) collective-permute-start(f32[56,128]{1,0:T(8,128)S(1)} %get-tuple-element.30), channel_id=1, source_target_pairs={{0,6},{1,7},{2,5},{3,4},{4,3},{5,2},{6,0},{7,1},{8,14},{9,15},{10,... | collective-permute-start | bytes 86024 | tf_op jit(solution)/shard_map/ppermute | solution.py:87
  6.8 3.9 %copy-start.4 = (f32[7,4,16,128]{3,2,1,0:T(8,128)S(1)}, f32[7,4,16,128]{3,2,1,0:T(8,128)}, u32[]{:S(2)}) copy-start(f32[7,4,16,128]{3,2,1,0:T(8,128)} %pop_heat.1) | copy-start | bytes 688132
  6.8 3.9 %copy-start.5 = (s32[4,16,128]{2,1,0:T(8,128)S(1)}, s32[4,16,128]{2,1,0:T(8,128)}, u32[]{:S(2)}) copy-start(s32[4,16,128]{2,1,0:T(8,128)} %flags.3) | copy-start | bytes 98308
  6.8 4.0 %collective-permute-start.3 = (f32[48,128]{1,0:T(8,128)S(1)}, f32[48,128]{1,0:T(8,128)S(1)}, u32[]{:S(2)}, u32[]{:S(2)}) collective-permute-start(f32[48,128]{1,0:T(8,128)S(1)} %get-tuple-element.29), channel_id=1, source_target_pairs={{0,3},{1,2},{2,1},{3,0},{4,7},{5,6},{6,5},{7,4},{8,11},{9,10},{10,... | collective-permute-start | bytes 73736 | tf_op jit(solution)/shard_map/ppermute | solution.py:87
  8.3 2.3 %copy-start.6 = (s32[16,128]{1,0:T(8,128)S(1)}, s32[16,128]{1,0:T(8,128)}, u32[]{:S(2)}) copy-start(s32[16,128]{1,0:T(8,128)} %nozzle.1) | copy-start | bytes 24580
  8.4 2.2 %copy-start.7 = (f32[3,64]{1,0:T(4,128)S(1)}, f32[3,64]{1,0:T(4,128)}, u32[]{:S(2)}) copy-start(f32[3,64]{1,0:T(4,128)} %jet_velocity.1) | copy-start | bytes 2308
  8.5 3.8 %collective-permute-start.5 = (f32[40,128]{1,0:T(8,128)S(1)}, f32[40,128]{1,0:T(8,128)S(1)}, u32[]{:S(2)}, u32[]{:S(2)}) collective-permute-start(f32[40,128]{1,0:T(8,128)S(1)} %get-tuple-element.22.refs_0_), channel_id=1, source_target_pairs={{0,8},{1,9},{2,10},{3,11},{4,12},{5,13},{6,14},{7,15},{8,0},{9,1},... | collective-permute-start | bytes 61448 | tf_op jit(solution)/shard_map/ppermute | solution.py:87
  10.1 2.2 %collective-permute-start.6 = (f32[40,128]{1,0:T(8,128)S(1)}, f32[40,128]{1,0:T(8,128)S(1)}, u32[]{:S(2)}, u32[]{:S(2)}) collective-permute-start(f32[40,128]{1,0:T(8,128)S(1)} %get-tuple-element.23.refs_1_), channel_id=1, source_target_pairs={{0,2},{1,3},{2,0},{3,1},{4,6},{5,7},{6,4},{7,5},{8,16},{9,17},{10,... | collective-permute-start | bytes 61448 | tf_op jit(solution)/shard_map/ppermute | solution.py:87
  10.1 2.2 %collective-permute-start.7 = (f32[40,128]{1,0:T(8,128)S(1)}, f32[40,128]{1,0:T(8,128)S(1)}, u32[]{:S(2)}, u32[]{:S(2)}) collective-permute-start(f32[40,128]{1,0:T(8,128)S(1)} %get-tuple-element.24.refs_2_), channel_id=1, source_target_pairs={{0,2},{1,3},{2,0},{3,1},{4,6},{5,7},{6,4},{7,5},{8,10},{9,11},{10,... | collective-permute-start | bytes 61448 | tf_op jit(solution)/shard_map/ppermute | solution.py:87
